TPU v7x, 128 devices: a whole 4x4x4 slice. The times are simulated.
128 devices in a mesh: tm: 32 (over y, x_hi, z), chan: 4 (over x_lo, core).
Axes of the slice: x: 4 (x_hi: 2, x_lo: 2; x = x_hi * 2 + x_lo), y: 4, z: 4, core: 2. Of those that a mesh axis runs over, the one named last changes fastest.
Arguments:
- series: float32 [256, 8192], P('chan', 'tm'), may hold values from -6 to 6
- lengths: int32 [64], replicated, may hold values from 42 to 128
Outputs:
- peak: float32 [8192], P('tm')
All inputs are finite; a program needn't handle non-finite values.
Results may differ from a plain program's by a relative error of at most 0.0015.
Values may be sent and summed in bfloat16 or wider, within the bound.
No kernel may reach another device: no remote copies, remote signals or barrier semaphores. Data moves between devices by JAX's collectives and lax.ppermute only.
A program may use at most 128 MiB of HBM per device.

v0:
```python
import jax
import jax.numpy as jnp
from jax import lax
from jax.sharding import PartitionSpec as P

WIN = 256
STEPS = 2


EPS = 1e-05
MASKED = -1000000000.0


def passed_along(block, axis, distance):
    devices = range(lax.axis_size(axis))
    route = [(i - distance, i) for i in devices if i - distance in devices]
    return lax.ppermute(block, axis, route)


def from_everyone(value, axis):
    devices = lax.axis_size(axis)
    return lax.all_to_all(
        jnp.broadcast_to(value[None], (devices, *value.shape)), axis, 0, 0, tiled=True
    )


def over_copies(value, axis):
    everything = from_everyone(value, axis)
    return jnp.sum(everything, axis=0)


def windows_of(extended):
    count = extended.shape[1] - WIN + 1
    zeros = jnp.zeros((extended.shape[0], 1), jnp.float32)
    running = jnp.cumsum(jnp.concatenate([zeros, extended], axis=1), axis=1)
    running_sq = jnp.cumsum(jnp.concatenate([zeros, extended * extended], axis=1), axis=1)
    mean_val = (running[:, WIN:] - running[:, :count]) * (1.0 / WIN)
    mean_sq = (running_sq[:, WIN:] - running_sq[:, :count]) * (1.0 / WIN)
    spread = jnp.maximum(mean_sq - mean_val * mean_val, 0.0)
    scale = lax.rsqrt(spread + EPS)
    starts = jnp.arange(count, dtype=jnp.int32)
    index = starts[:, None] + jnp.arange(WIN, dtype=jnp.int32)[None, :]
    gathered = extended[:, index]
    normed = (gathered - mean_val[:, :, None]) * scale[:, :, None]
    return normed.astype(jnp.bfloat16)


def validity(block, lengths, rows, total):
    local = jnp.arange(rows, dtype=jnp.int32)
    seg_len = rows // 2
    pair = lax.dynamic_slice_in_dim(lengths, block * 2, 2)
    limit = jnp.where(local < seg_len, pair[0], pair[1])
    offset = local % seg_len
    return (offset < limit) & (block * rows + local <= total - WIN)


def body(series, lengths):
    rows = series.shape[1]
    total = rows * lax.axis_size("tm")
    excl = WIN // 4
    block = lax.axis_index("tm")
    tail = passed_along(series[:, : WIN - 1], "tm", -1)
    extended = jnp.concatenate([series, tail], axis=1)
    rows_z = windows_of(extended)
    rows_ok = validity(block, lengths, rows, total)
    local = jnp.arange(rows, dtype=jnp.int32)
    best = jnp.full((local.shape[0],), MASKED, jnp.float32)
    cols_z = rows_z
    for step in range(STEPS + 1):
        if step > 0:
            cols_z = passed_along(cols_z, "tm", 1)
        other = block - step
        safe = jnp.maximum(other, 0)
        cols_ok = validity(safe, lengths, rows, total) & (other >= 0)
        partial_value = lax.dot_general(
            rows_z, cols_z, (((0, 2), (0, 2)), ((), ())), preferred_element_type=jnp.float32
        )
        summed = over_copies(partial_value, "chan")
        score = summed * (1.0 / WIN)
        lag = step * rows + local[:, None] - local[None, :]
        keep = rows_ok[:, None] & cols_ok[None, :] & (lag >= excl)
        best = jnp.maximum(best, jnp.max(jnp.where(keep, score, MASKED), axis=1))
    peak = jnp.where(best > 0.5 * MASKED, best, 0.0)
    return peak


def solution(mesh):
    return jax.shard_map(
        body,
        mesh=mesh,
        in_specs=(P("chan", "tm"), P()),
        out_specs=P("tm"),
        check_vma=False,
    )
```

profile of v0, /device:TPU:108, one launch (start us, length us, event | category | flops | bytes accessed | tf_op | source)
XLA Modules:
  0.0 689.8 jit_solution(11564945917627100405)
XLA Ops:
  0.0 0.9 copy.18
  0.9 2.3 collective-permute-start
  3.5 9.1 %collective-permute-done = f32[64,255]{0,1:T(8,128)S(1)} collective-permute-done((f32[64,255]{0,1:T(8,128)S(1)}, f32[64,255]{0,1:T(8,128)S(1)}, u32[]{:S(2)}, u32[]{:S(2)}) %collective-permute-start) | collective-permute-done | bytes 65312 | tf_op jit(solution)/shard_map/ppermute | solution.py:17
  12.8 1.2 reduce-window.16
  14.3 0.9 copy_bitcast_fusion.2
  15.3 1.2 reduce-window.14
  16.7 215.5 %gather_fusion = f32[65536,64]{1,0:T(8,128)} fusion(f32[64,511]{0,1:T(8,128)S(1)} %get-tuple-element.11, s32[65536]{0:T(1024)S(1)} %broadcast_clamp_fusion), kind=kCustom, calls=%fused_computation | custom fusion | bytes 33816576 | tf_op jit(solution)/shard_map/gather | solution.py:43
  232.2 26.2 %copy.25 = f32[256,256,64]{1,0,2:T(8,128)} copy(f32[256,256,64]{2,1,0:T(8,128)} %bitcast.49) | data formatting | bytes 33554432 | tf_op jit(solution)/shard_map/gather | solution.py:43
  258.5 7.6 %fusion.1 = bf16[64,256,256]{2,1,0:T(8,128)(2,1)S(1)} fusion(f32[256,256,64]{1,0,2:T(8,128)} %copy.25, f32[64,256]{1,0:T(8,128)S(1)} %get-tuple-element.8, f32[64,256]{1,0:T(8,128)S(1)} %get-tuple-element.9), kind=kLoop, calls=%fused_computation.3 | loop fusion | flops 12582912 | bytes 25296896 | tf_op jit(solution)/shard_map/convert_element_type | solution.py:45
  266.2 3.2 copy-done
  269.4 1.9 collective-permute-start.1
  271.3 181.4 %collective-permute-done.1 = bf16[64,256,256]{2,1,0:T(8,128)(2,1)} collective-permute-done((bf16[64,256,256]{2,1,0:T(8,128)(2,1)S(1)}, bf16[64,256,256]{2,1,0:T(8,128)(2,1)}, u32[]{:S(2)}, u32[]{:S(2)}) %collective-permute-start.1) | collective-permute-done | bytes 8388640 | tf_op jit(solution)/shard_map/ppermute | solution.py:17
  452.7 6.7 collective-permute-start.2
  459.4 8.1 %convolution_bitcast_fusion.2 = f32[256,256]{1,0:T(8,128)S(1)} fusion(bf16[64,256,256]{2,1,0:T(8,128)(2,1)} %copy-done), kind=kOutput, calls=%fused_computation.6 | convolution fusion | flops 2147483648 | bytes 8650752 | tf_op jit(solution)/shard_map/dot_general | solution.py:75
  467.5 1.2 broadcast_in_dim.82
  468.7 3.5 all-to-all-start
  472.2 8.1 %convolution_bitcast_fusion.1 = f32[256,256]{1,0:T(8,128)S(1)} fusion(bf16[64,256,256]{2,1,0:T(8,128)(2,1)} %copy-done, bf16[64,256,256]{2,1,0:T(8,128)(2,1)} %collective-permute-done.1), kind=kOutput, calls=%fused_computation.5 | convolution fusion | flops 2147483648 | bytes 17039360 | tf_op jit(solution)/shard_map/dot_general | solution.py:75
  480.3 170.3 %all-to-all-done = f32[4,256,256]{2,1,0:T(8,128)S(1)} async-done(((f32[4,256,256]{2,1,0:T(8,128)}), f32[4,256,256]{2,1,0:T(8,128)S(1)}, u32[]{:S(2)}, u32[]{:S(2)}) %all-to-all-start) | async-done | bytes 1048608 | tf_op jit(solution)/shard_map/all_to_all | solution.py:22
  650.7 1.2 broadcast_in_dim.87
  651.8 3.5 all-to-all-start.1
  655.4 8.1 %convolution_bitcast_fusion = f32[256,256]{1,0:T(8,128)S(1)} fusion(bf16[64,256,256]{2,1,0:T(8,128)(2,1)} %copy-done, bf16[64,256,256]{2,1,0:T(8,128)(2,1)} %collective-permute-done.2), kind=kOutput, calls=%fused_computation.4 | convolution fusion | flops 2147483648 | bytes 17039360 | tf_op jit(solution)/shard_map/dot_general | solution.py:75
  663.5 6.3 all-to-all-done.1
  669.8 1.1 broadcast_in_dim.90
  670.9 3.5 all-to-all-start.2
  674.5 0.7 fusion.17
  675.1 1.3 compare_and_fusion
  676.4 0.7 fusion.14
  677.1 1.3 and_and_fusion
  678.4 1.2 and_and_fusion.1
  679.6 1.3 and_and_fusion.2
  681.0 7.8 %all-to-all-done.2 = f32[4,256,256]{2,1,0:T(8,128)S(1)} async-done(((f32[4,256,256]{2,1,0:T(8,128)}), f32[4,256,256]{2,1,0:T(8,128)S(1)}, u32[]{:S(2)}, u32[]{:S(2)}) %all-to-all-start.2) | async-done | bytes 1048608 | tf_op jit(solution)/shard_map/all_to_all | solution.py:22
  689.3 0.6 compare_select_fusion.1
  (32 shorter events, 1.8 us)
Async XLA Ops:
  0.9 11.6 %collective-permute-start = (f32[64,255]{0,1:T(8,128)S(1)}, f32[64,255]{0,1:T(8,128)S(1)}, u32[]{:S(2)}, u32[]{:S(2)}) collective-permute-start(f32[64,255]{0,1:T(8,128)S(1)} %bitcast.52), channel_id=1, source_target_pairs={{4,0},{8,4},{12,8},{16,12},{20,16},{24,20},{28,24},{32,28},{36,32}... | collective-permute-start | bytes 195848 | tf_op jit(solution)/shard_map/ppermute | solution.py:17
  14.2 218.0 %copy-start.1 = (f32[64,5]{0,1:T(8,128)}, f32[64,5]{0,1:T(8,128)S(1)}, u32[]{:S(2)}) copy-start(f32[64,5]{0,1:T(8,128)S(1)} %reduce-window.19) | copy-start | bytes 3844
  16.7 215.5 %copy-start.2 = (f32[64,5]{0,1:T(8,128)}, f32[64,5]{0,1:T(8,128)S(1)}, u32[]{:S(2)}) copy-start(f32[64,5]{0,1:T(8,128)S(1)} %reduce-window.15) | copy-start | bytes 3844
  232.2 26.2 %slice-start = ((f32[64,5]{0,1:T(8,128)}), f32[64,4]{0,1:T(4,128)S(1)}, s32[]{:S(2)}) async-start(f32[64,5]{0,1:T(8,128)} %copy-done.1), calls=%async_computation.3 | async-start | bytes 4096 | tf_op jit(solution)/shard_map/slice.3
  232.2 26.2 %slice-start.1 = ((f32[64,5]{0,1:T(8,128)}), f32[64,4]{0,1:T(4,128)S(1)}, s32[]{:S(2)}) async-start(f32[64,5]{0,1:T(8,128)} %copy-done.2), calls=%async_computation.4 | async-start | bytes 4096 | tf_op jit(solution)/shard_map/slice.1
  266.2 3.2 copy-start
  269.4 183.3 %collective-permute-start.1 = (bf16[64,256,256]{2,1,0:T(8,128)(2,1)S(1)}, bf16[64,256,256]{2,1,0:T(8,128)(2,1)}, u32[]{:S(2)}, u32[]{:S(2)}) collective-permute-start(bf16[64,256,256]{2,1,0:T(8,128)(2,1)S(1)} %fusion.1), channel_id=1, source_target_pairs={{0,4},{4,8},{8,12},{12,16},{16,20},{20,24},{24,28},{28,32},{32,36}... | collective-permute-start | bytes 25165832 | tf_op jit(solution)/shard_map/ppermute | solution.py:17
  452.7 202.7 %collective-permute-start.2 = (bf16[64,256,256]{2,1,0:T(8,128)(2,1)}, bf16[64,256,256]{2,1,0:T(8,128)(2,1)}, u32[]{:S(2)}, u32[]{:S(2)}) collective-permute-start(bf16[64,256,256]{2,1,0:T(8,128)(2,1)} %collective-permute-done.1), channel_id=1, source_target_pairs={{0,4},{4,8},{8,12},{12,16},{16,20},{20,24},{24,28},{28,32},{32,36}... | collective-permute-start | bytes 25165832 | tf_op jit(solution)/shard_map/ppermute | solution.py:17
  468.7 182.0 %all-to-all-start = ((f32[4,256,256]{2,1,0:T(8,128)}), f32[4,256,256]{2,1,0:T(8,128)S(1)}, u32[]{:S(2)}, u32[]{:S(2)}) async-start(f32[4,256,256]{2,1,0:T(8,128)} %broadcast_in_dim.82), calls=%async_computation | async-start | bytes 2097152 | tf_op jit(solution)/shard_map/all_to_all | solution.py:22
  651.8 18.0 %all-to-all-start.1 = ((f32[4,256,256]{2,1,0:T(8,128)}), f32[4,256,256]{2,1,0:T(8,128)S(1)}, u32[]{:S(2)}, u32[]{:S(2)}) async-start(f32[4,256,256]{2,1,0:T(8,128)} %broadcast_in_dim.87), calls=%async_computation.1 | async-start | bytes 2097152 | tf_op jit(solution)/shard_map/all_to_all | solution.py:22
  655.4 19.0 %copy-start.3 = (s32[64]{0:T(128)S(1)}, s32[64]{0:T(128)}, u32[]{:S(2)}) copy-start(s32[64]{0:T(128)} %param.3) | copy-start | bytes 772
  670.9 18.0 %all-to-all-start.2 = ((f32[4,256,256]{2,1,0:T(8,128)}), f32[4,256,256]{2,1,0:T(8,128)S(1)}, u32[]{:S(2)}, u32[]{:S(2)}) async-start(f32[4,256,256]{2,1,0:T(8,128)} %broadcast_in_dim.90), calls=%async_computation.2 | async-start | bytes 2097152 | tf_op jit(solution)/shard_map/all_to_all | solution.py:22
where the time goes:
time: 691 us; the launch traced here: 690 us
  waiting for transfers between devices  375 us (54%)
  local copies, waits for them, and re-layouts  251 us (36%)
  matrix products  24.4 us (4%)
  starting transfers between devices  21.5 us (3%)
  other arithmetic  17.5 us (3%)
    gather x2, local copies, waits for them, and re-layouts, windows_of(): gathered = extended[:, index]  242 us
    ppermute x3, waiting for transfers between devices, passed_along(): return lax.ppermute(block, axis, route)  190 us
    all_to_all x3, waiting for transfers between devices, from_everyone(): lax.all_to_all(jnp.broadcast_to(value[None], (devices, *value.shape)), ax...  184 us
    dot_general x3, matrix products, body(): lax.dot_general(rows_z, cols_z, (((0, 2), (0, 2)), ((), ())), preferred_e...  24.4 us
  transfers between devices with their start and end apart: 6, of which 5 were waited for; matrix products, arithmetic and copies ran while one was open for 5% of the time, Pallas kernels for 0%

commit v1 on v0

v1 whole, which is shorter than its diff:
```python
import functools

import jax
import jax.numpy as jnp
from jax import lax
from jax.experimental import pallas as pl
from jax.experimental.pallas import tpu as pltpu
from jax.sharding import PartitionSpec as P

WIN = 256
HALF = WIN // 2
STEPS = 2
EPS = 1e-05
MASKED = -1000000000.0
EXCL = WIN // 4
KC = 16


def shifted(block, axis, distance):
    devices = range(lax.axis_size(axis))
    route = [(i - distance, i) for i in devices if i - distance in devices]
    return lax.ppermute(block, axis, route)


def swapped(block, axis, distance):
    count = lax.axis_size(axis)
    return lax.ppermute(block, axis, [(i, (i + distance) % count) for i in range(count)])


def corr_kernel(rows, cols, b2, b1, b0, bn, out, x2, ma, mb, va, vb, za, zb, acc):
    total = (STEPS + 1) * rows
    span = total + HALF
    joined = jnp.concatenate([b2[...], b1[...], b0[...], bn[...]], axis=1)
    both = jnp.concatenate([joined[:, :span], joined[:, HALF : HALF + span]], axis=0)
    for at in range(0, span, 128):
        x2[at : at + 128, :] = both[:, at : at + 128].T

    size = 128
    pieces = span // size
    length = 1
    src_m, src_v = x2, None
    bufs = [(ma, va), (mb, vb)]
    level = 0
    while length < HALF:
        dst_m, dst_v = bufs[level % 2]

        def step(p, carry, src_m=src_m, src_v=src_v, dst_m=dst_m, dst_v=dst_v, length=length):
            base = pl.multiple_of(p * size, size)
            m0 = src_m[pl.ds(base, size), :]
            m1 = src_m[pl.ds(base + length, size), :]
            gap = m0 - m1
            spread = gap * gap * (0.5 * length)
            if src_v is not None:
                spread = spread + (src_v[pl.ds(base, size), :] + src_v[pl.ds(base + length, size), :])
            dst_m[pl.ds(base, size), :] = (m0 + m1) * 0.5
            dst_v[pl.ds(base, size), :] = spread
            return carry

        lax.fori_loop(0, pieces, step, 0)
        src_m, src_v = dst_m, dst_v
        length *= 2
        level += 1
    end_m, end_v = bufs[level % 2]
    for at in range(0, total, size):
        m0 = src_m[at : at + size, :]
        v0 = src_v[at : at + size, :]
        m1 = pltpu.roll(m0, 64, 1)
        v1 = pltpu.roll(v0, 64, 1)
        gap = m0 - m1
        var = (v0 + v1 + gap * gap * (0.5 * HALF)) * (1.0 / WIN)
        end_m[at : at + size, :] = (m0 + m1) * 0.5
        end_v[at : at + size, :] = lax.rsqrt(var + EPS)

    group = 64

    def build(chunk, z):
        base = pl.multiple_of(chunk * KC, KC)
        for at in range(0, total, group):
            mean = end_m[at : at + group, :]
            scale = end_v[at : at + group, :]
            for k in range(KC):
                x = x2[pl.ds(base + (at + k), group), :]
                z[at : at + group, k * 128 : (k + 1) * 128] = ((x - mean) * scale).astype(jnp.bfloat16)

    def product(z):
        acc[...] += lax.dot_general(
            z[:cols, :], z[total - rows :, :], (((1,), (1,)), ((), ())), preferred_element_type=jnp.float32
        )

    acc[...] = jnp.zeros_like(acc)
    chunks = HALF // KC
    build(0, za)

    def pair(p, carry):
        build(2 * p + 1, zb)
        product(za)
        build(2 * p + 2, za)
        product(zb)
        return carry

    lax.fori_loop(0, chunks // 2 - 1, pair, 0)
    build(chunks - 1, zb)
    product(za)
    product(zb)
    out[...] = acc[...].astype(out.dtype)


def peak_kernel(rows, quarter, lens, p0, p1, p2, p3, out):
    block = lax.axis_index("tm")
    part = lax.axis_index("chan")
    total_rows = rows * lax.axis_size("tm")
    seg = rows // 2
    n_seg = 2 * (STEPS + 1)
    summed = (p0[...].astype(jnp.float32) + p1[...].astype(jnp.float32)) + (
        p2[...].astype(jnp.float32) + p3[...].astype(jnp.float32)
    )
    score = summed * (1.0 / WIN)
    shape = score.shape
    j = part * quarter + lax.broadcasted_iota(jnp.int32, shape, 0)
    i = STEPS * rows + lax.broadcasted_iota(jnp.int32, shape, 1)
    first = (block - STEPS) * rows
    limit = jnp.zeros(shape, jnp.int32)
    for s in range(n_seg):
        which = (block - STEPS) * 2 + s
        here = lens[jnp.maximum(which, 0)]
        here = jnp.where(which >= 0, here, 0)
        limit = jnp.where(j // seg == s, here, limit)
    last = total_rows - WIN
    ok = (j % seg < limit) & (j + first <= last) & (i - j >= EXCL)
    best = jnp.max(jnp.where(ok, score, MASKED), axis=0, keepdims=True)
    r = lax.broadcasted_iota(jnp.int32, best.shape, 1)
    own = jnp.where(r < seg, lens[block * 2], lens[block * 2 + 1])
    row_ok = (r % seg < own) & (block * rows + r <= last)
    out[...] = jnp.where(row_ok, best, MASKED)


def body(series, lengths):
    chans, rows = series.shape
    parts = lax.axis_size("chan")
    total = (STEPS + 1) * rows
    cols = total - EXCL
    quarter = cols // parts
    b1 = shifted(series, "tm", 1)
    b2 = shifted(series, "tm", 2)
    bn = shifted(series, "tm", -1)
    vmem = pl.BlockSpec(memory_space=pltpu.VMEM)
    f32 = jnp.float32
    room = total + HALF + HALF
    partial_value = pl.pallas_call(
        functools.partial(corr_kernel, rows, cols),
        out_shape=jax.ShapeDtypeStruct((cols, rows), f32),
        in_specs=[vmem] * 4,
        out_specs=vmem,
        scratch_shapes=[pltpu.VMEM((room, 128), f32)] * 5
        + [pltpu.VMEM((total, KC * 128), jnp.bfloat16)] * 2
        + [pltpu.VMEM((cols, rows), f32)],
        compiler_params=pltpu.CompilerParams(vmem_limit_bytes=40 << 20),
    )(b2, b1, series, bn)
    pieces = partial_value.reshape(parts, quarter, rows)
    got = lax.all_to_all(pieces, "chan", 0, 0, tiled=True)
    best = pl.pallas_call(
        functools.partial(peak_kernel, rows, quarter),
        out_shape=jax.ShapeDtypeStruct((1, rows), f32),
        in_specs=[pl.BlockSpec(memory_space=pltpu.SMEM)] + [vmem] * 4,
        out_specs=vmem,
    )(lengths, got[0], got[1], got[2], got[3])
    best = best.reshape(rows)
    others = [swapped(best, "chan", d) for d in range(1, parts)]
    for other in others:
        best = jnp.maximum(best, other)
    return jnp.where(best > 0.5 * MASKED, best, 0.0)


def solution(mesh):
    return jax.shard_map(
        body,
        mesh=mesh,
        in_specs=(P("chan", "tm"), P()),
        out_specs=P("tm"),
        check_vma=False,
    )
```

time: 691 us -> 53.1 us (0.08)
  waiting for transfers between devices: 375 us -> 11.9 us
  local copies, waits for them, and re-layouts: 251 us -> 2.4 us
  matrix products: 24.4 us -> 0 us
  other arithmetic: 17.5 us -> 0.57 us
  blocking collectives: 0 us -> 14.1 us
  Pallas kernels: 0 us -> 13.2 us
  starting transfers between devices: 21.5 us -> 10.5 us
    gather x2 -> x0, local copies, waits for them, and re-layouts: 242 us -> none  [windows_of(): gathered = extended[:, index]]
    all_to_all x3 -> x0, waiting for transfers between devices: 184 us -> none  [from_everyone(): lax.all_to_all(jnp.broadcast_to(value[None], (devices, *value.shape)), ax...]
    ppermute x3 -> x6, waiting for transfers between devices: 190 us -> 11.9 us  [the longest x3 8.95 us: shifted(): return lax.ppermute(block, axis, route)]
    dot_general x3 -> x0, matrix products: 24.4 us -> none  [body(): lax.dot_general(rows_z, cols_z, (((0, 2), (0, 2)), ((), ())), preferred_e...]
    all_to_all x0 -> x1, blocking collectives: none -> 14.1 us  [body(): got = lax.all_to_all(pieces, 'chan', 0, 0, tiled=True)]
    pallas_call x0 -> x2, Pallas kernels: none -> 13.2 us  [the longest x1 11.3 us: body(): pl.pallas_call(functools.partial(corr_kernel, rows, cols), out_shape=jax....]
    all_to_all x3 -> x0, starting transfers between devices: 10.5 us -> none  [from_everyone(): lax.all_to_all(jnp.broadcast_to(value[None], (devices, *value.shape)), ax...]
    convert_element_type x1 -> x0, other arithmetic: 7.6 us -> none  [windows_of(): return normed.astype(jnp.bfloat16)]
  transfers between devices with their start and end apart: 6 -> 6, of which waited for: 5 -> 4; matrix products, arithmetic and copies ran while one was open for 5% -> 0% of each run, Pallas kernels for 0% -> 0%
where the time goes in v1:
time: 53.1 us; the launch traced here: 52.9 us
  blocking collectives  14.1 us (27%)
  Pallas kernels  13.2 us (25%)
  waiting for transfers between devices  11.9 us (22%)
  starting transfers between devices  10.5 us (20%)
  local copies, waits for them, and re-layouts  2.4 us (5%)
  other arithmetic  0.57 us (1%)
    all_to_all x1, blocking collectives, body(): got = lax.all_to_all(pieces, 'chan', 0, 0, tiled=True)  14.1 us
    pallas_call x1, Pallas kernels, body(): pl.pallas_call(functools.partial(corr_kernel, rows, cols), out_shape=jax....  11.3 us
    ppermute x3, starting transfers between devices, shifted(): return lax.ppermute(block, axis, route)  9.15 us
    ppermute x3, waiting for transfers between devices, shifted(): return lax.ppermute(block, axis, route)  8.95 us
    ppermute x3, waiting for transfers between devices, swapped(): lax.ppermute(block, axis, [(i, (i + distance) % count) for i in range(cou...  2.99 us
    pallas_call x1, Pallas kernels, body(): pl.pallas_call(functools.partial(peak_kernel, rows, quarter), out_shape=j...  1.98 us
    unnamed x4, local copies, waits for them, and re-layouts  1.52 us
    ppermute x3, starting transfers between devices, swapped(): lax.ppermute(block, axis, [(i, (i + distance) % count) for i in range(cou...  1.4 us
  transfers between devices with their start and end apart: 6, of which 4 were waited for; matrix products, arithmetic and copies ran while one was open for 0% of the time, Pallas kernels for 0%

profile of v1, /device:TPU:108, one launch (start us, length us, event | category | flops | bytes accessed | tf_op | source)
XLA Modules:
  0.0 52.9 jit_solution(1854773052034379495)
XLA Ops:
  0.0 2.1 %collective-permute-start.1 = (f32[64,256]{1,0:T(8,128)}, f32[64,256]{1,0:T(8,128)S(1)}, u32[]{:S(2)}, u32[]{:S(2)}) collective-permute-start(f32[64,256]{1,0:T(8,128)} %b0.1), channel_id=1, source_target_pairs={{0,4},{4,8},{8,12},{12,16},{16,20},{20,24},{24,28},{28,32},{32,36}... | collective-permute-start | bytes 196616 | tf_op jit(solution)/shard_map/ppermute | solution.py:22
  2.1 5.2 %collective-permute-start = (f32[64,256]{1,0:T(8,128)}, f32[64,256]{1,0:T(8,128)S(1)}, u32[]{:S(2)}, u32[]{:S(2)}) collective-permute-start(f32[64,256]{1,0:T(8,128)} %b0.1), channel_id=1, source_target_pairs={{0,8},{4,12},{8,16},{12,20},{16,24},{20,28},{24,32},{28,36},{32,40... | collective-permute-start | bytes 196616 | tf_op jit(solution)/shard_map/ppermute | solution.py:22
  7.2 1.9 %collective-permute-start.2 = (f32[64,256]{1,0:T(8,128)}, f32[64,256]{1,0:T(8,128)S(1)}, u32[]{:S(2)}, u32[]{:S(2)}) collective-permute-start(f32[64,256]{1,0:T(8,128)} %b0.1), channel_id=1, source_target_pairs={{4,0},{8,4},{12,8},{16,12},{20,16},{24,20},{28,24},{32,28},{36,32}... | collective-permute-start | bytes 196616 | tf_op jit(solution)/shard_map/ppermute | solution.py:22
  9.2 0.0 collective-permute-done.1.b1
  9.2 0.7 %collective-permute-done.b2 = f32[64,256]{1,0:T(8,128)S(1)} collective-permute-done((f32[64,256]{1,0:T(8,128)}, f32[64,256]{1,0:T(8,128)S(1)}, u32[]{:S(2)}, u32[]{:S(2)}) %collective-permute-start) | collective-permute-done | bytes 65568 | tf_op jit(solution)/shard_map/ppermute | solution.py:22
  9.9 8.2 %collective-permute-done.2.bn = f32[64,256]{1,0:T(8,128)S(1)} collective-permute-done((f32[64,256]{1,0:T(8,128)}, f32[64,256]{1,0:T(8,128)S(1)}, u32[]{:S(2)}, u32[]{:S(2)}) %collective-permute-start.2) | collective-permute-done | bytes 65568 | tf_op jit(solution)/shard_map/ppermute | solution.py:22
  18.1 0.0 copy-start
  18.1 0.8 %copy-done = f32[64,256]{1,0:T(8,128)S(1)} copy-done((f32[64,256]{1,0:T(8,128)S(1)}, f32[64,256]{1,0:T(8,128)}, u32[]{:S(2)}) %copy-start) | copy-done | bytes 65560
  19.0 11.3 %shard_map.28 = f32[704,256]{1,0:T(8,128)S(1)} custom-call(f32[64,256]{1,0:T(8,128)S(1)} %collective-permute-done.b2, f32[64,256]{1,0:T(8,128)S(1)} %collective-permute-done.1.b1, f32[64,256]{1,0:T(8,128)S(1)} %copy-done, f32[64,256]{1,0:T(8,128)S(1)} %collective-permute-done.2.bn), custom_call_target="tpu_custom_call" | custom-call | tf_op jit(solution)/shard_map/pallas_call | solution.py:149
  30.2 14.1 %all_to_all.5 = f32[4,176,256]{2,1,0:T(8,128)S(1)} all-to-all(f32[4,176,256]{2,1,0:T(8,128)S(1)} %bitcast.10), channel_id=1, replica_groups=mesh['tm'=32,'chan'=4] {'chan'}, dimensions={0} | all-to-all | bytes 1441792 | tf_op jit(solution)/shard_map/all_to_all | solution.py:160
  44.4 0.9 %slice_bitcast_fusion = (f32[176,256]{1,0:T(8,128)}, f32[176,256]{1,0:T(8,128)}, f32[176,256]{1,0:T(8,128)}, f32[176,256]{1,0:T(8,128)}) fusion(f32[4,176,256]{2,1,0:T(8,128)S(1)} %all_to_all.5), kind=kLoop, calls=%fused_computation | loop fusion | bytes 1441792 | tf_op jit(solution)/shard_map/squeeze | solution.py:166
  45.2 2.0 %shard_map.29 = f32[1,256]{1,0:T(1,128)} custom-call(s32[64]{0:T(128)} %lens.1, f32[176,256]{1,0:T(8,128)} %get-tuple-element.8.p0, f32[176,256]{1,0:T(8,128)} %get-tuple-element.7.p1, f32[176,256]{1,0:T(8,128)} %get-tuple-element.6.p2, f32[176,256]{1,0:T(8,128)} %get-tuple-element.5.p3), custom_call_target="tpu_custom_call" | custom-call | tf_op jit(solution)/shard_map/pallas_call | solution.py:161
  47.2 0.0 copy-start.1
  47.2 0.7 %copy-done.1 = f32[1,256]{1,0:T(1,128)S(1)} copy-done((f32[1,256]{1,0:T(1,128)S(1)}, f32[1,256]{1,0:T(1,128)}, u32[]{:S(2)}) %copy-start.1) | copy-done | bytes 1048
  47.9 0.0 collective-permute-start.5
  47.9 1.4 %collective-permute-start.4 = (f32[256]{0:T(256)S(1)}, f32[256]{0:T(256)S(1)}, u32[]{:S(2)}, u32[]{:S(2)}) collective-permute-start(f32[256]{0:T(256)S(1)} %bitcast.12), channel_id=1, source_target_pairs={{0,2},{1,3},{2,0},{3,1},{4,6},{5,7},{6,4},{7,5},{8,10},{9,11},{10,... | collective-permute-start | bytes 3080 | tf_op jit(solution)/shard_map/ppermute | solution.py:27
  49.3 0.0 collective-permute-start.3
  49.3 0.0 collective-permute-done.5
  49.3 2.2 %collective-permute-done.4 = f32[256]{0:T(256)S(1)} collective-permute-done((f32[256]{0:T(256)S(1)}, f32[256]{0:T(256)S(1)}, u32[]{:S(2)}, u32[]{:S(2)}) %collective-permute-start.4) | collective-permute-done | bytes 1056 | tf_op jit(solution)/shard_map/ppermute | solution.py:27
  51.5 0.8 %collective-permute-done.3 = f32[256]{0:T(256)S(1)} collective-permute-done((f32[256]{0:T(256)S(1)}, f32[256]{0:T(256)S(1)}, u32[]{:S(2)}, u32[]{:S(2)}) %collective-permute-start.3) | collective-permute-done | bytes 1056 | tf_op jit(solution)/shard_map/ppermute | solution.py:27
  52.3 0.6 %compare_select_fusion = f32[256]{0:T(256)} fusion(f32[256]{0:T(256)S(1)} %collective-permute-done.5, f32[256]{0:T(256)S(1)} %collective-permute-done.4, f32[256]{0:T(256)S(1)} %bitcast.14, f32[256]{0:T(256)S(1)} %collective-permute-done.3), kind=kLoop, calls=%fused_computation.4 | loop fusion | flops 1280 | bytes 5120 | tf_op jit(solution)/shard_map/jit(_where)/select_n | solution.py:171
Async XLA Ops:
  0.0 9.2 %collective-permute-start.1 = (f32[64,256]{1,0:T(8,128)}, f32[64,256]{1,0:T(8,128)S(1)}, u32[]{:S(2)}, u32[]{:S(2)}) collective-permute-start(f32[64,256]{1,0:T(8,128)} %b0.1), channel_id=1, source_target_pairs={{0,4},{4,8},{8,12},{12,16},{16,20},{20,24},{24,28},{28,32},{32,36}... | collective-permute-start | bytes 196616 | tf_op jit(solution)/shard_map/ppermute | solution.py:22
  2.1 7.9 %collective-permute-start = (f32[64,256]{1,0:T(8,128)}, f32[64,256]{1,0:T(8,128)S(1)}, u32[]{:S(2)}, u32[]{:S(2)}) collective-permute-start(f32[64,256]{1,0:T(8,128)} %b0.1), channel_id=1, source_target_pairs={{0,8},{4,12},{8,16},{12,20},{16,24},{20,28},{24,32},{28,36},{32,40... | collective-permute-start | bytes 196616 | tf_op jit(solution)/shard_map/ppermute | solution.py:22
  7.2 10.9 %collective-permute-start.2 = (f32[64,256]{1,0:T(8,128)}, f32[64,256]{1,0:T(8,128)S(1)}, u32[]{:S(2)}, u32[]{:S(2)}) collective-permute-start(f32[64,256]{1,0:T(8,128)} %b0.1), channel_id=1, source_target_pairs={{4,0},{8,4},{12,8},{16,12},{20,16},{24,20},{28,24},{32,28},{36,32}... | collective-permute-start | bytes 196616 | tf_op jit(solution)/shard_map/ppermute | solution.py:22
  18.1 0.8 %copy-start = (f32[64,256]{1,0:T(8,128)S(1)}, f32[64,256]{1,0:T(8,128)}, u32[]{:S(2)}) copy-start(f32[64,256]{1,0:T(8,128)} %b0.1) | copy-start | bytes 196612
  47.2 0.7 %copy-start.1 = (f32[1,256]{1,0:T(1,128)S(1)}, f32[1,256]{1,0:T(1,128)}, u32[]{:S(2)}) copy-start(f32[1,256]{1,0:T(1,128)} %shard_map.29) | copy-start | bytes 3076
  47.9 1.4 %collective-permute-start.5 = (f32[256]{0:T(256)S(1)}, f32[256]{0:T(256)S(1)}, u32[]{:S(2)}, u32[]{:S(2)}) collective-permute-start(f32[256]{0:T(256)S(1)} %bitcast.11), channel_id=1, source_target_pairs={{0,3},{1,0},{2,1},{3,2},{4,7},{5,4},{6,5},{7,6},{8,11},{9,8},{10,9... | collective-permute-start | bytes 3080 | tf_op jit(solution)/shard_map/ppermute | solution.py:27
  47.9 3.6 %collective-permute-start.4 = (f32[256]{0:T(256)S(1)}, f32[256]{0:T(256)S(1)}, u32[]{:S(2)}, u32[]{:S(2)}) collective-permute-start(f32[256]{0:T(256)S(1)} %bitcast.12), channel_id=1, source_target_pairs={{0,2},{1,3},{2,0},{3,1},{4,6},{5,7},{6,4},{7,5},{8,10},{9,11},{10,... | collective-permute-start | bytes 3080 | tf_op jit(solution)/shard_map/ppermute | solution.py:27
  49.3 3.0 %collective-permute-start.3 = (f32[256]{0:T(256)S(1)}, f32[256]{0:T(256)S(1)}, u32[]{:S(2)}, u32[]{:S(2)}) collective-permute-start(f32[256]{0:T(256)S(1)} %bitcast.13), channel_id=1, source_target_pairs={{0,1},{1,2},{2,3},{3,0},{4,5},{5,6},{6,7},{7,4},{8,9},{9,10},{10,1... | collective-permute-start | bytes 3080 | tf_op jit(solution)/shard_map/ppermute | solution.py:27

commit v2 on v1

v2 whole, which is shorter than its diff:
```python
import functools

import jax
import jax.numpy as jnp
from jax import lax
from jax.experimental import pallas as pl
from jax.experimental.pallas import tpu as pltpu
from jax.sharding import PartitionSpec as P

WIN = 256
HALF = WIN // 2
STEPS = 2
EPS = 1e-05
MASKED = -1000000000.0
EXCL = WIN // 4
KC = 16
LANES = 128
VMEM_LIMIT = 40 << 20
SMALL_LIMIT = 8 << 20


def sent(block, axis, target):
    count = lax.axis_size(axis)
    return lax.ppermute(block, axis, [(i, target(i, count)) for i in range(count)])


def two_on(i, count):
    return (i + 2) % count


def even_pair(i, count):
    return i ^ 1


def odd_pair(i, count):
    if i == 0 or i == count - 1:
        return i
    return i + 1 if i % 2 == 1 else i - 1


def turned(distance):
    return lambda i, count: (i + distance) % count


def window_sums(src_m, bufs, span):
    size = 128
    src_v = None
    length = 1
    level = 0
    while length < HALF:
        dst_m, dst_v = bufs[level % 2]

        def step(p, carry, src_m=src_m, src_v=src_v, dst_m=dst_m, dst_v=dst_v, length=length):
            base = pl.multiple_of(p * size, size)
            m0 = src_m[pl.ds(base, size), :]
            m1 = src_m[pl.ds(base + length, size), :]
            gap = m0 - m1
            spread = gap * gap * (0.5 * length)
            if src_v is not None:
                spread = spread + (src_v[pl.ds(base, size), :] + src_v[pl.ds(base + length, size), :])
            dst_m[pl.ds(base, size), :] = (m0 + m1) * 0.5
            dst_v[pl.ds(base, size), :] = spread
            return carry

        lax.fori_loop(0, span // size, step, 0)
        src_m, src_v = dst_m, dst_v
        length *= 2
        level += 1
    return src_m, src_v, bufs[level % 2]


def corr_kernel(rows, cols, own_far, odd_side, b2, even_side, *refs):
    outs, (own, arrived, x2, ma, mb, va, vb, za, zb, acc) = refs[:4], refs[4:]
    fetch = pltpu.make_async_copy(own_far, own, arrived)
    fetch.start()
    total = (STEPS + 1) * rows
    span = total + HALF
    odd = lax.rem(lax.axis_index("tm"), 2) == 1
    from_odd, from_even = odd_side[...], even_side[...]
    before = jnp.where(odd, from_even, from_odd)
    after = jnp.where(odd, from_odd, from_even)
    fetch.wait()
    joined = jnp.concatenate([b2[...], before, own[...], after], axis=1)
    both = jnp.concatenate([joined[:, :span], joined[:, HALF : HALF + span]], axis=0)
    for at in range(0, span, LANES):
        x2[at : at + LANES, :] = both[:, at : at + LANES].T

    src_m, src_v, (end_m, end_v) = window_sums(x2, [(ma, va), (mb, vb)], span)
    for at in range(0, total, LANES):
        m0 = src_m[at : at + LANES, :]
        v0 = src_v[at : at + LANES, :]
        m1 = pltpu.roll(m0, LANES // 2, 1)
        v1 = pltpu.roll(v0, LANES // 2, 1)
        gap = m0 - m1
        var = (v0 + v1 + gap * gap * (0.5 * HALF)) * (1.0 / WIN)
        end_m[at : at + LANES, :] = (m0 + m1) * 0.5
        end_v[at : at + LANES, :] = lax.rsqrt(var + EPS)

    group = 64

    def build(chunk, z):
        base = pl.multiple_of(chunk * KC, KC)
        for at in range(0, total, group):
            mean = end_m[at : at + group, :]
            scale = end_v[at : at + group, :]
            for k in range(KC):
                x = x2[pl.ds(base + (at + k), group), :]
                z[at : at + group, k * LANES : (k + 1) * LANES] = ((x - mean) * scale).astype(jnp.bfloat16)

    def product(z):
        acc[...] += lax.dot_general(
            z[:cols, :], z[total - rows :, :], (((1,), (1,)), ((), ())), preferred_element_type=jnp.float32
        )

    acc[...] = jnp.zeros_like(acc)
    chunks = HALF // KC
    build(0, za)

    def pair(p, carry):
        build(2 * p + 1, zb)
        product(za)
        build(2 * p + 2, za)
        product(zb)
        return carry

    lax.fori_loop(0, chunks // 2 - 1, pair, 0)
    build(chunks - 1, zb)
    product(za)
    product(zb)
    part = lax.axis_index("chan")
    for d, out in enumerate(outs):
        which = lax.rem(part + d, len(outs))
        size = out.shape[0]
        out[...] = acc[pl.ds(pl.multiple_of(which * size, 16), size), :].astype(out.dtype)


def peak_kernel(rows, lens, p0, p1, p2, p3, out):
    quarter = p0.shape[0]
    block = lax.axis_index("tm")
    part = lax.axis_index("chan")
    last = rows * lax.axis_size("tm") - WIN
    seg = rows // 2
    start = (block - STEPS) * rows
    f32 = jnp.float32
    score = (p0[...] + p1[...].astype(f32)) + (p2[...].astype(f32) + p3[...].astype(f32))
    shape = (quarter, LANES)
    j = part * quarter + lax.broadcasted_iota(jnp.int32, shape, 0)
    stop = jnp.zeros(shape, jnp.int32)
    for s in range(2 * (STEPS + 1)):
        which = (block - STEPS) * 2 + s
        length = jnp.where(which >= 0, lens[jnp.maximum(which, 0)], 0)
        end = jnp.minimum(s * seg + length, last + 1 - start)
        stop = jnp.where(j >= s * seg, end, stop)
    reach = jnp.where(j < stop, j + EXCL, 2 * (STEPS + 1) * rows)
    lane = lax.broadcasted_iota(jnp.int32, shape, 1)
    for at in range(0, rows, LANES):
        i = lane + (STEPS * rows + at)
        best = jnp.max(jnp.where(i >= reach, score[:, at : at + LANES], MASKED), axis=0, keepdims=True)
        out[:, at : at + LANES] = best * (1.0 / WIN)


def close_kernel(rows, lens, a, b, c, d, out):
    block = lax.axis_index("tm")
    last = rows * lax.axis_size("tm") - WIN
    seg = rows // 2
    best = jnp.maximum(jnp.maximum(a[...], b[...]), jnp.maximum(c[...], d[...]))
    r = lax.broadcasted_iota(jnp.int32, best.shape, 1)
    stop = jnp.where(r < seg, lens[block * 2], seg + lens[block * 2 + 1])
    stop = jnp.minimum(stop, last + 1 - block * rows)
    floor = 0.5 * MASKED * (1.0 / WIN)
    out[...] = jnp.where((r < stop) & (best > floor), best, 0.0)


def body(series, lengths):
    chans, rows = series.shape
    parts = lax.axis_size("chan")
    total = (STEPS + 1) * rows
    cols = total - EXCL
    quarter = cols // parts
    b2 = sent(series, "tm", two_on)
    even_side = sent(series, "tm", even_pair)
    odd_side = sent(series, "tm", odd_pair)
    vmem = pl.BlockSpec(memory_space=pltpu.VMEM)
    smem = pl.BlockSpec(memory_space=pltpu.SMEM)
    f32 = jnp.float32
    bf16 = jnp.bfloat16
    room = total + HALF + HALF
    pieces = pl.pallas_call(
        functools.partial(corr_kernel, rows, cols),
        out_shape=[jax.ShapeDtypeStruct((quarter, rows), f32 if d == 0 else bf16) for d in range(parts)],
        in_specs=[pl.BlockSpec(memory_space=pltpu.HBM)] + [vmem] * 3,
        out_specs=[vmem] * parts,
        scratch_shapes=[pltpu.VMEM((chans, rows), f32), pltpu.SemaphoreType.DMA]
        + [pltpu.VMEM((room, LANES), f32)] * 5
        + [pltpu.VMEM((total, KC * LANES), bf16)] * 2
        + [pltpu.VMEM((cols, rows), f32)],
        compiler_params=pltpu.CompilerParams(vmem_limit_bytes=VMEM_LIMIT),
    )(series, odd_side, b2, even_side)
    got = [pieces[0]] + [sent(pieces[d], "chan", turned(d)) for d in range(1, parts)]
    best = pl.pallas_call(
        functools.partial(peak_kernel, rows),
        out_shape=jax.ShapeDtypeStruct((1, rows), f32),
        in_specs=[smem] + [vmem] * parts,
        out_specs=vmem,
        compiler_params=pltpu.CompilerParams(vmem_limit_bytes=SMALL_LIMIT),
    )(lengths, *got)
    all_best = [best] + [sent(best, "chan", turned(d)) for d in range(1, parts)]
    peak = pl.pallas_call(
        functools.partial(close_kernel, rows),
        out_shape=jax.ShapeDtypeStruct((1, rows), f32),
        in_specs=[smem] + [vmem] * parts,
        out_specs=vmem,
        compiler_params=pltpu.CompilerParams(vmem_limit_bytes=SMALL_LIMIT),
    )(lengths, *all_best)
    return peak.reshape(rows)


def solution(mesh):
    return jax.shard_map(
        body,
        mesh=mesh,
        in_specs=(P("chan", "tm"), P()),
        out_specs=P("tm"),
        check_vma=False,
    )
```

time: 53.1 us -> 40.5 us (0.76)
  the two profiles are of different devices: /device:TPU:108 before, /device:TPU:16 now
where the time goes in v2:
time: 40.5 us; the launch traced here: 40.3 us
  starting transfers between devices  15.4 us (38%)
  Pallas kernels  13.2 us (33%)
  waiting for transfers between devices  10.8 us (27%)
  local copies, waits for them, and re-layouts  0.84 us (2%)
    ppermute x9, starting transfers between devices, sent(): lax.ppermute(block, axis, [(i, target(i, count)) for i in range(count)])  15.4 us
    pallas_call x1, Pallas kernels, body(): pl.pallas_call(functools.partial(corr_kernel, rows, cols), out_shape=[jax...  11.4 us
    ppermute x9, waiting for transfers between devices, sent(): lax.ppermute(block, axis, [(i, target(i, count)) for i in range(count)])  10.8 us
    pallas_call x1, Pallas kernels, body(): pl.pallas_call(functools.partial(close_kernel, rows), out_shape=jax.Shape...  1.12 us
    unnamed x4, local copies, waits for them, and re-layouts  0.84 us
  transfers between devices with their start and end apart: 9, of which 6 were waited for; matrix products, arithmetic and copies ran while one was open for 0% of the time, Pallas kernels for 0%

profile of v2, /device:TPU:16, one launch (start us, length us, event | category | flops | bytes accessed | tf_op | source)
XLA Modules:
  0.0 40.3 jit_solution(7301483480448029988)
XLA Ops:
  0.0 3.9 %collective-permute-start.1 = (f32[64,256]{1,0:T(8,128)}, f32[64,256]{1,0:T(8,128)S(1)}, u32[]{:S(2)}, u32[]{:S(2)}) collective-permute-start(f32[64,256]{1,0:T(8,128)} %own_far.1), channel_id=1, source_target_pairs={{0,8},{4,12},{8,16},{12,20},{16,24},{20,28},{24,32},{28,36},{32,40... | collective-permute-start | bytes 196616 | tf_op jit(solution)/shard_map/ppermute | solution.py:24
  3.9 5.9 %collective-permute-start = (f32[64,256]{1,0:T(8,128)}, f32[64,256]{1,0:T(8,128)S(1)}, u32[]{:S(2)}, u32[]{:S(2)}) collective-permute-start(f32[64,256]{1,0:T(8,128)} %own_far.1), channel_id=1, source_target_pairs={{0,0},{4,8},{8,4},{12,16},{16,12},{20,24},{24,20},{28,32},{32,28},... | collective-permute-start | bytes 196616 | tf_op jit(solution)/shard_map/ppermute | solution.py:24
  9.8 0.1 collective-permute-start.2
  9.9 0.0 collective-permute-done.1.b2
  9.9 4.8 %collective-permute-done.odd_side = f32[64,256]{1,0:T(8,128)S(1)} collective-permute-done((f32[64,256]{1,0:T(8,128)}, f32[64,256]{1,0:T(8,128)S(1)}, u32[]{:S(2)}, u32[]{:S(2)}) %collective-permute-start) | collective-permute-done | bytes 65568 | tf_op jit(solution)/shard_map/ppermute | solution.py:24
  14.7 0.0 collective-permute-done.2.even_side
  14.8 0.0 copy-start
  14.8 0.8 %copy-done = f32[64,256]{1,0:T(8,128)S(1)} copy-done((f32[64,256]{1,0:T(8,128)S(1)}, f32[64,256]{1,0:T(8,128)}, u32[]{:S(2)}) %copy-start) | copy-done | bytes 65560
  15.6 11.4 %shard_map.28 = (f32[176,256]{1,0:T(8,128)S(1)}, bf16[176,256]{1,0:T(8,128)(2,1)S(1)}, bf16[176,256]{1,0:T(8,128)(2,1)S(1)}, bf16[176,256]{1,0:T(8,128)(2,1)S(1)}) custom-call(f32[64,256]{1,0:T(8,128)S(1)} %copy-done, f32[64,256]{1,0:T(8,128)S(1)} %collective-permute-done.odd_side, f32[64,256]{1,0:T(8,128)S(1)} %collective-permute-done.1.b2, ...), custom_call_target="tpu_custom_call" | custom-call | tf_op jit(solution)/shard_map/pallas_call | solution.py:188
  27.0 0.1 collective-permute-start.3
  27.1 1.6 %collective-permute-start.4 = (bf16[176,256]{1,0:T(8,128)(2,1)S(1)}, bf16[176,256]{1,0:T(8,128)(2,1)S(1)}, u32[]{:S(2)}, u32[]{:S(2)}) collective-permute-start(bf16[176,256]{1,0:T(8,128)(2,1)S(1)} %get-tuple-element.11), channel_id=1, source_target_pairs={{0,2},{1,3},{2,0},{3,1},{4,6},{5,7},{6,4},{7,5},{8,10},{9,11},{10,... | collective-permute-start | bytes 270344 | tf_op jit(solution)/shard_map/ppermute | solution.py:24
  28.7 0.0 copy-start.1
  28.7 1.4 %collective-permute-start.5 = (bf16[176,256]{1,0:T(8,128)(2,1)S(1)}, bf16[176,256]{1,0:T(8,128)(2,1)S(1)}, u32[]{:S(2)}, u32[]{:S(2)}) collective-permute-start(bf16[176,256]{1,0:T(8,128)(2,1)S(1)} %get-tuple-element.12), channel_id=1, source_target_pairs={{0,3},{1,0},{2,1},{3,2},{4,7},{5,4},{6,5},{7,6},{8,11},{9,8},{10,9... | collective-permute-start | bytes 270344 | tf_op jit(solution)/shard_map/ppermute | solution.py:24
  30.1 1.3 %collective-permute-done.3.p1 = bf16[176,256]{1,0:T(8,128)(2,1)S(1)} collective-permute-done((bf16[176,256]{1,0:T(8,128)(2,1)S(1)}, bf16[176,256]{1,0:T(8,128)(2,1)S(1)}, u32[]{:S(2)}, u32[]{:S(2)}) %collective-permute-start.3) | collective-permute-done | bytes 90144 | tf_op jit(solution)/shard_map/ppermute | solution.py:24
  31.4 1.2 %collective-permute-done.4.p2 = bf16[176,256]{1,0:T(8,128)(2,1)S(1)} collective-permute-done((bf16[176,256]{1,0:T(8,128)(2,1)S(1)}, bf16[176,256]{1,0:T(8,128)(2,1)S(1)}, u32[]{:S(2)}, u32[]{:S(2)}) %collective-permute-start.4) | collective-permute-done | bytes 90144 | tf_op jit(solution)/shard_map/ppermute | solution.py:24
  32.6 0.3 collective-permute-done.5.p3
  33.0 0.0 copy-done.1
  33.0 0.7 %shard_map.29.a = f32[1,256]{1,0:T(1,128)S(1)} custom-call(s32[64]{0:T(128)S(1)} %copy-done.1, f32[176,256]{1,0:T(8,128)S(1)} %get-tuple-element.9.p0, bf16[176,256]{1,0:T(8,128)(2,1)S(1)} %collective-permute-done.3.p1, bf16[176,256]{1,0:T(8,128)(2,1)S(1)} %collective-permute-done.4.p2, bf16[176,256]{1,0:T(8,128)(2,1)S(1)} %collective-permute-done.5.p3), custom_call_target="tpu_custom_call" | custom-call | tf_op jit(solution)/shard_map/pallas_call | solution.py:200
  33.6 2.0 %collective-permute-start.8 = (f32[1,256]{1,0:T(1,128)S(1)}, f32[1,256]{1,0:T(1,128)S(1)}, u32[]{:S(2)}, u32[]{:S(2)}) collective-permute-start(f32[1,256]{1,0:T(1,128)S(1)} %shard_map.29.a), channel_id=1, source_target_pairs={{0,3},{1,0},{2,1},{3,2},{4,7},{5,4},{6,5},{7,6},{8,11},{9,8},{10,9... | collective-permute-start | bytes 3080 | tf_op jit(solution)/shard_map/ppermute | solution.py:24
  35.6 0.5 %collective-permute-start.7 = (f32[1,256]{1,0:T(1,128)S(1)}, f32[1,256]{1,0:T(1,128)S(1)}, u32[]{:S(2)}, u32[]{:S(2)}) collective-permute-start(f32[1,256]{1,0:T(1,128)S(1)} %shard_map.29.a), channel_id=1, source_target_pairs={{0,2},{1,3},{2,0},{3,1},{4,6},{5,7},{6,4},{7,5},{8,10},{9,11},{10,... | collective-permute-start | bytes 3080 | tf_op jit(solution)/shard_map/ppermute | solution.py:24
  36.1 0.0 collective-permute-start.6
  36.1 0.8 %collective-permute-done.8.d = f32[1,256]{1,0:T(1,128)S(1)} collective-permute-done((f32[1,256]{1,0:T(1,128)S(1)}, f32[1,256]{1,0:T(1,128)S(1)}, u32[]{:S(2)}, u32[]{:S(2)}) %collective-permute-start.8) | collective-permute-done | bytes 1056 | tf_op jit(solution)/shard_map/ppermute | solution.py:24
  36.9 2.3 %collective-permute-done.7.c = f32[1,256]{1,0:T(1,128)S(1)} collective-permute-done((f32[1,256]{1,0:T(1,128)S(1)}, f32[1,256]{1,0:T(1,128)S(1)}, u32[]{:S(2)}, u32[]{:S(2)}) %collective-permute-start.7) | collective-permute-done | bytes 1056 | tf_op jit(solution)/shard_map/ppermute | solution.py:24
  39.2 0.0 collective-permute-done.6.b
  39.2 1.1 %shard_map.30 = f32[1,256]{1,0:T(1,128)} custom-call(s32[64]{0:T(128)S(1)} %copy-done.1, f32[1,256]{1,0:T(1,128)S(1)} %shard_map.29.a, f32[1,256]{1,0:T(1,128)S(1)} %collective-permute-done.6.b, f32[1,256]{1,0:T(1,128)S(1)} %collective-permute-done.7.c, f32[1,256]{1,0:T(1,128)S(1)} %collective-permute-done.8.d), custom_call_target="tpu_custom_call" | custom-call | tf_op jit(solution)/shard_map/pallas_call | solution.py:208
Async XLA Ops:
  0.0 9.9 %collective-permute-start.1 = (f32[64,256]{1,0:T(8,128)}, f32[64,256]{1,0:T(8,128)S(1)}, u32[]{:S(2)}, u32[]{:S(2)}) collective-permute-start(f32[64,256]{1,0:T(8,128)} %own_far.1), channel_id=1, source_target_pairs={{0,8},{4,12},{8,16},{12,20},{16,24},{20,28},{24,32},{28,36},{32,40... | collective-permute-start | bytes 196616 | tf_op jit(solution)/shard_map/ppermute | solution.py:24
  3.9 10.9 %collective-permute-start = (f32[64,256]{1,0:T(8,128)}, f32[64,256]{1,0:T(8,128)S(1)}, u32[]{:S(2)}, u32[]{:S(2)}) collective-permute-start(f32[64,256]{1,0:T(8,128)} %own_far.1), channel_id=1, source_target_pairs={{0,0},{4,8},{8,4},{12,16},{16,12},{20,24},{24,20},{28,32},{32,28},... | collective-permute-start | bytes 196616 | tf_op jit(solution)/shard_map/ppermute | solution.py:24
  9.8 5.0 %collective-permute-start.2 = (f32[64,256]{1,0:T(8,128)}, f32[64,256]{1,0:T(8,128)S(1)}, u32[]{:S(2)}, u32[]{:S(2)}) collective-permute-start(f32[64,256]{1,0:T(8,128)} %own_far.1), channel_id=1, source_target_pairs={{0,4},{4,0},{8,12},{12,8},{16,20},{20,16},{24,28},{28,24},{32,36},... | collective-permute-start | bytes 196616 | tf_op jit(solution)/shard_map/ppermute | solution.py:24
  14.8 0.8 %copy-start = (f32[64,256]{1,0:T(8,128)S(1)}, f32[64,256]{1,0:T(8,128)}, u32[]{:S(2)}) copy-start(f32[64,256]{1,0:T(8,128)} %own_far.1) | copy-start | bytes 196612
  27.0 4.4 %collective-permute-start.3 = (bf16[176,256]{1,0:T(8,128)(2,1)S(1)}, bf16[176,256]{1,0:T(8,128)(2,1)S(1)}, u32[]{:S(2)}, u32[]{:S(2)}) collective-permute-start(bf16[176,256]{1,0:T(8,128)(2,1)S(1)} %get-tuple-element.10), channel_id=1, source_target_pairs={{0,1},{1,2},{2,3},{3,0},{4,5},{5,6},{6,7},{7,4},{8,9},{9,10},{10,1... | collective-permute-start | bytes 270344 | tf_op jit(solution)/shard_map/ppermute | solution.py:24
  27.1 5.5 %collective-permute-start.4 = (bf16[176,256]{1,0:T(8,128)(2,1)S(1)}, bf16[176,256]{1,0:T(8,128)(2,1)S(1)}, u32[]{:S(2)}, u32[]{:S(2)}) collective-permute-start(bf16[176,256]{1,0:T(8,128)(2,1)S(1)} %get-tuple-element.11), channel_id=1, source_target_pairs={{0,2},{1,3},{2,0},{3,1},{4,6},{5,7},{6,4},{7,5},{8,10},{9,11},{10,... | collective-permute-start | bytes 270344 | tf_op jit(solution)/shard_map/ppermute | solution.py:24
  28.7 4.3 %copy-start.1 = (s32[64]{0:T(128)S(1)}, s32[64]{0:T(128)}, u32[]{:S(2)}) copy-start(s32[64]{0:T(128)} %lens.3) | copy-start | bytes 772
  28.7 4.3 %collective-permute-start.5 = (bf16[176,256]{1,0:T(8,128)(2,1)S(1)}, bf16[176,256]{1,0:T(8,128)(2,1)S(1)}, u32[]{:S(2)}, u32[]{:S(2)}) collective-permute-start(bf16[176,256]{1,0:T(8,128)(2,1)S(1)} %get-tuple-element.12), channel_id=1, source_target_pairs={{0,3},{1,0},{2,1},{3,2},{4,7},{5,4},{6,5},{7,6},{8,11},{9,8},{10,9... | collective-permute-start | bytes 270344 | tf_op jit(solution)/shard_map/ppermute | solution.py:24
  33.6 3.3 %collective-permute-start.8 = (f32[1,256]{1,0:T(1,128)S(1)}, f32[1,256]{1,0:T(1,128)S(1)}, u32[]{:S(2)}, u32[]{:S(2)}) collective-permute-start(f32[1,256]{1,0:T(1,128)S(1)} %shard_map.29.a), channel_id=1, source_target_pairs={{0,3},{1,0},{2,1},{3,2},{4,7},{5,4},{6,5},{7,6},{8,11},{9,8},{10,9... | collective-permute-start | bytes 3080 | tf_op jit(solution)/shard_map/ppermute | solution.py:24
  35.6 3.6 %collective-permute-start.7 = (f32[1,256]{1,0:T(1,128)S(1)}, f32[1,256]{1,0:T(1,128)S(1)}, u32[]{:S(2)}, u32[]{:S(2)}) collective-permute-start(f32[1,256]{1,0:T(1,128)S(1)} %shard_map.29.a), channel_id=1, source_target_pairs={{0,2},{1,3},{2,0},{3,1},{4,6},{5,7},{6,4},{7,5},{8,10},{9,11},{10,... | collective-permute-start | bytes 3080 | tf_op jit(solution)/shard_map/ppermute | solution.py:24
  36.1 3.0 %collective-permute-start.6 = (f32[1,256]{1,0:T(1,128)S(1)}, f32[1,256]{1,0:T(1,128)S(1)}, u32[]{:S(2)}, u32[]{:S(2)}) collective-permute-start(f32[1,256]{1,0:T(1,128)S(1)} %shard_map.29.a), channel_id=1, source_target_pairs={{0,1},{1,2},{2,3},{3,0},{4,5},{5,6},{6,7},{7,4},{8,9},{9,10},{10,1... | collective-permute-start | bytes 3080 | tf_op jit(solution)/shard_map/ppermute | solution.py:24

commit v3 on v2

--- a/solution.py
+++ b/solution.py
@@ -15,6 +15,7 @@
 EXCL = WIN // 4
 KC = 16
 LANES = 128
+ALIGN = 8
 VMEM_LIMIT = 40 << 20
 SMALL_LIMIT = 8 << 20
 
@@ -38,8 +39,8 @@
     return i + 1 if i % 2 == 1 else i - 1
 
 
-def turned(distance):
-    return lambda i, count: (i + distance) % count
+def across(distance):
+    return lambda i, count: i ^ distance
 
 
 def window_sums(src_m, bufs, span):
@@ -70,7 +71,7 @@
 
 
 def corr_kernel(rows, cols, own_far, odd_side, b2, even_side, *refs):
-    outs, (own, arrived, x2, ma, mb, va, vb, za, zb, acc) = refs[:4], refs[4:]
+    outs, (own, arrived, x2, x8, ma, mb, va, vb, za, zb, acc) = refs[:4], refs[4:]
     fetch = pltpu.make_async_copy(own_far, own, arrived)
     fetch.start()
     total = (STEPS + 1) * rows
@@ -96,6 +97,10 @@
         end_m[at : at + LANES, :] = (m0 + m1) * 0.5
         end_v[at : at + LANES, :] = lax.rsqrt(var + EPS)
 
+    for s in range(ALIGN):
+        for at in range(0, span, LANES):
+            x8[s, at : at + LANES, :] = x2[at + s : at + s + LANES, :]
+
     group = 64
 
     def build(chunk, z):
@@ -104,7 +109,8 @@
             mean = end_m[at : at + group, :]
             scale = end_v[at : at + group, :]
             for k in range(KC):
-                x = x2[pl.ds(base + (at + k), group), :]
+                start = pl.multiple_of(base + (at + k // ALIGN * ALIGN), ALIGN)
+                x = x8[k % ALIGN, pl.ds(start, group), :]
                 z[at : at + group, k * LANES : (k + 1) * LANES] = ((x - mean) * scale).astype(jnp.bfloat16)
 
     def product(z):
@@ -129,7 +135,7 @@
     product(zb)
     part = lax.axis_index("chan")
     for d, out in enumerate(outs):
-        which = lax.rem(part + d, len(outs))
+        which = part ^ d
         size = out.shape[0]
         out[...] = acc[pl.ds(pl.multiple_of(which * size, 16), size), :].astype(out.dtype)
 
@@ -142,7 +148,7 @@
     seg = rows // 2
     start = (block - STEPS) * rows
     f32 = jnp.float32
-    score = (p0[...] + p1[...].astype(f32)) + (p2[...].astype(f32) + p3[...].astype(f32))
+    score = (p0[...] + p1[...]) + (p2[...].astype(f32) + p3[...].astype(f32))
     shape = (quarter, LANES)
     j = part * quarter + lax.broadcasted_iota(jnp.int32, shape, 0)
     stop = jnp.zeros(shape, jnp.int32)
@@ -156,19 +162,10 @@
     for at in range(0, rows, LANES):
         i = lane + (STEPS * rows + at)
         best = jnp.max(jnp.where(i >= reach, score[:, at : at + LANES], MASKED), axis=0, keepdims=True)
-        out[:, at : at + LANES] = best * (1.0 / WIN)
-
-
-def close_kernel(rows, lens, a, b, c, d, out):
-    block = lax.axis_index("tm")
-    last = rows * lax.axis_size("tm") - WIN
-    seg = rows // 2
-    best = jnp.maximum(jnp.maximum(a[...], b[...]), jnp.maximum(c[...], d[...]))
-    r = lax.broadcasted_iota(jnp.int32, best.shape, 1)
-    stop = jnp.where(r < seg, lens[block * 2], seg + lens[block * 2 + 1])
-    stop = jnp.minimum(stop, last + 1 - block * rows)
-    floor = 0.5 * MASKED * (1.0 / WIN)
-    out[...] = jnp.where((r < stop) & (best > floor), best, 0.0)
+        best = jnp.where(best > 0.5 * MASKED, best * (1.0 / WIN), MASKED)
+        r = i[:1, :] - STEPS * rows
+        own = jnp.where(r < seg, lens[block * 2], seg + lens[block * 2 + 1])
+        out[:, at : at + LANES] = jnp.where(r < jnp.minimum(own, last + 1 - block * rows), best, MASKED)
 
 
 def body(series, lengths):
@@ -187,16 +184,17 @@
     room = total + HALF + HALF
     pieces = pl.pallas_call(
         functools.partial(corr_kernel, rows, cols),
-        out_shape=[jax.ShapeDtypeStruct((quarter, rows), f32 if d == 0 else bf16) for d in range(parts)],
+        out_shape=[jax.ShapeDtypeStruct((quarter, rows), f32 if d < 2 else bf16) for d in range(parts)],
         in_specs=[pl.BlockSpec(memory_space=pltpu.HBM)] + [vmem] * 3,
         out_specs=[vmem] * parts,
-        scratch_shapes=[pltpu.VMEM((chans, rows), f32), pltpu.SemaphoreType.DMA]
-        + [pltpu.VMEM((room, LANES), f32)] * 5
+        scratch_shapes=[pltpu.VMEM((chans, rows), f32), pltpu.SemaphoreType.DMA, pltpu.VMEM((room, LANES), f32)]
+        + [pltpu.VMEM((ALIGN, room, LANES), f32)]
+        + [pltpu.VMEM((room, LANES), f32)] * 4
         + [pltpu.VMEM((total, KC * LANES), bf16)] * 2
         + [pltpu.VMEM((cols, rows), f32)],
         compiler_params=pltpu.CompilerParams(vmem_limit_bytes=VMEM_LIMIT),
     )(series, odd_side, b2, even_side)
-    got = [pieces[0]] + [sent(pieces[d], "chan", turned(d)) for d in range(1, parts)]
+    got = [pieces[0]] + [sent(pieces[d], "chan", across(d)) for d in range(1, parts)]
     best = pl.pallas_call(
         functools.partial(peak_kernel, rows),
         out_shape=jax.ShapeDtypeStruct((1, rows), f32),
@@ -204,15 +202,10 @@
         out_specs=vmem,
         compiler_params=pltpu.CompilerParams(vmem_limit_bytes=SMALL_LIMIT),
     )(lengths, *got)
-    all_best = [best] + [sent(best, "chan", turned(d)) for d in range(1, parts)]
-    peak = pl.pallas_call(
-        functools.partial(close_kernel, rows),
-        out_shape=jax.ShapeDtypeStruct((1, rows), f32),
-        in_specs=[smem] + [vmem] * parts,
-        out_specs=vmem,
-        compiler_params=pltpu.CompilerParams(vmem_limit_bytes=SMALL_LIMIT),
-    )(lengths, *all_best)
-    return peak.reshape(rows)
+    peers = [sent(best, "chan", across(d)) for d in range(1, parts)]
+    for peer in peers:
+        best = jnp.maximum(best, peer)
+    return jnp.where(best > 0.5 * MASKED, best, 0.0).reshape(rows)
 
 
 def solution(mesh):

time: 40.5 us -> 40.2 us (level)
  waiting for transfers between devices: 10.8 us -> 12.5 us
  starting transfers between devices: 15.4 us -> 13.8 us
  Pallas kernels: 13.2 us -> 12.2 us
  other arithmetic: 0 us -> 0.57 us
    ppermute x9, waiting for transfers between devices: 10.8 us -> 12.5 us  [sent(): lax.ppermute(block, axis, [(i, target(i, count)) for i in range(count)])]
    ppermute x9, starting transfers between devices: 15.4 us -> 13.8 us  [sent(): lax.ppermute(block, axis, [(i, target(i, count)) for i in range(count)])]
    pallas_call x1 -> x0, Pallas kernels: 1.12 us -> none  [body(): pl.pallas_call(functools.partial(close_kernel, rows), out_shape=jax.Shape...]
    select_n x0 -> x1, other arithmetic: none -> 0.57 us  [body(): return jnp.where(best > 0.5 * MASKED, best, 0.0).reshape(rows)]
  transfers between devices with their start and end apart: 9 -> 9, of which waited for: 6 -> 5; matrix products, arithmetic and copies ran while one was open for 0% -> 0% of each run, Pallas kernels for 0% -> 0%
where the time goes in v3:
time: 40.2 us; the launch traced here: 40 us
  starting transfers between devices  13.8 us (34%)
  waiting for transfers between devices  12.5 us (31%)
  Pallas kernels  12.2 us (30%)
  local copies, waits for them, and re-layouts  0.84 us (2%)
  other arithmetic  0.57 us (1%)
    ppermute x9, starting transfers between devices, sent(): lax.ppermute(block, axis, [(i, target(i, count)) for i in range(count)])  13.8 us
    ppermute x9, waiting for transfers between devices, sent(): lax.ppermute(block, axis, [(i, target(i, count)) for i in range(count)])  12.5 us
    pallas_call x1, Pallas kernels, body(): pl.pallas_call(functools.partial(corr_kernel, rows, cols), out_shape=[jax...  11.5 us
    unnamed x4, local copies, waits for them, and re-layouts  0.84 us
  transfers between devices with their start and end apart: 9, of which 5 were waited for; matrix products, arithmetic and copies ran while one was open for 0% of the time, Pallas kernels for 0%

profile of v3, /device:TPU:16, one launch (start us, length us, event | category | flops | bytes accessed | tf_op | source)
XLA Modules:
  0.0 40.0 jit_solution(4096105420602346565)
XLA Ops:
  0.0 3.9 %collective-permute-start.1 = (f32[64,256]{1,0:T(8,128)}, f32[64,256]{1,0:T(8,128)S(1)}, u32[]{:S(2)}, u32[]{:S(2)}) collective-permute-start(f32[64,256]{1,0:T(8,128)} %own_far.1), channel_id=1, source_target_pairs={{0,8},{4,12},{8,16},{12,20},{16,24},{20,28},{24,32},{28,36},{32,40... | collective-permute-start | bytes 196616 | tf_op jit(solution)/shard_map/ppermute | solution.py:25
  3.9 5.9 %collective-permute-start = (f32[64,256]{1,0:T(8,128)}, f32[64,256]{1,0:T(8,128)S(1)}, u32[]{:S(2)}, u32[]{:S(2)}) collective-permute-start(f32[64,256]{1,0:T(8,128)} %own_far.1), channel_id=1, source_target_pairs={{0,0},{4,8},{8,4},{12,16},{16,12},{20,24},{24,20},{28,32},{32,28},... | collective-permute-start | bytes 196616 | tf_op jit(solution)/shard_map/ppermute | solution.py:25
  9.8 0.1 collective-permute-start.2
  9.9 0.0 collective-permute-done.1.b2
  9.9 4.8 %collective-permute-done.odd_side = f32[64,256]{1,0:T(8,128)S(1)} collective-permute-done((f32[64,256]{1,0:T(8,128)}, f32[64,256]{1,0:T(8,128)S(1)}, u32[]{:S(2)}, u32[]{:S(2)}) %collective-permute-start) | collective-permute-done | bytes 65568 | tf_op jit(solution)/shard_map/ppermute | solution.py:25
  14.7 0.0 collective-permute-done.2.even_side
  14.8 0.0 copy-start
  14.8 0.8 %copy-done = f32[64,256]{1,0:T(8,128)S(1)} copy-done((f32[64,256]{1,0:T(8,128)S(1)}, f32[64,256]{1,0:T(8,128)}, u32[]{:S(2)}) %copy-start) | copy-done | bytes 65560
  15.6 11.5 %shard_map.28 = (f32[176,256]{1,0:T(8,128)S(1)}, f32[176,256]{1,0:T(8,128)S(1)}, bf16[176,256]{1,0:T(8,128)(2,1)S(1)}, bf16[176,256]{1,0:T(8,128)(2,1)S(1)}) custom-call(f32[64,256]{1,0:T(8,128)S(1)} %copy-done, f32[64,256]{1,0:T(8,128)S(1)} %collective-permute-done.odd_side, f32[64,256]{1,0:T(8,128)S(1)} %collective-permute-done.1.b2, ...), custom_call_target="tpu_custom_call" | custom-call | tf_op jit(solution)/shard_map/pallas_call | solution.py:185
  27.1 0.1 collective-permute-start.3
  27.2 1.6 %collective-permute-start.4 = (bf16[176,256]{1,0:T(8,128)(2,1)S(1)}, bf16[176,256]{1,0:T(8,128)(2,1)S(1)}, u32[]{:S(2)}, u32[]{:S(2)}) collective-permute-start(bf16[176,256]{1,0:T(8,128)(2,1)S(1)} %get-tuple-element.11), channel_id=1, source_target_pairs={{0,2},{1,3},{2,0},{3,1},{4,6},{5,7},{6,4},{7,5},{8,10},{9,11},{10,... | collective-permute-start | bytes 270344 | tf_op jit(solution)/shard_map/ppermute | solution.py:25
  28.7 0.0 copy-start.1
  28.8 0.3 collective-permute-start.5
  29.0 3.7 %collective-permute-done.4.p2 = bf16[176,256]{1,0:T(8,128)(2,1)S(1)} collective-permute-done((bf16[176,256]{1,0:T(8,128)(2,1)S(1)}, bf16[176,256]{1,0:T(8,128)(2,1)S(1)}, u32[]{:S(2)}, u32[]{:S(2)}) %collective-permute-start.4) | collective-permute-done | bytes 90144 | tf_op jit(solution)/shard_map/ppermute | solution.py:25
  32.7 0.9 %collective-permute-done.5.p3 = bf16[176,256]{1,0:T(8,128)(2,1)S(1)} collective-permute-done((bf16[176,256]{1,0:T(8,128)(2,1)S(1)}, bf16[176,256]{1,0:T(8,128)(2,1)S(1)}, u32[]{:S(2)}, u32[]{:S(2)}) %collective-permute-start.5) | collective-permute-done | bytes 90144 | tf_op jit(solution)/shard_map/ppermute | solution.py:25
  33.7 0.0 collective-permute-done.3.p1
  33.7 0.0 copy-done.1
  33.7 0.7 %shard_map.29 = f32[1,256]{1,0:T(1,128)S(1)} custom-call(s32[64]{0:T(128)S(1)} %copy-done.1, f32[176,256]{1,0:T(8,128)S(1)} %get-tuple-element.9.p0, f32[176,256]{1,0:T(8,128)S(1)} %collective-permute-done.3.p1, bf16[176,256]{1,0:T(8,128)(2,1)S(1)} %collective-permute-done.4.p2, bf16[176,256]{1,0:T(8,128)(2,1)S(1)} %collective-permute-done.5.p3), custom_call_target="tpu_custom_call" | custom-call | tf_op jit(solution)/shard_map/pallas_call | solution.py:198
  34.3 1.5 %collective-permute-start.8 = (f32[1,256]{1,0:T(1,128)S(1)}, f32[1,256]{1,0:T(1,128)S(1)}, u32[]{:S(2)}, u32[]{:S(2)}) collective-permute-start(f32[1,256]{1,0:T(1,128)S(1)} %shard_map.29), channel_id=1, source_target_pairs={{0,3},{1,2},{2,1},{3,0},{4,7},{5,6},{6,5},{7,4},{8,11},{9,10},{10,... | collective-permute-start | bytes 3080 | tf_op jit(solution)/shard_map/ppermute | solution.py:25
  35.8 0.5 %collective-permute-start.7 = (f32[1,256]{1,0:T(1,128)S(1)}, f32[1,256]{1,0:T(1,128)S(1)}, u32[]{:S(2)}, u32[]{:S(2)}) collective-permute-start(f32[1,256]{1,0:T(1,128)S(1)} %shard_map.29), channel_id=1, source_target_pairs={{0,2},{1,3},{2,0},{3,1},{4,6},{5,7},{6,4},{7,5},{8,10},{9,11},{10,... | collective-permute-start | bytes 3080 | tf_op jit(solution)/shard_map/ppermute | solution.py:25
  36.4 0.0 collective-permute-start.6
  36.4 1.0 %collective-permute-done.8 = f32[1,256]{1,0:T(1,128)S(1)} collective-permute-done((f32[1,256]{1,0:T(1,128)S(1)}, f32[1,256]{1,0:T(1,128)S(1)}, u32[]{:S(2)}, u32[]{:S(2)}) %collective-permute-start.8) | collective-permute-done | bytes 1056 | tf_op jit(solution)/shard_map/ppermute | solution.py:25
  37.4 2.0 %collective-permute-done.7 = f32[1,256]{1,0:T(1,128)S(1)} collective-permute-done((f32[1,256]{1,0:T(1,128)S(1)}, f32[1,256]{1,0:T(1,128)S(1)}, u32[]{:S(2)}, u32[]{:S(2)}) %collective-permute-start.7) | collective-permute-done | bytes 1056 | tf_op jit(solution)/shard_map/ppermute | solution.py:25
  39.4 0.0 collective-permute-done.6
  39.4 0.6 %compare_select_fusion = f32[1,256]{1,0:T(1,128)} fusion(f32[1,256]{1,0:T(1,128)S(1)} %collective-permute-done.8, f32[1,256]{1,0:T(1,128)S(1)} %collective-permute-done.7, f32[1,256]{1,0:T(1,128)S(1)} %shard_map.29, f32[1,256]{1,0:T(1,128)S(1)} %collective-permute-done.6), kind=kLoop, calls=%fused_computation | loop fusion | flops 1280 | bytes 5120 | tf_op jit(solution)/shard_map/jit(_where)/select_n | solution.py:208
Async XLA Ops:
  0.0 9.9 %collective-permute-start.1 = (f32[64,256]{1,0:T(8,128)}, f32[64,256]{1,0:T(8,128)S(1)}, u32[]{:S(2)}, u32[]{:S(2)}) collective-permute-start(f32[64,256]{1,0:T(8,128)} %own_far.1), channel_id=1, source_target_pairs={{0,8},{4,12},{8,16},{12,20},{16,24},{20,28},{24,32},{28,36},{32,40... | collective-permute-start | bytes 196616 | tf_op jit(solution)/shard_map/ppermute | solution.py:25
  3.9 10.9 %collective-permute-start = (f32[64,256]{1,0:T(8,128)}, f32[64,256]{1,0:T(8,128)S(1)}, u32[]{:S(2)}, u32[]{:S(2)}) collective-permute-start(f32[64,256]{1,0:T(8,128)} %own_far.1), channel_id=1, source_target_pairs={{0,0},{4,8},{8,4},{12,16},{16,12},{20,24},{24,20},{28,32},{32,28},... | collective-permute-start | bytes 196616 | tf_op jit(solution)/shard_map/ppermute | solution.py:25
  9.8 5.0 %collective-permute-start.2 = (f32[64,256]{1,0:T(8,128)}, f32[64,256]{1,0:T(8,128)S(1)}, u32[]{:S(2)}, u32[]{:S(2)}) collective-permute-start(f32[64,256]{1,0:T(8,128)} %own_far.1), channel_id=1, source_target_pairs={{0,4},{4,0},{8,12},{12,8},{16,20},{20,16},{24,28},{28,24},{32,36},... | collective-permute-start | bytes 196616 | tf_op jit(solution)/shard_map/ppermute | solution.py:25
  14.8 0.8 %copy-start = (f32[64,256]{1,0:T(8,128)S(1)}, f32[64,256]{1,0:T(8,128)}, u32[]{:S(2)}) copy-start(f32[64,256]{1,0:T(8,128)} %own_far.1) | copy-start | bytes 196612
  27.1 6.6 %collective-permute-start.3 = (f32[176,256]{1,0:T(8,128)S(1)}, f32[176,256]{1,0:T(8,128)S(1)}, u32[]{:S(2)}, u32[]{:S(2)}) collective-permute-start(f32[176,256]{1,0:T(8,128)S(1)} %get-tuple-element.10), channel_id=1, source_target_pairs={{0,1},{1,0},{2,3},{3,2},{4,5},{5,4},{6,7},{7,6},{8,9},{9,8},{10,11... | collective-permute-start | bytes 540680 | tf_op jit(solution)/shard_map/ppermute | solution.py:25
  27.2 5.5 %collective-permute-start.4 = (bf16[176,256]{1,0:T(8,128)(2,1)S(1)}, bf16[176,256]{1,0:T(8,128)(2,1)S(1)}, u32[]{:S(2)}, u32[]{:S(2)}) collective-permute-start(bf16[176,256]{1,0:T(8,128)(2,1)S(1)} %get-tuple-element.11), channel_id=1, source_target_pairs={{0,2},{1,3},{2,0},{3,1},{4,6},{5,7},{6,4},{7,5},{8,10},{9,11},{10,... | collective-permute-start | bytes 270344 | tf_op jit(solution)/shard_map/ppermute | solution.py:25
  28.7 4.9 %copy-start.1 = (s32[64]{0:T(128)S(1)}, s32[64]{0:T(128)}, u32[]{:S(2)}) copy-start(s32[64]{0:T(128)} %lens.1) | copy-start | bytes 772
  28.8 4.9 %collective-permute-start.5 = (bf16[176,256]{1,0:T(8,128)(2,1)S(1)}, bf16[176,256]{1,0:T(8,128)(2,1)S(1)}, u32[]{:S(2)}, u32[]{:S(2)}) collective-permute-start(bf16[176,256]{1,0:T(8,128)(2,1)S(1)} %get-tuple-element.12), channel_id=1, source_target_pairs={{0,3},{1,2},{2,1},{3,0},{4,7},{5,6},{6,5},{7,4},{8,11},{9,10},{10,... | collective-permute-start | bytes 270344 | tf_op jit(solution)/shard_map/ppermute | solution.py:25
  34.3 3.1 %collective-permute-start.8 = (f32[1,256]{1,0:T(1,128)S(1)}, f32[1,256]{1,0:T(1,128)S(1)}, u32[]{:S(2)}, u32[]{:S(2)}) collective-permute-start(f32[1,256]{1,0:T(1,128)S(1)} %shard_map.29), channel_id=1, source_target_pairs={{0,3},{1,2},{2,1},{3,0},{4,7},{5,6},{6,5},{7,4},{8,11},{9,10},{10,... | collective-permute-start | bytes 3080 | tf_op jit(solution)/shard_map/ppermute | solution.py:25
  35.8 3.6 %collective-permute-start.7 = (f32[1,256]{1,0:T(1,128)S(1)}, f32[1,256]{1,0:T(1,128)S(1)}, u32[]{:S(2)}, u32[]{:S(2)}) collective-permute-start(f32[1,256]{1,0:T(1,128)S(1)} %shard_map.29), channel_id=1, source_target_pairs={{0,2},{1,3},{2,0},{3,1},{4,6},{5,7},{6,4},{7,5},{8,10},{9,11},{10,... | collective-permute-start | bytes 3080 | tf_op jit(solution)/shard_map/ppermute | solution.py:25
  36.4 3.0 %collective-permute-start.6 = (f32[1,256]{1,0:T(1,128)S(1)}, f32[1,256]{1,0:T(1,128)S(1)}, u32[]{:S(2)}, u32[]{:S(2)}) collective-permute-start(f32[1,256]{1,0:T(1,128)S(1)} %shard_map.29), channel_id=1, source_target_pairs={{0,1},{1,0},{2,3},{3,2},{4,5},{5,4},{6,7},{7,6},{8,9},{9,8},{10,11... | collective-permute-start | bytes 3080 | tf_op jit(solution)/shard_map/ppermute | solution.py:25

commit v4 on v3

--- a/solution.py
+++ b/solution.py
@@ -13,7 +13,8 @@
 EPS = 1e-05
 MASKED = -1000000000.0
 EXCL = WIN // 4
-KC = 16
+STEP_K = 4
+GROUP = 64
 LANES = 128
 ALIGN = 8
 VMEM_LIMIT = 40 << 20
@@ -71,7 +72,7 @@
 
 
 def corr_kernel(rows, cols, own_far, odd_side, b2, even_side, *refs):
-    outs, (own, arrived, x2, x8, ma, mb, va, vb, za, zb, acc) = refs[:4], refs[4:]
+    outs, (own, arrived, x2, x8, ma, mb, va, vb, zr, acc) = refs[:4], refs[4:]
     fetch = pltpu.make_async_copy(own_far, own, arrived)
     fetch.start()
     total = (STEPS + 1) * rows
@@ -101,38 +102,57 @@
         for at in range(0, span, LANES):
             x8[s, at : at + LANES, :] = x2[at + s : at + s + LANES, :]
 
-    group = 64
-
-    def build(chunk, z):
-        base = pl.multiple_of(chunk * KC, KC)
-        for at in range(0, total, group):
-            mean = end_m[at : at + group, :]
-            scale = end_v[at : at + group, :]
-            for k in range(KC):
-                start = pl.multiple_of(base + (at + k // ALIGN * ALIGN), ALIGN)
-                x = x8[k % ALIGN, pl.ds(start, group), :]
-                z[at : at + group, k * LANES : (k + 1) * LANES] = ((x - mean) * scale).astype(jnp.bfloat16)
-
-    def product(z):
-        acc[...] += lax.dot_general(
-            z[:cols, :], z[total - rows :, :], (((1,), (1,)), ((), ())), preferred_element_type=jnp.float32
-        )
-
-    acc[...] = jnp.zeros_like(acc)
-    chunks = HALF // KC
-    build(0, za)
-
-    def pair(p, carry):
-        build(2 * p + 1, zb)
-        product(za)
-        build(2 * p + 2, za)
-        product(zb)
-        return carry
-
-    lax.fori_loop(0, chunks // 2 - 1, pair, 0)
-    build(chunks - 1, zb)
-    product(za)
-    product(zb)
+    def windows(at, size, step):
+        mean = end_m[at : at + size, :]
+        scale = end_v[at : at + size, :]
+        lag = lax.rem(step, 2) * STEP_K
+        start = pl.multiple_of(step // 2 * ALIGN + at, ALIGN)
+        z = []
+        for k in range(STEP_K):
+            x = x8[lag + k, pl.ds(start, size), :]
+            z.append(((x - mean) * scale).astype(jnp.bfloat16))
+        return jnp.concatenate(z[:2], axis=1), jnp.concatenate(z[2:], axis=1)
+
+    first_row = total - rows
+
+    def stage(step):
+        slot = lax.rem(step, 2)
+        for at in range(0, rows, GROUP):
+            for unit, z in enumerate(windows(first_row + at, GROUP, step)):
+                zr[slot, unit, at : at + GROUP, :] = z
+        for unit in range(2):
+            pltpu.matmul_push_rhs(zr[slot, unit], 0, unit, transpose=True)
+
+    def stream(sums, step, following):
+        slot = lax.rem(step, 2)
+        for g, at in enumerate(range(0, cols, GROUP)):
+            if at < first_row:
+                pair = windows(at, GROUP, step)
+            else:
+                pair = [zr[slot, unit, at - first_row : at - first_row + GROUP, :] for unit in range(2)]
+            for unit in range(2):
+                pltpu.matmul_acc_lhs(sums[unit][g], pair[unit], 0 if g == 0 else None)
+            if g == 0 and following:
+                stage(step + 1)
+
+    def contract(*sums):
+        sums = sums[: len(sums) // 2], sums[len(sums) // 2 :]
+        for g in range(cols // GROUP):
+            for unit in range(2):
+                pltpu.matmul_pop(sums[unit][g])
+        steps = HALF // STEP_K
+        stage(0)
+
+        def advance(step, carry):
+            stream(sums, step, True)
+            return carry
+
+        lax.fori_loop(0, steps - 1, advance, 0)
+        stream(sums, steps - 1, False)
+        for g, at in enumerate(range(0, cols, GROUP)):
+            acc[at : at + GROUP, :] = pltpu.matmul_pop(sums[0][g]) + pltpu.matmul_pop(sums[1][g])
+
+    pl.run_scoped(contract, *[pltpu.ACC(unit)((GROUP, rows), jnp.float32) for unit in range(2) for _ in range(cols // GROUP)])
     part = lax.axis_index("chan")
     for d, out in enumerate(outs):
         which = part ^ d
@@ -190,8 +210,7 @@
         scratch_shapes=[pltpu.VMEM((chans, rows), f32), pltpu.SemaphoreType.DMA, pltpu.VMEM((room, LANES), f32)]
         + [pltpu.VMEM((ALIGN, room, LANES), f32)]
         + [pltpu.VMEM((room, LANES), f32)] * 4
-        + [pltpu.VMEM((total, KC * LANES), bf16)] * 2
-        + [pltpu.VMEM((cols, rows), f32)],
+        + [pltpu.VMEM((2, 2, rows, 2 * LANES), bf16), pltpu.VMEM((cols, rows), f32)],
         compiler_params=pltpu.CompilerParams(vmem_limit_bytes=VMEM_LIMIT),
     )(series, odd_side, b2, even_side)
     got = [pieces[0]] + [sent(pieces[d], "chan", across(d)) for d in range(1, parts)]

time: 40.2 us -> 38 us (0.945)
  the two profiles are of different devices: /device:TPU:16 before, /device:TPU:8 now
where the time goes in v4:
time: 38 us; the launch traced here: 37.8 us
  starting transfers between devices  13.8 us (36%)
  waiting for transfers between devices  12.5 us (33%)
  Pallas kernels  10 us (26%)
  local copies, waits for them, and re-layouts  0.84 us (2%)
  other arithmetic  0.57 us (1%)
    ppermute x9, starting transfers between devices, sent(): lax.ppermute(block, axis, [(i, target(i, count)) for i in range(count)])  13.8 us
    ppermute x9, waiting for transfers between devices, sent(): lax.ppermute(block, axis, [(i, target(i, count)) for i in range(count)])  12.5 us
    pallas_call x1, Pallas kernels, body(): pl.pallas_call(functools.partial(corr_kernel, rows, cols), out_shape=[jax...  9.35 us
    unnamed x4, local copies, waits for them, and re-layouts  0.84 us
  transfers between devices with their start and end apart: 9, of which 5 were waited for; matrix products, arithmetic and copies ran while one was open for 0% of the time, Pallas kernels for 0%

profile of v4, /device:TPU:8, one launch (start us, length us, event | category | flops | bytes accessed | tf_op | source)
XLA Modules:
  0.0 37.8 jit_solution(12247495860088770438)
XLA Ops:
  0.0 3.9 %collective-permute-start.1 = (f32[64,256]{1,0:T(8,128)}, f32[64,256]{1,0:T(8,128)S(1)}, u32[]{:S(2)}, u32[]{:S(2)}) collective-permute-start(f32[64,256]{1,0:T(8,128)} %own_far.1), channel_id=1, source_target_pairs={{0,8},{4,12},{8,16},{12,20},{16,24},{20,28},{24,32},{28,36},{32,40... | collective-permute-start | bytes 196616 | tf_op jit(solution)/shard_map/ppermute | solution.py:26
  3.9 5.9 %collective-permute-start = (f32[64,256]{1,0:T(8,128)}, f32[64,256]{1,0:T(8,128)S(1)}, u32[]{:S(2)}, u32[]{:S(2)}) collective-permute-start(f32[64,256]{1,0:T(8,128)} %own_far.1), channel_id=1, source_target_pairs={{0,0},{4,8},{8,4},{12,16},{16,12},{20,24},{24,20},{28,32},{32,28},... | collective-permute-start | bytes 196616 | tf_op jit(solution)/shard_map/ppermute | solution.py:26
  9.8 0.1 collective-permute-start.2
  9.9 0.0 collective-permute-done.1.b2
  9.9 4.8 %collective-permute-done.odd_side = f32[64,256]{1,0:T(8,128)S(1)} collective-permute-done((f32[64,256]{1,0:T(8,128)}, f32[64,256]{1,0:T(8,128)S(1)}, u32[]{:S(2)}, u32[]{:S(2)}) %collective-permute-start) | collective-permute-done | bytes 65568 | tf_op jit(solution)/shard_map/ppermute | solution.py:26
  14.7 0.0 collective-permute-done.2.even_side
  14.8 0.0 copy-start
  14.8 0.8 %copy-done = f32[64,256]{1,0:T(8,128)S(1)} copy-done((f32[64,256]{1,0:T(8,128)S(1)}, f32[64,256]{1,0:T(8,128)}, u32[]{:S(2)}) %copy-start) | copy-done | bytes 65560
  15.6 9.4 %shard_map.28 = (f32[176,256]{1,0:T(8,128)S(1)}, f32[176,256]{1,0:T(8,128)S(1)}, bf16[176,256]{1,0:T(8,128)(2,1)S(1)}, bf16[176,256]{1,0:T(8,128)(2,1)S(1)}) custom-call(f32[64,256]{1,0:T(8,128)S(1)} %copy-done, f32[64,256]{1,0:T(8,128)S(1)} %collective-permute-done.odd_side, f32[64,256]{1,0:T(8,128)S(1)} %collective-permute-done.1.b2, ...), custom_call_target="tpu_custom_call" | custom-call | tf_op jit(solution)/shard_map/pallas_call | solution.py:205
  25.0 0.1 collective-permute-start.3
  25.0 1.6 %collective-permute-start.4 = (bf16[176,256]{1,0:T(8,128)(2,1)S(1)}, bf16[176,256]{1,0:T(8,128)(2,1)S(1)}, u32[]{:S(2)}, u32[]{:S(2)}) collective-permute-start(bf16[176,256]{1,0:T(8,128)(2,1)S(1)} %get-tuple-element.11), channel_id=1, source_target_pairs={{0,2},{1,3},{2,0},{3,1},{4,6},{5,7},{6,4},{7,5},{8,10},{9,11},{10,... | collective-permute-start | bytes 270344 | tf_op jit(solution)/shard_map/ppermute | solution.py:26
  26.6 0.0 copy-start.1
  26.6 0.3 collective-permute-start.5
  26.9 3.7 %collective-permute-done.4.p2 = bf16[176,256]{1,0:T(8,128)(2,1)S(1)} collective-permute-done((bf16[176,256]{1,0:T(8,128)(2,1)S(1)}, bf16[176,256]{1,0:T(8,128)(2,1)S(1)}, u32[]{:S(2)}, u32[]{:S(2)}) %collective-permute-start.4) | collective-permute-done | bytes 90144 | tf_op jit(solution)/shard_map/ppermute | solution.py:26
  30.6 1.0 %collective-permute-done.5.p3 = bf16[176,256]{1,0:T(8,128)(2,1)S(1)} collective-permute-done((bf16[176,256]{1,0:T(8,128)(2,1)S(1)}, bf16[176,256]{1,0:T(8,128)(2,1)S(1)}, u32[]{:S(2)}, u32[]{:S(2)}) %collective-permute-start.5) | collective-permute-done | bytes 90144 | tf_op jit(solution)/shard_map/ppermute | solution.py:26
  31.5 0.0 collective-permute-done.3.p1
  31.5 0.0 copy-done.1
  31.5 0.7 %shard_map.29 = f32[1,256]{1,0:T(1,128)S(1)} custom-call(s32[64]{0:T(128)S(1)} %copy-done.1, f32[176,256]{1,0:T(8,128)S(1)} %get-tuple-element.9.p0, f32[176,256]{1,0:T(8,128)S(1)} %collective-permute-done.3.p1, bf16[176,256]{1,0:T(8,128)(2,1)S(1)} %collective-permute-done.4.p2, bf16[176,256]{1,0:T(8,128)(2,1)S(1)} %collective-permute-done.5.p3), custom_call_target="tpu_custom_call" | custom-call | tf_op jit(solution)/shard_map/pallas_call | solution.py:217
  32.2 1.5 %collective-permute-start.8 = (f32[1,256]{1,0:T(1,128)S(1)}, f32[1,256]{1,0:T(1,128)S(1)}, u32[]{:S(2)}, u32[]{:S(2)}) collective-permute-start(f32[1,256]{1,0:T(1,128)S(1)} %shard_map.29), channel_id=1, source_target_pairs={{0,3},{1,2},{2,1},{3,0},{4,7},{5,6},{6,5},{7,4},{8,11},{9,10},{10,... | collective-permute-start | bytes 3080 | tf_op jit(solution)/shard_map/ppermute | solution.py:26
  33.7 0.5 %collective-permute-start.7 = (f32[1,256]{1,0:T(1,128)S(1)}, f32[1,256]{1,0:T(1,128)S(1)}, u32[]{:S(2)}, u32[]{:S(2)}) collective-permute-start(f32[1,256]{1,0:T(1,128)S(1)} %shard_map.29), channel_id=1, source_target_pairs={{0,2},{1,3},{2,0},{3,1},{4,6},{5,7},{6,4},{7,5},{8,10},{9,11},{10,... | collective-permute-start | bytes 3080 | tf_op jit(solution)/shard_map/ppermute | solution.py:26
  34.2 0.0 collective-permute-start.6
  34.2 1.1 %collective-permute-done.8 = f32[1,256]{1,0:T(1,128)S(1)} collective-permute-done((f32[1,256]{1,0:T(1,128)S(1)}, f32[1,256]{1,0:T(1,128)S(1)}, u32[]{:S(2)}, u32[]{:S(2)}) %collective-permute-start.8) | collective-permute-done | bytes 1056 | tf_op jit(solution)/shard_map/ppermute | solution.py:26
  35.3 2.0 %collective-permute-done.7 = f32[1,256]{1,0:T(1,128)S(1)} collective-permute-done((f32[1,256]{1,0:T(1,128)S(1)}, f32[1,256]{1,0:T(1,128)S(1)}, u32[]{:S(2)}, u32[]{:S(2)}) %collective-permute-start.7) | collective-permute-done | bytes 1056 | tf_op jit(solution)/shard_map/ppermute | solution.py:26
  37.3 0.0 collective-permute-done.6
  37.3 0.6 %compare_select_fusion = f32[1,256]{1,0:T(1,128)} fusion(f32[1,256]{1,0:T(1,128)S(1)} %collective-permute-done.8, f32[1,256]{1,0:T(1,128)S(1)} %collective-permute-done.7, f32[1,256]{1,0:T(1,128)S(1)} %shard_map.29, f32[1,256]{1,0:T(1,128)S(1)} %collective-permute-done.6), kind=kLoop, calls=%fused_computation | loop fusion | flops 1280 | bytes 5120 | tf_op jit(solution)/shard_map/jit(_where)/select_n | solution.py:227
Async XLA Ops:
  0.0 9.9 %collective-permute-start.1 = (f32[64,256]{1,0:T(8,128)}, f32[64,256]{1,0:T(8,128)S(1)}, u32[]{:S(2)}, u32[]{:S(2)}) collective-permute-start(f32[64,256]{1,0:T(8,128)} %own_far.1), channel_id=1, source_target_pairs={{0,8},{4,12},{8,16},{12,20},{16,24},{20,28},{24,32},{28,36},{32,40... | collective-permute-start | bytes 196616 | tf_op jit(solution)/shard_map/ppermute | solution.py:26
  3.9 10.9 %collective-permute-start = (f32[64,256]{1,0:T(8,128)}, f32[64,256]{1,0:T(8,128)S(1)}, u32[]{:S(2)}, u32[]{:S(2)}) collective-permute-start(f32[64,256]{1,0:T(8,128)} %own_far.1), channel_id=1, source_target_pairs={{0,0},{4,8},{8,4},{12,16},{16,12},{20,24},{24,20},{28,32},{32,28},... | collective-permute-start | bytes 196616 | tf_op jit(solution)/shard_map/ppermute | solution.py:26
  9.8 5.0 %collective-permute-start.2 = (f32[64,256]{1,0:T(8,128)}, f32[64,256]{1,0:T(8,128)S(1)}, u32[]{:S(2)}, u32[]{:S(2)}) collective-permute-start(f32[64,256]{1,0:T(8,128)} %own_far.1), channel_id=1, source_target_pairs={{0,4},{4,0},{8,12},{12,8},{16,20},{20,16},{24,28},{28,24},{32,36},... | collective-permute-start | bytes 196616 | tf_op jit(solution)/shard_map/ppermute | solution.py:26
  14.8 0.8 %copy-start = (f32[64,256]{1,0:T(8,128)S(1)}, f32[64,256]{1,0:T(8,128)}, u32[]{:S(2)}) copy-start(f32[64,256]{1,0:T(8,128)} %own_far.1) | copy-start | bytes 196612
  25.0 6.6 %collective-permute-start.3 = (f32[176,256]{1,0:T(8,128)S(1)}, f32[176,256]{1,0:T(8,128)S(1)}, u32[]{:S(2)}, u32[]{:S(2)}) collective-permute-start(f32[176,256]{1,0:T(8,128)S(1)} %get-tuple-element.10), channel_id=1, source_target_pairs={{0,1},{1,0},{2,3},{3,2},{4,5},{5,4},{6,7},{7,6},{8,9},{9,8},{10,11... | collective-permute-start | bytes 540680 | tf_op jit(solution)/shard_map/ppermute | solution.py:26
  25.0 5.5 %collective-permute-start.4 = (bf16[176,256]{1,0:T(8,128)(2,1)S(1)}, bf16[176,256]{1,0:T(8,128)(2,1)S(1)}, u32[]{:S(2)}, u32[]{:S(2)}) collective-permute-start(bf16[176,256]{1,0:T(8,128)(2,1)S(1)} %get-tuple-element.11), channel_id=1, source_target_pairs={{0,2},{1,3},{2,0},{3,1},{4,6},{5,7},{6,4},{7,5},{8,10},{9,11},{10,... | collective-permute-start | bytes 270344 | tf_op jit(solution)/shard_map/ppermute | solution.py:26
  26.6 4.9 %copy-start.1 = (s32[64]{0:T(128)S(1)}, s32[64]{0:T(128)}, u32[]{:S(2)}) copy-start(s32[64]{0:T(128)} %lens.1) | copy-start | bytes 772
  26.6 4.9 %collective-permute-start.5 = (bf16[176,256]{1,0:T(8,128)(2,1)S(1)}, bf16[176,256]{1,0:T(8,128)(2,1)S(1)}, u32[]{:S(2)}, u32[]{:S(2)}) collective-permute-start(bf16[176,256]{1,0:T(8,128)(2,1)S(1)} %get-tuple-element.12), channel_id=1, source_target_pairs={{0,3},{1,2},{2,1},{3,0},{4,7},{5,6},{6,5},{7,4},{8,11},{9,10},{10,... | collective-permute-start | bytes 270344 | tf_op jit(solution)/shard_map/ppermute | solution.py:26
  32.2 3.1 %collective-permute-start.8 = (f32[1,256]{1,0:T(1,128)S(1)}, f32[1,256]{1,0:T(1,128)S(1)}, u32[]{:S(2)}, u32[]{:S(2)}) collective-permute-start(f32[1,256]{1,0:T(1,128)S(1)} %shard_map.29), channel_id=1, source_target_pairs={{0,3},{1,2},{2,1},{3,0},{4,7},{5,6},{6,5},{7,4},{8,11},{9,10},{10,... | collective-permute-start | bytes 3080 | tf_op jit(solution)/shard_map/ppermute | solution.py:26
  33.7 3.6 %collective-permute-start.7 = (f32[1,256]{1,0:T(1,128)S(1)}, f32[1,256]{1,0:T(1,128)S(1)}, u32[]{:S(2)}, u32[]{:S(2)}) collective-permute-start(f32[1,256]{1,0:T(1,128)S(1)} %shard_map.29), channel_id=1, source_target_pairs={{0,2},{1,3},{2,0},{3,1},{4,6},{5,7},{6,4},{7,5},{8,10},{9,11},{10,... | collective-permute-start | bytes 3080 | tf_op jit(solution)/shard_map/ppermute | solution.py:26
  34.2 3.0 %collective-permute-start.6 = (f32[1,256]{1,0:T(1,128)S(1)}, f32[1,256]{1,0:T(1,128)S(1)}, u32[]{:S(2)}, u32[]{:S(2)}) collective-permute-start(f32[1,256]{1,0:T(1,128)S(1)} %shard_map.29), channel_id=1, source_target_pairs={{0,1},{1,0},{2,3},{3,2},{4,5},{5,4},{6,7},{7,6},{8,9},{9,8},{10,11... | collective-permute-start | bytes 3080 | tf_op jit(solution)/shard_map/ppermute | solution.py:26

commit v5 on v3

--- a/solution.py
+++ b/solution.py
@@ -13,10 +13,12 @@
 EPS = 1e-05
 MASKED = -1000000000.0
 EXCL = WIN // 4
-KC = 16
+STEP_K = 4
+GROUP = 32
+UNITS = 2
 LANES = 128
 ALIGN = 8
-VMEM_LIMIT = 40 << 20
+VMEM_LIMIT = 16 << 20
 SMALL_LIMIT = 8 << 20
 
 
@@ -70,23 +72,73 @@
     return src_m, src_v, bufs[level % 2]
 
 
-def corr_kernel(rows, cols, own_far, odd_side, b2, even_side, *refs):
-    outs, (own, arrived, x2, x8, ma, mb, va, vb, za, zb, acc) = refs[:4], refs[4:]
-    fetch = pltpu.make_async_copy(own_far, own, arrived)
-    fetch.start()
+def contract(base, x8, mean_ref, scale_ref, zr, out, fill):
+    rows = zr.shape[2]
+    size = out.shape[0]
+    first_row = STEPS * rows
+
+    def windows(at, step):
+        mean = mean_ref[pl.ds(at, GROUP), :]
+        scale = scale_ref[pl.ds(at, GROUP), :]
+        lag = lax.rem(step, 2) * STEP_K
+        start = pl.multiple_of(step // 2 * ALIGN + at, ALIGN)
+        z = []
+        for k in range(STEP_K):
+            x = x8[lag + k, pl.ds(start, GROUP), :]
+            z.append(((x - mean) * scale).astype(jnp.bfloat16))
+        return jnp.concatenate(z[:2], axis=1), jnp.concatenate(z[2:], axis=1)
+
+    def stage(step):
+        if fill:
+            for at in range(0, rows, GROUP):
+                for unit, z in enumerate(windows(first_row + at, step)):
+                    zr[step, unit, at : at + GROUP, :] = z
+        for unit in range(UNITS):
+            pltpu.matmul_push_rhs(zr[step, unit], 0, unit, transpose=True)
+
+    def run(*sums):
+        sums = sums[: len(sums) // UNITS], sums[len(sums) // UNITS :]
+
+        def stream(step, following):
+            for g, at in enumerate(range(0, size, GROUP)):
+                pair = windows(pl.multiple_of(base + at, GROUP), step)
+                for unit in range(UNITS):
+                    pltpu.matmul_acc_lhs(sums[unit][g], pair[unit], 0 if g == 0 else None)
+                if g == 0 and following:
+                    stage(step + 1)
+
+        for g in range(size // GROUP):
+            for unit in range(UNITS):
+                pltpu.matmul_pop(sums[unit][g])
+        steps = HALF // STEP_K
+        stage(0)
+
+        def advance(step, carry):
+            stream(step, True)
+            return carry
+
+        lax.fori_loop(0, steps - 1, advance, 0)
+        stream(steps - 1, False)
+        for g, at in enumerate(range(0, size, GROUP)):
+            both = pltpu.matmul_pop(sums[0][g]) + pltpu.matmul_pop(sums[1][g])
+            out[at : at + GROUP, :] = both.astype(out.dtype)
+
+    pl.run_scoped(run, *[pltpu.ACC(unit)((GROUP, rows), jnp.float32) for unit in range(UNITS) for _ in range(size // GROUP)])
+
+
+def far_kernel(rows, own, odd_side, b2, even_side, out, x8, end_m, end_v, zr, x2, ma, mb, va, vb):
     total = (STEPS + 1) * rows
     span = total + HALF
     odd = lax.rem(lax.axis_index("tm"), 2) == 1
     from_odd, from_even = odd_side[...], even_side[...]
     before = jnp.where(odd, from_even, from_odd)
     after = jnp.where(odd, from_odd, from_even)
-    fetch.wait()
     joined = jnp.concatenate([b2[...], before, own[...], after], axis=1)
     both = jnp.concatenate([joined[:, :span], joined[:, HALF : HALF + span]], axis=0)
     for at in range(0, span, LANES):
         x2[at : at + LANES, :] = both[:, at : at + LANES].T
 
-    src_m, src_v, (end_m, end_v) = window_sums(x2, [(ma, va), (mb, vb)], span)
+    src_m, src_v, _ = window_sums(x2, [(ma, va), (mb, vb)], span)
     for at in range(0, total, LANES):
         m0 = src_m[at : at + LANES, :]
         v0 = src_v[at : at + LANES, :]
@@ -101,49 +153,19 @@
         for at in range(0, span, LANES):
             x8[s, at : at + LANES, :] = x2[at + s : at + s + LANES, :]
 
-    group = 64
-
-    def build(chunk, z):
-        base = pl.multiple_of(chunk * KC, KC)
-        for at in range(0, total, group):
-            mean = end_m[at : at + group, :]
-            scale = end_v[at : at + group, :]
-            for k in range(KC):
-                start = pl.multiple_of(base + (at + k // ALIGN * ALIGN), ALIGN)
-                x = x8[k % ALIGN, pl.ds(start, group), :]
-                z[at : at + group, k * LANES : (k + 1) * LANES] = ((x - mean) * scale).astype(jnp.bfloat16)
-
-    def product(z):
-        acc[...] += lax.dot_general(
-            z[:cols, :], z[total - rows :, :], (((1,), (1,)), ((), ())), preferred_element_type=jnp.float32
-        )
-
-    acc[...] = jnp.zeros_like(acc)
-    chunks = HALF // KC
-    build(0, za)
-
-    def pair(p, carry):
-        build(2 * p + 1, zb)
-        product(za)
-        build(2 * p + 2, za)
-        product(zb)
-        return carry
-
-    lax.fori_loop(0, chunks // 2 - 1, pair, 0)
-    build(chunks - 1, zb)
-    product(za)
-    product(zb)
-    part = lax.axis_index("chan")
-    for d, out in enumerate(outs):
-        which = part ^ d
-        size = out.shape[0]
-        out[...] = acc[pl.ds(pl.multiple_of(which * size, 16), size), :].astype(out.dtype)
+    base = (1 - lax.axis_index("chan") // 2) * out.shape[0]
+    contract(base, x8, end_m, end_v, zr, out, True)
+
+
+def near_kernel(x8, end_m, end_v, zr, out):
+    base = lax.axis_index("chan") // 2 * out.shape[0]
+    contract(base, x8, end_m, end_v, zr, out, False)
 
 
 def peak_kernel(rows, lens, p0, p1, p2, p3, out):
     quarter = p0.shape[0]
     block = lax.axis_index("tm")
-    part = lax.axis_index("chan")
+    part = lax.axis_index("chan") // 2
     last = rows * lax.axis_size("tm") - WIN
     seg = rows // 2
     start = (block - STEPS) * rows
@@ -170,41 +192,50 @@
 
 def body(series, lengths):
     chans, rows = series.shape
-    parts = lax.axis_size("chan")
     total = (STEPS + 1) * rows
     cols = total - EXCL
-    quarter = cols // parts
+    side = cols // 2
+    even_side = sent(series, "tm", even_pair)
     b2 = sent(series, "tm", two_on)
-    even_side = sent(series, "tm", even_pair)
     odd_side = sent(series, "tm", odd_pair)
     vmem = pl.BlockSpec(memory_space=pltpu.VMEM)
     smem = pl.BlockSpec(memory_space=pltpu.SMEM)
     f32 = jnp.float32
     bf16 = jnp.bfloat16
     room = total + HALF + HALF
-    pieces = pl.pallas_call(
-        functools.partial(corr_kernel, rows, cols),
-        out_shape=[jax.ShapeDtypeStruct((quarter, rows), f32 if d < 2 else bf16) for d in range(parts)],
-        in_specs=[pl.BlockSpec(memory_space=pltpu.HBM)] + [vmem] * 3,
-        out_specs=[vmem] * parts,
-        scratch_shapes=[pltpu.VMEM((chans, rows), f32), pltpu.SemaphoreType.DMA, pltpu.VMEM((room, LANES), f32)]
-        + [pltpu.VMEM((ALIGN, room, LANES), f32)]
-        + [pltpu.VMEM((room, LANES), f32)] * 4
-        + [pltpu.VMEM((total, KC * LANES), bf16)] * 2
-        + [pltpu.VMEM((cols, rows), f32)],
+    tall = jax.ShapeDtypeStruct((room, LANES), f32)
+    far, *shared = pl.pallas_call(
+        functools.partial(far_kernel, rows),
+        out_shape=[
+            jax.ShapeDtypeStruct((side, rows), bf16),
+            jax.ShapeDtypeStruct((ALIGN, room, LANES), f32),
+            tall,
+            tall,
+            jax.ShapeDtypeStruct((HALF // STEP_K, UNITS, rows, 2 * LANES), bf16),
+        ],
+        in_specs=[vmem] * 4,
+        out_specs=[vmem] * 5,
+        scratch_shapes=[pltpu.VMEM((room, LANES), f32)] * 5,
         compiler_params=pltpu.CompilerParams(vmem_limit_bytes=VMEM_LIMIT),
     )(series, odd_side, b2, even_side)
-    got = [pieces[0]] + [sent(pieces[d], "chan", across(d)) for d in range(1, parts)]
+    far_got = sent(far, "chan", across(2))
+    near = pl.pallas_call(
+        near_kernel,
+        out_shape=jax.ShapeDtypeStruct((side, rows), f32),
+        in_specs=[vmem] * 4,
+        out_specs=vmem,
+        compiler_params=pltpu.CompilerParams(vmem_limit_bytes=SMALL_LIMIT),
+    )(*shared)
+    near_peer = sent(near, "chan", across(1))
+    far_peer = sent(far_got, "chan", across(1))
     best = pl.pallas_call(
         functools.partial(peak_kernel, rows),
         out_shape=jax.ShapeDtypeStruct((1, rows), f32),
-        in_specs=[smem] + [vmem] * parts,
+        in_specs=[smem] + [vmem] * 4,
         out_specs=vmem,
         compiler_params=pltpu.CompilerParams(vmem_limit_bytes=SMALL_LIMIT),
-    )(lengths, *got)
-    peers = [sent(best, "chan", across(d)) for d in range(1, parts)]
-    for peer in peers:
-        best = jnp.maximum(best, peer)
+    )(lengths, near, near_peer, far_got, far_peer)
+    best = jnp.maximum(best, sent(best, "chan", across(2)))
     return jnp.where(best > 0.5 * MASKED, best, 0.0).reshape(rows)
 
 

time: 40.2 us -> 34.6 us (0.86)
  the two profiles are of different devices: /device:TPU:16 before, /device:TPU:8 now
where the time goes in v5:
time: 34.6 us; the launch traced here: 34.4 us
  starting transfers between devices  13.1 us (38%)
  Pallas kernels  11 us (32%)
  waiting for transfers between devices  8.85 us (26%)
  local copies, waits for them, and re-layouts  0.84 us (2%)
  other arithmetic  0.57 us (2%)
    ppermute x7, starting transfers between devices, sent(): lax.ppermute(block, axis, [(i, target(i, count)) for i in range(count)])  13.1 us
    ppermute x7, waiting for transfers between devices, sent(): lax.ppermute(block, axis, [(i, target(i, count)) for i in range(count)])  8.85 us
    pallas_call x1, Pallas kernels, body(): pl.pallas_call(functools.partial(far_kernel, rows), out_shape=[jax.ShapeD...  6.33 us
    pallas_call x1, Pallas kernels, body(): pl.pallas_call(near_kernel, out_shape=jax.ShapeDtypeStruct((side, rows),...  3.81 us
    unnamed x4, local copies, waits for them, and re-layouts  0.84 us
    pallas_call x1, Pallas kernels, body(): pl.pallas_call(functools.partial(peak_kernel, rows), out_shape=jax.ShapeD...  0.84 us
  transfers between devices with their start and end apart: 7, of which 4 were waited for; matrix products, arithmetic and copies ran while one was open for 0% of the time, Pallas kernels for 11%

profile of v5, /device:TPU:8, one launch (start us, length us, event | category | flops | bytes accessed | tf_op | source)
XLA Modules:
  0.0 34.4 jit_solution(17923123112971239474)
XLA Ops:
  0.0 3.9 %collective-permute-start.1 = (f32[64,256]{1,0:T(8,128)}, f32[64,256]{1,0:T(8,128)S(1)}, u32[]{:S(2)}, u32[]{:S(2)}) collective-permute-start(f32[64,256]{1,0:T(8,128)} %own.1), channel_id=1, source_target_pairs={{0,8},{4,12},{8,16},{12,20},{16,24},{20,28},{24,32},{28,36},{32,40... | collective-permute-start | bytes 196616 | tf_op jit(solution)/shard_map/ppermute | solution.py:27
  3.9 5.9 %collective-permute-start = (f32[64,256]{1,0:T(8,128)}, f32[64,256]{1,0:T(8,128)S(1)}, u32[]{:S(2)}, u32[]{:S(2)}) collective-permute-start(f32[64,256]{1,0:T(8,128)} %own.1), channel_id=1, source_target_pairs={{0,0},{4,8},{8,4},{12,16},{16,12},{20,24},{24,20},{28,32},{32,28},... | collective-permute-start | bytes 196616 | tf_op jit(solution)/shard_map/ppermute | solution.py:27
  9.8 0.1 collective-permute-start.2
  9.9 0.0 collective-permute-done.1.b2
  9.9 4.8 %collective-permute-done.odd_side = f32[64,256]{1,0:T(8,128)S(1)} collective-permute-done((f32[64,256]{1,0:T(8,128)}, f32[64,256]{1,0:T(8,128)S(1)}, u32[]{:S(2)}, u32[]{:S(2)}) %collective-permute-start) | collective-permute-done | bytes 65568 | tf_op jit(solution)/shard_map/ppermute | solution.py:27
  14.7 0.0 collective-permute-done.2.even_side
  14.8 0.0 copy-start
  14.8 0.8 %copy-done = f32[64,256]{1,0:T(8,128)S(1)} copy-done((f32[64,256]{1,0:T(8,128)S(1)}, f32[64,256]{1,0:T(8,128)}, u32[]{:S(2)}) %copy-start) | copy-done | bytes 65560
  15.6 0.0 copy-start.1
  15.6 6.3 %shard_map.28 = (bf16[352,256]{1,0:T(8,128)(2,1)S(1)}, f32[8,1024,128]{2,1,0:T(8,128)S(1)}, f32[1024,128]{1,0:T(8,128)S(1)}, f32[1024,128]{1,0:T(8,128)S(1)}, bf16[32,2,256,256]{3,2,1,0:T(8,128)(2,1)S(1)}) custom-call(f32[64,256]{1,0:T(8,128)S(1)} %copy-done, f32[64,256]{1,0:T(8,128)S(1)} %collective-permute-done.odd_side, ...), custom_call_target="tpu_custom_call" | custom-call | tf_op jit(solution)/shard_map/pallas_call | solution.py:207
  21.9 1.6 %collective-permute-start.4 = (bf16[352,256]{1,0:T(8,128)(2,1)S(1)}, bf16[352,256]{1,0:T(8,128)(2,1)S(1)}, u32[]{:S(2)}, u32[]{:S(2)}) collective-permute-start(bf16[352,256]{1,0:T(8,128)(2,1)S(1)} %get-tuple-element.14), channel_id=1, source_target_pairs={{0,2},{1,3},{2,0},{3,1},{4,6},{5,7},{6,4},{7,5},{8,10},{9,11},{10,... | collective-permute-start | bytes 540680 | tf_op jit(solution)/shard_map/ppermute | solution.py:27
  23.5 3.8 %shard_map.29.p0 = f32[352,256]{1,0:T(8,128)S(1)} custom-call(f32[8,1024,128]{2,1,0:T(8,128)S(1)} %get-tuple-element.10.x8, f32[1024,128]{1,0:T(8,128)S(1)} %get-tuple-element.11.end_m, f32[1024,128]{1,0:T(8,128)S(1)} %get-tuple-element.12.end_v, bf16[32,2,256,256]{3,2,1,0:T(8,128)(2,1)S(1)} %get-tuple-element.13.zr), custom_call_target="tpu_custom_call" | custom-call | tf_op jit(solution)/shard_map/pallas_call | solution.py:222
  27.3 0.1 collective-permute-start.3
  27.4 0.1 collective-permute-done.4.p2
  27.5 0.4 %collective-permute-start.5 = (bf16[352,256]{1,0:T(8,128)(2,1)S(1)}, bf16[352,256]{1,0:T(8,128)(2,1)S(1)}, u32[]{:S(2)}, u32[]{:S(2)}) collective-permute-start(bf16[352,256]{1,0:T(8,128)(2,1)S(1)} %collective-permute-done.4.p2), channel_id=1, source_target_pairs={{0,1},{1,0},{2,3},{3,2},{4,5},{5,4},{6,7},{7,6},{8,9},{9,8},{10,11... | collective-permute-start | bytes 540680 | tf_op jit(solution)/shard_map/ppermute | solution.py:27
  27.9 1.4 %collective-permute-done.5.p3 = bf16[352,256]{1,0:T(8,128)(2,1)S(1)} collective-permute-done((bf16[352,256]{1,0:T(8,128)(2,1)S(1)}, bf16[352,256]{1,0:T(8,128)(2,1)S(1)}, u32[]{:S(2)}, u32[]{:S(2)}) %collective-permute-start.5) | collective-permute-done | bytes 180256 | tf_op jit(solution)/shard_map/ppermute | solution.py:27
  29.3 0.0 collective-permute-done.3.p1
  29.3 0.0 copy-done.1
  29.3 0.8 %shard_map.30 = f32[1,256]{1,0:T(1,128)S(1)} custom-call(s32[64]{0:T(128)S(1)} %copy-done.1, f32[352,256]{1,0:T(8,128)S(1)} %shard_map.29.p0, f32[352,256]{1,0:T(8,128)S(1)} %collective-permute-done.3.p1, bf16[352,256]{1,0:T(8,128)(2,1)S(1)} %collective-permute-done.4.p2, bf16[352,256]{1,0:T(8,128)(2,1)S(1)} %collective-permute-done.5.p3), custom_call_target="tpu_custom_call" | custom-call | tf_op jit(solution)/shard_map/pallas_call | solution.py:231
  30.2 1.2 %collective-permute-start.6 = (f32[1,256]{1,0:T(1,128)S(1)}, f32[1,256]{1,0:T(1,128)S(1)}, u32[]{:S(2)}, u32[]{:S(2)}) collective-permute-start(f32[1,256]{1,0:T(1,128)S(1)} %shard_map.30), channel_id=1, source_target_pairs={{0,2},{1,3},{2,0},{3,1},{4,6},{5,7},{6,4},{7,5},{8,10},{9,11},{10,... | collective-permute-start | bytes 3080 | tf_op jit(solution)/shard_map/ppermute | solution.py:27
  31.3 2.5 %collective-permute-done.6 = f32[1,256]{1,0:T(1,128)S(1)} collective-permute-done((f32[1,256]{1,0:T(1,128)S(1)}, f32[1,256]{1,0:T(1,128)S(1)}, u32[]{:S(2)}, u32[]{:S(2)}) %collective-permute-start.6) | collective-permute-done | bytes 1056 | tf_op jit(solution)/shard_map/ppermute | solution.py:27
  33.8 0.6 %compare_select_fusion = f32[1,256]{1,0:T(1,128)} fusion(f32[1,256]{1,0:T(1,128)S(1)} %shard_map.30, f32[1,256]{1,0:T(1,128)S(1)} %collective-permute-done.6), kind=kLoop, calls=%fused_computation | loop fusion | flops 768 | bytes 3072 | tf_op jit(solution)/shard_map/jit(_where)/select_n | solution.py:239
Async XLA Ops:
  0.0 9.9 %collective-permute-start.1 = (f32[64,256]{1,0:T(8,128)}, f32[64,256]{1,0:T(8,128)S(1)}, u32[]{:S(2)}, u32[]{:S(2)}) collective-permute-start(f32[64,256]{1,0:T(8,128)} %own.1), channel_id=1, source_target_pairs={{0,8},{4,12},{8,16},{12,20},{16,24},{20,28},{24,32},{28,36},{32,40... | collective-permute-start | bytes 196616 | tf_op jit(solution)/shard_map/ppermute | solution.py:27
  3.9 10.9 %collective-permute-start = (f32[64,256]{1,0:T(8,128)}, f32[64,256]{1,0:T(8,128)S(1)}, u32[]{:S(2)}, u32[]{:S(2)}) collective-permute-start(f32[64,256]{1,0:T(8,128)} %own.1), channel_id=1, source_target_pairs={{0,0},{4,8},{8,4},{12,16},{16,12},{20,24},{24,20},{28,32},{32,28},... | collective-permute-start | bytes 196616 | tf_op jit(solution)/shard_map/ppermute | solution.py:27
  9.8 5.0 %collective-permute-start.2 = (f32[64,256]{1,0:T(8,128)}, f32[64,256]{1,0:T(8,128)S(1)}, u32[]{:S(2)}, u32[]{:S(2)}) collective-permute-start(f32[64,256]{1,0:T(8,128)} %own.1), channel_id=1, source_target_pairs={{0,4},{4,0},{8,12},{12,8},{16,20},{20,16},{24,28},{28,24},{32,36},... | collective-permute-start | bytes 196616 | tf_op jit(solution)/shard_map/ppermute | solution.py:27
  14.8 0.8 %copy-start = (f32[64,256]{1,0:T(8,128)S(1)}, f32[64,256]{1,0:T(8,128)}, u32[]{:S(2)}) copy-start(f32[64,256]{1,0:T(8,128)} %own.1) | copy-start | bytes 196612
  15.6 13.7 %copy-start.1 = (s32[64]{0:T(128)S(1)}, s32[64]{0:T(128)}, u32[]{:S(2)}) copy-start(s32[64]{0:T(128)} %lens.1) | copy-start | bytes 772
  21.9 5.6 %collective-permute-start.4 = (bf16[352,256]{1,0:T(8,128)(2,1)S(1)}, bf16[352,256]{1,0:T(8,128)(2,1)S(1)}, u32[]{:S(2)}, u32[]{:S(2)}) collective-permute-start(bf16[352,256]{1,0:T(8,128)(2,1)S(1)} %get-tuple-element.14), channel_id=1, source_target_pairs={{0,2},{1,3},{2,0},{3,1},{4,6},{5,7},{6,4},{7,5},{8,10},{9,11},{10,... | collective-permute-start | bytes 540680 | tf_op jit(solution)/shard_map/ppermute | solution.py:27
  27.3 2.0 %collective-permute-start.3 = (f32[352,256]{1,0:T(8,128)S(1)}, f32[352,256]{1,0:T(8,128)S(1)}, u32[]{:S(2)}, u32[]{:S(2)}) collective-permute-start(f32[352,256]{1,0:T(8,128)S(1)} %shard_map.29.p0), channel_id=1, source_target_pairs={{0,1},{1,0},{2,3},{3,2},{4,5},{5,4},{6,7},{7,6},{8,9},{9,8},{10,11... | collective-permute-start | bytes 1081352 | tf_op jit(solution)/shard_map/ppermute | solution.py:27
  27.5 1.8 %collective-permute-start.5 = (bf16[352,256]{1,0:T(8,128)(2,1)S(1)}, bf16[352,256]{1,0:T(8,128)(2,1)S(1)}, u32[]{:S(2)}, u32[]{:S(2)}) collective-permute-start(bf16[352,256]{1,0:T(8,128)(2,1)S(1)} %collective-permute-done.4.p2), channel_id=1, source_target_pairs={{0,1},{1,0},{2,3},{3,2},{4,5},{5,4},{6,7},{7,6},{8,9},{9,8},{10,11... | collective-permute-start | bytes 540680 | tf_op jit(solution)/shard_map/ppermute | solution.py:27
  30.2 3.6 %collective-permute-start.6 = (f32[1,256]{1,0:T(1,128)S(1)}, f32[1,256]{1,0:T(1,128)S(1)}, u32[]{:S(2)}, u32[]{:S(2)}) collective-permute-start(f32[1,256]{1,0:T(1,128)S(1)} %shard_map.30), channel_id=1, source_target_pairs={{0,2},{1,3},{2,0},{3,1},{4,6},{5,7},{6,4},{7,5},{8,10},{9,11},{10,... | collective-permute-start | bytes 3080 | tf_op jit(solution)/shard_map/ppermute | solution.py:27

commit v6 on v5

--- a/solution.py
+++ b/solution.py
@@ -27,18 +27,23 @@
     return lax.ppermute(block, axis, [(i, target(i, count)) for i in range(count)])
 
 
-def two_on(i, count):
-    return (i + 2) % count
-
-
-def even_pair(i, count):
+LINE = 4
+
+
+def first_step(i, count):
+    return (i + (2, 2, -1, 1)[i % LINE]) % count
+
+
+def second_step(i, count):
+    if i in (0, count - 1):
+        return i
+    if i == count - 2:
+        return 1
+    return i + (-1, 1, 2, 2)[i % LINE]
+
+
+def third_step(i, count):
     return i ^ 1
-
-
-def odd_pair(i, count):
-    if i == 0 or i == count - 1:
-        return i
-    return i + 1 if i % 2 == 1 else i - 1
 
 
 def across(distance):
@@ -126,14 +131,16 @@
     pl.run_scoped(run, *[pltpu.ACC(unit)((GROUP, rows), jnp.float32) for unit in range(UNITS) for _ in range(size // GROUP)])
 
 
-def far_kernel(rows, own, odd_side, b2, even_side, out, x8, end_m, end_v, zr, x2, ma, mb, va, vb):
+def far_kernel(rows, own, from_first, from_third, from_second, out, x8, end_m, end_v, zr, x2, ma, mb, va, vb):
     total = (STEPS + 1) * rows
     span = total + HALF
-    odd = lax.rem(lax.axis_index("tm"), 2) == 1
-    from_odd, from_even = odd_side[...], even_side[...]
-    before = jnp.where(odd, from_even, from_odd)
-    after = jnp.where(odd, from_odd, from_even)
-    joined = jnp.concatenate([b2[...], before, own[...], after], axis=1)
+    place = lax.rem(lax.axis_index("tm"), LINE)
+    first, second, third = from_first[...], from_second[...], from_third[...]
+    earlier = jnp.where(place < 2, second, first)
+    odd = lax.rem(place, 2) == 1
+    before = jnp.where(odd, third, jnp.where(place == 0, first, second))
+    after = jnp.where(odd, jnp.where(place == 1, first, second), third)
+    joined = jnp.concatenate([earlier, before, own[...], after], axis=1)
     both = jnp.concatenate([joined[:, :span], joined[:, HALF : HALF + span]], axis=0)
     for at in range(0, span, LANES):
         x2[at : at + LANES, :] = both[:, at : at + LANES].T
@@ -195,9 +202,10 @@
     total = (STEPS + 1) * rows
     cols = total - EXCL
     side = cols // 2
-    even_side = sent(series, "tm", even_pair)
-    b2 = sent(series, "tm", two_on)
-    odd_side = sent(series, "tm", odd_pair)
+    own = jnp.maximum(series, jnp.finfo(series.dtype).min)
+    from_first = sent(series, "tm", first_step)
+    from_second = sent(series, "tm", second_step)
+    from_third = sent(series, "tm", third_step)
     vmem = pl.BlockSpec(memory_space=pltpu.VMEM)
     smem = pl.BlockSpec(memory_space=pltpu.SMEM)
     f32 = jnp.float32
@@ -217,7 +225,7 @@
         out_specs=[vmem] * 5,
         scratch_shapes=[pltpu.VMEM((room, LANES), f32)] * 5,
         compiler_params=pltpu.CompilerParams(vmem_limit_bytes=VMEM_LIMIT),
-    )(series, odd_side, b2, even_side)
+    )(own, from_first, from_third, from_second)
     far_got = sent(far, "chan", across(2))
     near = pl.pallas_call(
         near_kernel,

time: 34.6 us -> 34.2 us (0.988)
  the two profiles are of different devices: /device:TPU:8 before, /device:TPU:16 now
where the time goes in v6:
time: 34.2 us; the launch traced here: 34 us
  starting transfers between devices  11.9 us (35%)
  Pallas kernels  11 us (32%)
  waiting for transfers between devices  9.54 us (28%)
  other arithmetic  1.44 us (4%)
    ppermute x7, starting transfers between devices, sent(): lax.ppermute(block, axis, [(i, target(i, count)) for i in range(count)])  11.9 us
    ppermute x7, waiting for transfers between devices, sent(): lax.ppermute(block, axis, [(i, target(i, count)) for i in range(count)])  9.54 us
    pallas_call x1, Pallas kernels, body(): pl.pallas_call(functools.partial(far_kernel, rows), out_shape=[jax.ShapeD...  6.34 us
    pallas_call x1, Pallas kernels, body(): pl.pallas_call(near_kernel, out_shape=jax.ShapeDtypeStruct((side, rows),...  3.81 us
    max x1, other arithmetic, body(): own = jnp.maximum(series, jnp.finfo(series.dtype).min)  0.87 us
    pallas_call x1, Pallas kernels, body(): pl.pallas_call(functools.partial(peak_kernel, rows), out_shape=jax.ShapeD...  0.84 us
  transfers between devices with their start and end apart: 7, of which 3 were waited for; matrix products, arithmetic and copies ran while one was open for 3% of the time, Pallas kernels for 11%

profile of v6, /device:TPU:16, one launch (start us, length us, event | category | flops | bytes accessed | tf_op | source)
XLA Modules:
  0.0 34.0 jit_solution(751342710409580499)
XLA Ops:
  0.0 0.0 copy-start
  0.0 3.9 %collective-permute-start = (f32[64,256]{1,0:T(8,128)}, f32[64,256]{1,0:T(8,128)S(1)}, u32[]{:S(2)}, u32[]{:S(2)}) collective-permute-start(f32[64,256]{1,0:T(8,128)} %param.2), channel_id=1, source_target_pairs={{0,8},{4,12},{8,4},{12,16},{16,24},{20,28},{24,20},{28,32},{32,40}... | collective-permute-start | bytes 196616 | tf_op jit(solution)/shard_map/ppermute | solution.py:27
  3.9 4.6 %collective-permute-start.2 = (f32[64,256]{1,0:T(8,128)}, f32[64,256]{1,0:T(8,128)S(1)}, u32[]{:S(2)}, u32[]{:S(2)}) collective-permute-start(f32[64,256]{1,0:T(8,128)} %param.2), channel_id=1, source_target_pairs={{0,0},{4,8},{8,16},{12,20},{16,12},{20,24},{24,32},{28,36},{32,28}... | collective-permute-start | bytes 196616 | tf_op jit(solution)/shard_map/ppermute | solution.py:27
  8.4 0.1 collective-permute-start.1
  8.5 0.9 %broadcast_maximum_fusion.own = f32[64,256]{1,0:T(8,128)S(1)} fusion(f32[64,256]{1,0:T(8,128)} %param.2), kind=kLoop, calls=%fused_computation | loop fusion | flops 16384 | bytes 131072 | tf_op jit(solution)/shard_map/max | solution.py:205
  9.4 0.0 collective-permute-done.from_first
  9.4 5.6 %collective-permute-done.2.from_second = f32[64,256]{1,0:T(8,128)S(1)} collective-permute-done((f32[64,256]{1,0:T(8,128)}, f32[64,256]{1,0:T(8,128)S(1)}, u32[]{:S(2)}, u32[]{:S(2)}) %collective-permute-start.2) | collective-permute-done | bytes 65568 | tf_op jit(solution)/shard_map/ppermute | solution.py:27
  15.0 0.0 collective-permute-done.1.from_third
  15.0 6.3 %shard_map.28 = (bf16[352,256]{1,0:T(8,128)(2,1)S(1)}, f32[8,1024,128]{2,1,0:T(8,128)S(1)}, f32[1024,128]{1,0:T(8,128)S(1)}, f32[1024,128]{1,0:T(8,128)S(1)}, bf16[32,2,256,256]{3,2,1,0:T(8,128)(2,1)S(1)}) custom-call(f32[64,256]{1,0:T(8,128)S(1)} %broadcast_maximum_fusion.own, f32[64,256]{1,0:T(8,128)S(1)} %collective-permute-done.from_first, ...), custom_call_target="tpu_custom_call" | custom-call | tf_op jit(solution)/shard_map/pallas_call | solution.py:215
  21.4 1.7 %collective-permute-start.4 = (bf16[352,256]{1,0:T(8,128)(2,1)S(1)}, bf16[352,256]{1,0:T(8,128)(2,1)S(1)}, u32[]{:S(2)}, u32[]{:S(2)}) collective-permute-start(bf16[352,256]{1,0:T(8,128)(2,1)S(1)} %get-tuple-element.14), channel_id=1, source_target_pairs={{0,2},{1,3},{2,0},{3,1},{4,6},{5,7},{6,4},{7,5},{8,10},{9,11},{10,... | collective-permute-start | bytes 540680 | tf_op jit(solution)/shard_map/ppermute | solution.py:27
  23.1 3.8 %shard_map.29.p0 = f32[352,256]{1,0:T(8,128)S(1)} custom-call(f32[8,1024,128]{2,1,0:T(8,128)S(1)} %get-tuple-element.10.x8, f32[1024,128]{1,0:T(8,128)S(1)} %get-tuple-element.11.end_m, f32[1024,128]{1,0:T(8,128)S(1)} %get-tuple-element.12.end_v, bf16[32,2,256,256]{3,2,1,0:T(8,128)(2,1)S(1)} %get-tuple-element.13.zr), custom_call_target="tpu_custom_call" | custom-call | tf_op jit(solution)/shard_map/pallas_call | solution.py:230
  26.9 0.1 collective-permute-start.3
  27.0 0.0 collective-permute-done.4.p2
  27.0 0.5 %collective-permute-start.5 = (bf16[352,256]{1,0:T(8,128)(2,1)S(1)}, bf16[352,256]{1,0:T(8,128)(2,1)S(1)}, u32[]{:S(2)}, u32[]{:S(2)}) collective-permute-start(bf16[352,256]{1,0:T(8,128)(2,1)S(1)} %collective-permute-done.4.p2), channel_id=1, source_target_pairs={{0,1},{1,0},{2,3},{3,2},{4,5},{5,4},{6,7},{7,6},{8,9},{9,8},{10,11... | collective-permute-start | bytes 540680 | tf_op jit(solution)/shard_map/ppermute | solution.py:27
  27.5 1.4 %collective-permute-done.5.p3 = bf16[352,256]{1,0:T(8,128)(2,1)S(1)} collective-permute-done((bf16[352,256]{1,0:T(8,128)(2,1)S(1)}, bf16[352,256]{1,0:T(8,128)(2,1)S(1)}, u32[]{:S(2)}, u32[]{:S(2)}) %collective-permute-start.5) | collective-permute-done | bytes 180256 | tf_op jit(solution)/shard_map/ppermute | solution.py:27
  28.9 0.0 collective-permute-done.3.p1
  28.9 0.0 copy-done
  28.9 0.8 %shard_map.30 = f32[1,256]{1,0:T(1,128)S(1)} custom-call(s32[64]{0:T(128)S(1)} %copy-done, f32[352,256]{1,0:T(8,128)S(1)} %shard_map.29.p0, f32[352,256]{1,0:T(8,128)S(1)} %collective-permute-done.3.p1, bf16[352,256]{1,0:T(8,128)(2,1)S(1)} %collective-permute-done.4.p2, bf16[352,256]{1,0:T(8,128)(2,1)S(1)} %collective-permute-done.5.p3), custom_call_target="tpu_custom_call" | custom-call | tf_op jit(solution)/shard_map/pallas_call | solution.py:239
  29.8 1.2 %collective-permute-start.6 = (f32[1,256]{1,0:T(1,128)S(1)}, f32[1,256]{1,0:T(1,128)S(1)}, u32[]{:S(2)}, u32[]{:S(2)}) collective-permute-start(f32[1,256]{1,0:T(1,128)S(1)} %shard_map.30), channel_id=1, source_target_pairs={{0,2},{1,3},{2,0},{3,1},{4,6},{5,7},{6,4},{7,5},{8,10},{9,11},{10,... | collective-permute-start | bytes 3080 | tf_op jit(solution)/shard_map/ppermute | solution.py:27
  30.9 2.5 %collective-permute-done.6 = f32[1,256]{1,0:T(1,128)S(1)} collective-permute-done((f32[1,256]{1,0:T(1,128)S(1)}, f32[1,256]{1,0:T(1,128)S(1)}, u32[]{:S(2)}, u32[]{:S(2)}) %collective-permute-start.6) | collective-permute-done | bytes 1056 | tf_op jit(solution)/shard_map/ppermute | solution.py:27
  33.4 0.6 %compare_select_fusion = f32[1,256]{1,0:T(1,128)} fusion(f32[1,256]{1,0:T(1,128)S(1)} %shard_map.30, f32[1,256]{1,0:T(1,128)S(1)} %collective-permute-done.6), kind=kLoop, calls=%fused_computation.1 | loop fusion | flops 768 | bytes 3072 | tf_op jit(solution)/shard_map/jit(_where)/select_n | solution.py:247
Async XLA Ops:
  0.0 28.9 %copy-start = (s32[64]{0:T(128)S(1)}, s32[64]{0:T(128)}, u32[]{:S(2)}) copy-start(s32[64]{0:T(128)} %lens.1) | copy-start | bytes 772
  0.0 9.4 %collective-permute-start = (f32[64,256]{1,0:T(8,128)}, f32[64,256]{1,0:T(8,128)S(1)}, u32[]{:S(2)}, u32[]{:S(2)}) collective-permute-start(f32[64,256]{1,0:T(8,128)} %param.2), channel_id=1, source_target_pairs={{0,8},{4,12},{8,4},{12,16},{16,24},{20,28},{24,20},{28,32},{32,40}... | collective-permute-start | bytes 196616 | tf_op jit(solution)/shard_map/ppermute | solution.py:27
  3.9 11.2 %collective-permute-start.2 = (f32[64,256]{1,0:T(8,128)}, f32[64,256]{1,0:T(8,128)S(1)}, u32[]{:S(2)}, u32[]{:S(2)}) collective-permute-start(f32[64,256]{1,0:T(8,128)} %param.2), channel_id=1, source_target_pairs={{0,0},{4,8},{8,16},{12,20},{16,12},{20,24},{24,32},{28,36},{32,28}... | collective-permute-start | bytes 196616 | tf_op jit(solution)/shard_map/ppermute | solution.py:27
  8.4 6.6 %collective-permute-start.1 = (f32[64,256]{1,0:T(8,128)}, f32[64,256]{1,0:T(8,128)S(1)}, u32[]{:S(2)}, u32[]{:S(2)}) collective-permute-start(f32[64,256]{1,0:T(8,128)} %param.2), channel_id=1, source_target_pairs={{0,4},{4,0},{8,12},{12,8},{16,20},{20,16},{24,28},{28,24},{32,36},... | collective-permute-start | bytes 196616 | tf_op jit(solution)/shard_map/ppermute | solution.py:27
  21.4 5.6 %collective-permute-start.4 = (bf16[352,256]{1,0:T(8,128)(2,1)S(1)}, bf16[352,256]{1,0:T(8,128)(2,1)S(1)}, u32[]{:S(2)}, u32[]{:S(2)}) collective-permute-start(bf16[352,256]{1,0:T(8,128)(2,1)S(1)} %get-tuple-element.14), channel_id=1, source_target_pairs={{0,2},{1,3},{2,0},{3,1},{4,6},{5,7},{6,4},{7,5},{8,10},{9,11},{10,... | collective-permute-start | bytes 540680 | tf_op jit(solution)/shard_map/ppermute | solution.py:27
  26.9 2.0 %collective-permute-start.3 = (f32[352,256]{1,0:T(8,128)S(1)}, f32[352,256]{1,0:T(8,128)S(1)}, u32[]{:S(2)}, u32[]{:S(2)}) collective-permute-start(f32[352,256]{1,0:T(8,128)S(1)} %shard_map.29.p0), channel_id=1, source_target_pairs={{0,1},{1,0},{2,3},{3,2},{4,5},{5,4},{6,7},{7,6},{8,9},{9,8},{10,11... | collective-permute-start | bytes 1081352 | tf_op jit(solution)/shard_map/ppermute | solution.py:27
  27.0 1.9 %collective-permute-start.5 = (bf16[352,256]{1,0:T(8,128)(2,1)S(1)}, bf16[352,256]{1,0:T(8,128)(2,1)S(1)}, u32[]{:S(2)}, u32[]{:S(2)}) collective-permute-start(bf16[352,256]{1,0:T(8,128)(2,1)S(1)} %collective-permute-done.4.p2), channel_id=1, source_target_pairs={{0,1},{1,0},{2,3},{3,2},{4,5},{5,4},{6,7},{7,6},{8,9},{9,8},{10,11... | collective-permute-start | bytes 540680 | tf_op jit(solution)/shard_map/ppermute | solution.py:27
  29.8 3.6 %collective-permute-start.6 = (f32[1,256]{1,0:T(1,128)S(1)}, f32[1,256]{1,0:T(1,128)S(1)}, u32[]{:S(2)}, u32[]{:S(2)}) collective-permute-start(f32[1,256]{1,0:T(1,128)S(1)} %shard_map.30), channel_id=1, source_target_pairs={{0,2},{1,3},{2,0},{3,1},{4,6},{5,7},{6,4},{7,5},{8,10},{9,11},{10,... | collective-permute-start | bytes 3080 | tf_op jit(solution)/shard_map/ppermute | solution.py:27

commit v7 on v6

--- a/solution.py
+++ b/solution.py
@@ -35,11 +35,7 @@
 
 
 def second_step(i, count):
-    if i in (0, count - 1):
-        return i
-    if i == count - 2:
-        return 1
-    return i + (-1, 1, 2, 2)[i % LINE]
+    return (i + (-1, 1, 2, 2)[i % LINE]) % count
 
 
 def third_step(i, count):

time: 34.2 us -> 33.4 us (0.977)
  the two profiles are of different devices: /device:TPU:16 before, /device:TPU:0 now
where the time goes in v7:
time: 33.4 us; the launch traced here: 33.3 us
  starting transfers between devices  12.1 us (36%)
  Pallas kernels  11 us (33%)
  waiting for transfers between devices  8.66 us (26%)
  other arithmetic  1.48 us (4%)
    ppermute x7, starting transfers between devices, sent(): lax.ppermute(block, axis, [(i, target(i, count)) for i in range(count)])  12.1 us
    ppermute x7, waiting for transfers between devices, sent(): lax.ppermute(block, axis, [(i, target(i, count)) for i in range(count)])  8.66 us
    pallas_call x1, Pallas kernels, body(): pl.pallas_call(functools.partial(far_kernel, rows), out_shape=[jax.ShapeD...  6.33 us
    pallas_call x1, Pallas kernels, body(): pl.pallas_call(near_kernel, out_shape=jax.ShapeDtypeStruct((side, rows),...  3.81 us
    max x1, other arithmetic, body(): own = jnp.maximum(series, jnp.finfo(series.dtype).min)  0.91 us
    pallas_call x1, Pallas kernels, body(): pl.pallas_call(functools.partial(peak_kernel, rows), out_shape=jax.ShapeD...  0.84 us
  transfers between devices with their start and end apart: 7, of which 5 were waited for; matrix products, arithmetic and copies ran while one was open for 3% of the time, Pallas kernels for 11%

profile of v7, /device:TPU:0, one launch (start us, length us, event | category | flops | bytes accessed | tf_op | source)
XLA Modules:
  0.0 33.3 jit_solution(11957135653884436373)
XLA Ops:
  0.0 0.0 copy-start
  0.0 4.0 %collective-permute-start = (f32[64,256]{1,0:T(8,128)}, f32[64,256]{1,0:T(8,128)S(1)}, u32[]{:S(2)}, u32[]{:S(2)}) collective-permute-start(f32[64,256]{1,0:T(8,128)} %param.2), channel_id=1, source_target_pairs={{0,8},{4,12},{8,4},{12,16},{16,24},{20,28},{24,20},{28,32},{32,40}... | collective-permute-start | bytes 196616 | tf_op jit(solution)/shard_map/ppermute | solution.py:27
  4.0 5.1 %collective-permute-start.2 = (f32[64,256]{1,0:T(8,128)}, f32[64,256]{1,0:T(8,128)S(1)}, u32[]{:S(2)}, u32[]{:S(2)}) collective-permute-start(f32[64,256]{1,0:T(8,128)} %param.2), channel_id=1, source_target_pairs={{0,124},{4,8},{8,16},{12,20},{16,12},{20,24},{24,32},{28,36},{32,2... | collective-permute-start | bytes 196616 | tf_op jit(solution)/shard_map/ppermute | solution.py:27
  9.1 0.0 collective-permute-start.1
  9.1 0.9 %broadcast_maximum_fusion.own = f32[64,256]{1,0:T(8,128)S(1)} fusion(f32[64,256]{1,0:T(8,128)} %param.2), kind=kLoop, calls=%fused_computation | loop fusion | flops 16384 | bytes 131072 | tf_op jit(solution)/shard_map/max | solution.py:201
  10.0 1.5 %collective-permute-done.from_first = f32[64,256]{1,0:T(8,128)S(1)} collective-permute-done((f32[64,256]{1,0:T(8,128)}, f32[64,256]{1,0:T(8,128)S(1)}, u32[]{:S(2)}, u32[]{:S(2)}) %collective-permute-start) | collective-permute-done | bytes 65568 | tf_op jit(solution)/shard_map/ppermute | solution.py:27
  11.5 3.1 %collective-permute-done.2.from_second = f32[64,256]{1,0:T(8,128)S(1)} collective-permute-done((f32[64,256]{1,0:T(8,128)}, f32[64,256]{1,0:T(8,128)S(1)}, u32[]{:S(2)}, u32[]{:S(2)}) %collective-permute-start.2) | collective-permute-done | bytes 65568 | tf_op jit(solution)/shard_map/ppermute | solution.py:27
  14.6 0.0 collective-permute-done.1.from_third
  14.6 6.3 %shard_map.28 = (bf16[352,256]{1,0:T(8,128)(2,1)S(1)}, f32[8,1024,128]{2,1,0:T(8,128)S(1)}, f32[1024,128]{1,0:T(8,128)S(1)}, f32[1024,128]{1,0:T(8,128)S(1)}, bf16[32,2,256,256]{3,2,1,0:T(8,128)(2,1)S(1)}) custom-call(f32[64,256]{1,0:T(8,128)S(1)} %broadcast_maximum_fusion.own, f32[64,256]{1,0:T(8,128)S(1)} %collective-permute-done.from_first, ...), custom_call_target="tpu_custom_call" | custom-call | tf_op jit(solution)/shard_map/pallas_call | solution.py:211
  20.9 1.5 %collective-permute-start.4 = (bf16[352,256]{1,0:T(8,128)(2,1)S(1)}, bf16[352,256]{1,0:T(8,128)(2,1)S(1)}, u32[]{:S(2)}, u32[]{:S(2)}) collective-permute-start(bf16[352,256]{1,0:T(8,128)(2,1)S(1)} %get-tuple-element.14), channel_id=1, source_target_pairs={{0,2},{1,3},{2,0},{3,1},{4,6},{5,7},{6,4},{7,5},{8,10},{9,11},{10,... | collective-permute-start | bytes 540680 | tf_op jit(solution)/shard_map/ppermute | solution.py:27
  22.4 3.8 %shard_map.29.p0 = f32[352,256]{1,0:T(8,128)S(1)} custom-call(f32[8,1024,128]{2,1,0:T(8,128)S(1)} %get-tuple-element.10.x8, f32[1024,128]{1,0:T(8,128)S(1)} %get-tuple-element.11.end_m, f32[1024,128]{1,0:T(8,128)S(1)} %get-tuple-element.12.end_v, bf16[32,2,256,256]{3,2,1,0:T(8,128)(2,1)S(1)} %get-tuple-element.13.zr), custom_call_target="tpu_custom_call" | custom-call | tf_op jit(solution)/shard_map/pallas_call | solution.py:226
  26.2 0.1 collective-permute-start.3
  26.3 0.2 collective-permute-done.4.p2
  26.5 0.3 collective-permute-start.5
  26.8 1.4 %collective-permute-done.5.p3 = bf16[352,256]{1,0:T(8,128)(2,1)S(1)} collective-permute-done((bf16[352,256]{1,0:T(8,128)(2,1)S(1)}, bf16[352,256]{1,0:T(8,128)(2,1)S(1)}, u32[]{:S(2)}, u32[]{:S(2)}) %collective-permute-start.5) | collective-permute-done | bytes 180256 | tf_op jit(solution)/shard_map/ppermute | solution.py:27
  28.2 0.0 collective-permute-done.3.p1
  28.2 0.0 copy-done
  28.2 0.8 %shard_map.30 = f32[1,256]{1,0:T(1,128)S(1)} custom-call(s32[64]{0:T(128)S(1)} %copy-done, f32[352,256]{1,0:T(8,128)S(1)} %shard_map.29.p0, f32[352,256]{1,0:T(8,128)S(1)} %collective-permute-done.3.p1, bf16[352,256]{1,0:T(8,128)(2,1)S(1)} %collective-permute-done.4.p2, bf16[352,256]{1,0:T(8,128)(2,1)S(1)} %collective-permute-done.5.p3), custom_call_target="tpu_custom_call" | custom-call | tf_op jit(solution)/shard_map/pallas_call | solution.py:235
  29.1 1.2 %collective-permute-start.6 = (f32[1,256]{1,0:T(1,128)S(1)}, f32[1,256]{1,0:T(1,128)S(1)}, u32[]{:S(2)}, u32[]{:S(2)}) collective-permute-start(f32[1,256]{1,0:T(1,128)S(1)} %shard_map.30), channel_id=1, source_target_pairs={{0,2},{1,3},{2,0},{3,1},{4,6},{5,7},{6,4},{7,5},{8,10},{9,11},{10,... | collective-permute-start | bytes 3080 | tf_op jit(solution)/shard_map/ppermute | solution.py:27
  30.2 2.5 %collective-permute-done.6 = f32[1,256]{1,0:T(1,128)S(1)} collective-permute-done((f32[1,256]{1,0:T(1,128)S(1)}, f32[1,256]{1,0:T(1,128)S(1)}, u32[]{:S(2)}, u32[]{:S(2)}) %collective-permute-start.6) | collective-permute-done | bytes 1056 | tf_op jit(solution)/shard_map/ppermute | solution.py:27
  32.7 0.6 %compare_select_fusion = f32[1,256]{1,0:T(1,128)} fusion(f32[1,256]{1,0:T(1,128)S(1)} %shard_map.30, f32[1,256]{1,0:T(1,128)S(1)} %collective-permute-done.6), kind=kLoop, calls=%fused_computation.1 | loop fusion | flops 768 | bytes 3072 | tf_op jit(solution)/shard_map/jit(_where)/select_n | solution.py:243
Async XLA Ops:
  0.0 28.2 %copy-start = (s32[64]{0:T(128)S(1)}, s32[64]{0:T(128)}, u32[]{:S(2)}) copy-start(s32[64]{0:T(128)} %lens.1) | copy-start | bytes 772
  0.0 11.5 %collective-permute-start = (f32[64,256]{1,0:T(8,128)}, f32[64,256]{1,0:T(8,128)S(1)}, u32[]{:S(2)}, u32[]{:S(2)}) collective-permute-start(f32[64,256]{1,0:T(8,128)} %param.2), channel_id=1, source_target_pairs={{0,8},{4,12},{8,4},{12,16},{16,24},{20,28},{24,20},{28,32},{32,40}... | collective-permute-start | bytes 196616 | tf_op jit(solution)/shard_map/ppermute | solution.py:27
  4.0 10.6 %collective-permute-start.2 = (f32[64,256]{1,0:T(8,128)}, f32[64,256]{1,0:T(8,128)S(1)}, u32[]{:S(2)}, u32[]{:S(2)}) collective-permute-start(f32[64,256]{1,0:T(8,128)} %param.2), channel_id=1, source_target_pairs={{0,124},{4,8},{8,16},{12,20},{16,12},{20,24},{24,32},{28,36},{32,2... | collective-permute-start | bytes 196616 | tf_op jit(solution)/shard_map/ppermute | solution.py:27
  9.1 5.5 %collective-permute-start.1 = (f32[64,256]{1,0:T(8,128)}, f32[64,256]{1,0:T(8,128)S(1)}, u32[]{:S(2)}, u32[]{:S(2)}) collective-permute-start(f32[64,256]{1,0:T(8,128)} %param.2), channel_id=1, source_target_pairs={{0,4},{4,0},{8,12},{12,8},{16,20},{20,16},{24,28},{28,24},{32,36},... | collective-permute-start | bytes 196616 | tf_op jit(solution)/shard_map/ppermute | solution.py:27
  20.9 5.6 %collective-permute-start.4 = (bf16[352,256]{1,0:T(8,128)(2,1)S(1)}, bf16[352,256]{1,0:T(8,128)(2,1)S(1)}, u32[]{:S(2)}, u32[]{:S(2)}) collective-permute-start(bf16[352,256]{1,0:T(8,128)(2,1)S(1)} %get-tuple-element.14), channel_id=1, source_target_pairs={{0,2},{1,3},{2,0},{3,1},{4,6},{5,7},{6,4},{7,5},{8,10},{9,11},{10,... | collective-permute-start | bytes 540680 | tf_op jit(solution)/shard_map/ppermute | solution.py:27
  26.2 2.0 %collective-permute-start.3 = (f32[352,256]{1,0:T(8,128)S(1)}, f32[352,256]{1,0:T(8,128)S(1)}, u32[]{:S(2)}, u32[]{:S(2)}) collective-permute-start(f32[352,256]{1,0:T(8,128)S(1)} %shard_map.29.p0), channel_id=1, source_target_pairs={{0,1},{1,0},{2,3},{3,2},{4,5},{5,4},{6,7},{7,6},{8,9},{9,8},{10,11... | collective-permute-start | bytes 1081352 | tf_op jit(solution)/shard_map/ppermute | solution.py:27
  26.5 1.7 %collective-permute-start.5 = (bf16[352,256]{1,0:T(8,128)(2,1)S(1)}, bf16[352,256]{1,0:T(8,128)(2,1)S(1)}, u32[]{:S(2)}, u32[]{:S(2)}) collective-permute-start(bf16[352,256]{1,0:T(8,128)(2,1)S(1)} %collective-permute-done.4.p2), channel_id=1, source_target_pairs={{0,1},{1,0},{2,3},{3,2},{4,5},{5,4},{6,7},{7,6},{8,9},{9,8},{10,11... | collective-permute-start | bytes 540680 | tf_op jit(solution)/shard_map/ppermute | solution.py:27
  29.1 3.6 %collective-permute-start.6 = (f32[1,256]{1,0:T(1,128)S(1)}, f32[1,256]{1,0:T(1,128)S(1)}, u32[]{:S(2)}, u32[]{:S(2)}) collective-permute-start(f32[1,256]{1,0:T(1,128)S(1)} %shard_map.30), channel_id=1, source_target_pairs={{0,2},{1,3},{2,0},{3,1},{4,6},{5,7},{6,4},{7,5},{8,10},{9,11},{10,... | collective-permute-start | bytes 3080 | tf_op jit(solution)/shard_map/ppermute | solution.py:27

commit v8 on v7

--- a/solution.py
+++ b/solution.py
@@ -18,7 +18,6 @@
 UNITS = 2
 LANES = 128
 ALIGN = 8
-VMEM_LIMIT = 16 << 20
 SMALL_LIMIT = 8 << 20
 
 
@@ -35,7 +34,13 @@
 
 
 def second_step(i, count):
-    return (i + (-1, 1, 2, 2)[i % LINE]) % count
+    if i == 0:
+        return 1
+    if i == count - 2:
+        return count - 1
+    if i == count - 1:
+        return 0
+    return i + (-1, 1, 2, 2)[i % LINE]
 
 
 def third_step(i, count):
@@ -127,34 +132,59 @@
     pl.run_scoped(run, *[pltpu.ACC(unit)((GROUP, rows), jnp.float32) for unit in range(UNITS) for _ in range(size // GROUP)])
 
 
-def far_kernel(rows, own, from_first, from_third, from_second, out, x8, end_m, end_v, zr, x2, ma, mb, va, vb):
-    total = (STEPS + 1) * rows
-    span = total + HALF
-    place = lax.rem(lax.axis_index("tm"), LINE)
-    first, second, third = from_first[...], from_second[...], from_third[...]
-    earlier = jnp.where(place < 2, second, first)
-    odd = lax.rem(place, 2) == 1
-    before = jnp.where(odd, third, jnp.where(place == 0, first, second))
-    after = jnp.where(odd, jnp.where(place == 1, first, second), third)
-    joined = jnp.concatenate([earlier, before, own[...], after], axis=1)
+def prepare(at_block, left, right, x8, end_m, end_v, work):
+    x2, ma, mb, va, vb = work
+    rows = left.shape[1]
+    span = rows + HALF
+    first = at_block * rows
+    joined = jnp.concatenate([left, right], axis=1)
     both = jnp.concatenate([joined[:, :span], joined[:, HALF : HALF + span]], axis=0)
     for at in range(0, span, LANES):
         x2[at : at + LANES, :] = both[:, at : at + LANES].T
-
     src_m, src_v, _ = window_sums(x2, [(ma, va), (mb, vb)], span)
-    for at in range(0, total, LANES):
+    for at in range(0, rows, LANES):
         m0 = src_m[at : at + LANES, :]
         v0 = src_v[at : at + LANES, :]
         m1 = pltpu.roll(m0, LANES // 2, 1)
         v1 = pltpu.roll(v0, LANES // 2, 1)
         gap = m0 - m1
         var = (v0 + v1 + gap * gap * (0.5 * HALF)) * (1.0 / WIN)
-        end_m[at : at + LANES, :] = (m0 + m1) * 0.5
-        end_v[at : at + LANES, :] = lax.rsqrt(var + EPS)
-
+        end_m[first + at : first + at + LANES, :] = (m0 + m1) * 0.5
+        end_v[first + at : first + at + LANES, :] = lax.rsqrt(var + EPS)
+    held = span if at_block == STEPS else rows
     for s in range(ALIGN):
-        for at in range(0, span, LANES):
-            x8[s, at : at + LANES, :] = x2[at + s : at + s + LANES, :]
+        for at in range(0, held, LANES):
+            x8[s, first + at : first + at + LANES, :] = x2[at + s : at + s + LANES, :]
+
+
+def neighbours(place, from_first, from_second, from_third):
+    second = from_first if from_second is None else from_second
+    earlier = jnp.where(place < 2, second, from_first)
+    odd = lax.rem(place, 2) == 1
+    before = jnp.where(odd, from_third, jnp.where(place == 0, from_first, second))
+    after = jnp.where(odd, jnp.where(place == 1, from_first, second), from_third)
+    return earlier, before, after
+
+
+def early_kernel(own, from_first, from_third, x8, end_m, end_v, *work):
+    place = lax.rem(lax.axis_index("tm"), LINE)
+
+    @pl.when(place < 2)
+    def _():
+        _, before, after = neighbours(place, from_first[...], None, from_third[...])
+        prepare(1, before, own[...], x8, end_m, end_v, work)
+        prepare(2, own[...], after, x8, end_m, end_v, work)
+
+
+def far_kernel(own, from_first, from_third, from_second, _x8, _m, _v, out, x8, end_m, end_v, zr, *work):
+    place = lax.rem(lax.axis_index("tm"), LINE)
+    earlier, before, after = neighbours(place, from_first[...], from_second[...], from_third[...])
+    prepare(0, earlier, before, x8, end_m, end_v, work)
+
+    @pl.when(place >= 2)
+    def _():
+        prepare(1, before, own[...], x8, end_m, end_v, work)
+        prepare(2, own[...], after, x8, end_m, end_v, work)
 
     base = (1 - lax.axis_index("chan") // 2) * out.shape[0]
     contract(base, x8, end_m, end_v, zr, out, True)
@@ -208,20 +238,31 @@
     bf16 = jnp.bfloat16
     room = total + HALF + HALF
     tall = jax.ShapeDtypeStruct((room, LANES), f32)
+    shifted = jax.ShapeDtypeStruct((ALIGN, room, LANES), f32)
+    work = [pltpu.VMEM((rows + 2 * HALF, LANES), f32)] * 5
+    early = pl.pallas_call(
+        early_kernel,
+        out_shape=[shifted, tall, tall],
+        in_specs=[vmem] * 3,
+        out_specs=[vmem] * 3,
+        scratch_shapes=work,
+        compiler_params=pltpu.CompilerParams(vmem_limit_bytes=SMALL_LIMIT),
+    )(own, from_first, from_third)
     far, *shared = pl.pallas_call(
-        functools.partial(far_kernel, rows),
+        far_kernel,
         out_shape=[
             jax.ShapeDtypeStruct((side, rows), bf16),
-            jax.ShapeDtypeStruct((ALIGN, room, LANES), f32),
+            shifted,
             tall,
             tall,
             jax.ShapeDtypeStruct((HALF // STEP_K, UNITS, rows, 2 * LANES), bf16),
         ],
-        in_specs=[vmem] * 4,
+        in_specs=[vmem] * 7,
         out_specs=[vmem] * 5,
-        scratch_shapes=[pltpu.VMEM((room, LANES), f32)] * 5,
-        compiler_params=pltpu.CompilerParams(vmem_limit_bytes=VMEM_LIMIT),
-    )(own, from_first, from_third, from_second)
+        input_output_aliases={4: 1, 5: 2, 6: 3},
+        scratch_shapes=work,
+        compiler_params=pltpu.CompilerParams(vmem_limit_bytes=SMALL_LIMIT),
+    )(own, from_first, from_third, from_second, *early)
     far_got = sent(far, "chan", across(2))
     near = pl.pallas_call(
         near_kernel,

time: 33.4 us -> 32.3 us (0.967)
  starting transfers between devices: 12.1 us -> 8.23 us
  waiting for transfers between devices: 8.66 us -> 10.9 us
  Pallas kernels: 11 us -> 11.5 us
    ppermute x7, starting transfers between devices: 12.1 us -> 8.23 us  [sent(): lax.ppermute(block, axis, [(i, target(i, count)) for i in range(count)])]
    ppermute x7, waiting for transfers between devices: 8.66 us -> 10.9 us  [sent(): lax.ppermute(block, axis, [(i, target(i, count)) for i in range(count)])]
    pallas_call x1 -> x2, Pallas kernels: 6.33 us -> 6.88 us  [the longest x1 5.53 us: body(): pl.pallas_call(far_kernel, out_shape=[jax.ShapeDtypeStruct((side, rows),...]
  transfers between devices with their start and end apart: 7 -> 7, of which waited for: 5 -> 5; matrix products, arithmetic and copies ran while one was open for 3% -> 3% of each run, Pallas kernels for 11% -> 16%
where the time goes in v8:
time: 32.3 us; the launch traced here: 32.2 us
  Pallas kernels  11.5 us (36%)
  waiting for transfers between devices  10.9 us (34%)
  starting transfers between devices  8.23 us (25%)
  other arithmetic  1.45 us (4%)
    ppermute x7, waiting for transfers between devices, sent(): lax.ppermute(block, axis, [(i, target(i, count)) for i in range(count)])  10.9 us
    ppermute x7, starting transfers between devices, sent(): lax.ppermute(block, axis, [(i, target(i, count)) for i in range(count)])  8.23 us
    pallas_call x1, Pallas kernels, body(): pl.pallas_call(far_kernel, out_shape=[jax.ShapeDtypeStruct((side, rows),...  5.53 us
    pallas_call x1, Pallas kernels, body(): pl.pallas_call(near_kernel, out_shape=jax.ShapeDtypeStruct((side, rows),...  3.81 us
    pallas_call x1, Pallas kernels, body(): pl.pallas_call(early_kernel, out_shape=[shifted, tall, tall], in_specs=[v...  1.35 us
    max x1, other arithmetic, body(): own = jnp.maximum(series, jnp.finfo(series.dtype).min)  0.88 us
    pallas_call x1, Pallas kernels, body(): pl.pallas_call(functools.partial(peak_kernel, rows), out_shape=jax.ShapeD...  0.83 us
  transfers between devices with their start and end apart: 7, of which 5 were waited for; matrix products, arithmetic and copies ran while one was open for 3% of the time, Pallas kernels for 16%

profile of v8, /device:TPU:0, one launch (start us, length us, event | category | flops | bytes accessed | tf_op | source)
XLA Modules:
  0.0 32.2 jit_solution(11514060663316245294)
XLA Ops:
  0.0 4.0 %collective-permute-start = (f32[64,256]{1,0:T(8,128)}, f32[64,256]{1,0:T(8,128)S(1)}, u32[]{:S(2)}, u32[]{:S(2)}) collective-permute-start(f32[64,256]{1,0:T(8,128)} %param.2), channel_id=1, source_target_pairs={{0,8},{4,12},{8,4},{12,16},{16,24},{20,28},{24,20},{28,32},{32,40}... | collective-permute-start | bytes 196616 | tf_op jit(solution)/shard_map/ppermute | solution.py:26
  4.0 1.0 %collective-permute-start.2 = (f32[64,256]{1,0:T(8,128)}, f32[64,256]{1,0:T(8,128)S(1)}, u32[]{:S(2)}, u32[]{:S(2)}) collective-permute-start(f32[64,256]{1,0:T(8,128)} %param.2), channel_id=1, source_target_pairs={{0,4},{4,8},{8,16},{12,20},{16,12},{20,24},{24,32},{28,36},{32,28}... | collective-permute-start | bytes 196616 | tf_op jit(solution)/shard_map/ppermute | solution.py:26
  5.0 0.0 collective-permute-start.1
  5.0 0.9 %broadcast_maximum_fusion.own = f32[64,256]{1,0:T(8,128)S(1)} fusion(f32[64,256]{1,0:T(8,128)} %param.2), kind=kLoop, calls=%fused_computation | loop fusion | flops 16384 | bytes 131072 | tf_op jit(solution)/shard_map/max | solution.py:231
  5.9 5.6 %collective-permute-done.from_first = f32[64,256]{1,0:T(8,128)S(1)} collective-permute-done((f32[64,256]{1,0:T(8,128)}, f32[64,256]{1,0:T(8,128)S(1)}, u32[]{:S(2)}, u32[]{:S(2)}) %collective-permute-start) | collective-permute-done | bytes 65568 | tf_op jit(solution)/shard_map/ppermute | solution.py:26
  11.5 0.0 collective-permute-done.1.from_third
  11.5 1.4 %shard_map.28 = (f32[8,1024,128]{2,1,0:T(8,128)S(1)}, f32[1024,128]{1,0:T(8,128)S(1)}, f32[1024,128]{1,0:T(8,128)S(1)}) custom-call(f32[64,256]{1,0:T(8,128)S(1)} %broadcast_maximum_fusion.own, f32[64,256]{1,0:T(8,128)S(1)} %collective-permute-done.from_first, f32[64,256]{1,0:T(8,128)S(1)} %collective-permute-done.1.from_third), custom_call_target="tpu_custom_call" | custom-call | tf_op jit(solution)/shard_map/pallas_call | solution.py:243
  12.9 1.3 %collective-permute-done.2.from_second = f32[64,256]{1,0:T(8,128)S(1)} collective-permute-done((f32[64,256]{1,0:T(8,128)}, f32[64,256]{1,0:T(8,128)S(1)}, u32[]{:S(2)}, u32[]{:S(2)}) %collective-permute-start.2) | collective-permute-done | bytes 65568 | tf_op jit(solution)/shard_map/ppermute | solution.py:26
  14.2 5.5 %shard_map.29 = (bf16[352,256]{1,0:T(8,128)(2,1)S(1)}, f32[8,1024,128]{2,1,0:T(8,128)S(1)}, f32[1024,128]{1,0:T(8,128)S(1)}, f32[1024,128]{1,0:T(8,128)S(1)}, bf16[32,2,256,256]{3,2,1,0:T(8,128)(2,1)S(1)}) custom-call(f32[64,256]{1,0:T(8,128)S(1)} %broadcast_maximum_fusion.own, ...), custom_call_target="tpu_custom_call", output_to_operand_aliasing={{1}: (4, {}), {2}: (5, {}), {3}: (6, {})} | custom-call | tf_op jit(solution)/shard_map/pallas_call | solution.py:251
  19.7 1.6 %collective-permute-start.4 = (bf16[352,256]{1,0:T(8,128)(2,1)S(1)}, bf16[352,256]{1,0:T(8,128)(2,1)S(1)}, u32[]{:S(2)}, u32[]{:S(2)}) collective-permute-start(bf16[352,256]{1,0:T(8,128)(2,1)S(1)} %get-tuple-element.20), channel_id=1, source_target_pairs={{0,2},{1,3},{2,0},{3,1},{4,6},{5,7},{6,4},{7,5},{8,10},{9,11},{10,... | collective-permute-start | bytes 540680 | tf_op jit(solution)/shard_map/ppermute | solution.py:26
  21.3 0.0 copy-start
  21.3 3.8 %shard_map.30.p0 = f32[352,256]{1,0:T(8,128)S(1)} custom-call(f32[8,1024,128]{2,1,0:T(8,128)S(1)} %get-tuple-element.16.x8, f32[1024,128]{1,0:T(8,128)S(1)} %get-tuple-element.17.end_m, f32[1024,128]{1,0:T(8,128)S(1)} %get-tuple-element.18.end_v, bf16[32,2,256,256]{3,2,1,0:T(8,128)(2,1)S(1)} %get-tuple-element.19.zr), custom_call_target="tpu_custom_call" | custom-call | tf_op jit(solution)/shard_map/pallas_call | solution.py:267
  25.1 0.1 collective-permute-start.3
  25.2 0.1 collective-permute-done.4.p2
  25.3 0.4 %collective-permute-start.5 = (bf16[352,256]{1,0:T(8,128)(2,1)S(1)}, bf16[352,256]{1,0:T(8,128)(2,1)S(1)}, u32[]{:S(2)}, u32[]{:S(2)}) collective-permute-start(bf16[352,256]{1,0:T(8,128)(2,1)S(1)} %collective-permute-done.4.p2), channel_id=1, source_target_pairs={{0,1},{1,0},{2,3},{3,2},{4,5},{5,4},{6,7},{7,6},{8,9},{9,8},{10,11... | collective-permute-start | bytes 540680 | tf_op jit(solution)/shard_map/ppermute | solution.py:26
  25.7 1.4 %collective-permute-done.5.p3 = bf16[352,256]{1,0:T(8,128)(2,1)S(1)} collective-permute-done((bf16[352,256]{1,0:T(8,128)(2,1)S(1)}, bf16[352,256]{1,0:T(8,128)(2,1)S(1)}, u32[]{:S(2)}, u32[]{:S(2)}) %collective-permute-start.5) | collective-permute-done | bytes 180256 | tf_op jit(solution)/shard_map/ppermute | solution.py:26
  27.1 0.0 collective-permute-done.3.p1
  27.1 0.0 copy-done
  27.1 0.8 %shard_map.31 = f32[1,256]{1,0:T(1,128)S(1)} custom-call(s32[64]{0:T(128)S(1)} %copy-done, f32[352,256]{1,0:T(8,128)S(1)} %shard_map.30.p0, f32[352,256]{1,0:T(8,128)S(1)} %collective-permute-done.3.p1, bf16[352,256]{1,0:T(8,128)(2,1)S(1)} %collective-permute-done.4.p2, bf16[352,256]{1,0:T(8,128)(2,1)S(1)} %collective-permute-done.5.p3), custom_call_target="tpu_custom_call" | custom-call | tf_op jit(solution)/shard_map/pallas_call | solution.py:276
  27.9 1.2 %collective-permute-start.6 = (f32[1,256]{1,0:T(1,128)S(1)}, f32[1,256]{1,0:T(1,128)S(1)}, u32[]{:S(2)}, u32[]{:S(2)}) collective-permute-start(f32[1,256]{1,0:T(1,128)S(1)} %shard_map.31), channel_id=1, source_target_pairs={{0,2},{1,3},{2,0},{3,1},{4,6},{5,7},{6,4},{7,5},{8,10},{9,11},{10,... | collective-permute-start | bytes 3080 | tf_op jit(solution)/shard_map/ppermute | solution.py:26
  29.1 2.5 %collective-permute-done.6 = f32[1,256]{1,0:T(1,128)S(1)} collective-permute-done((f32[1,256]{1,0:T(1,128)S(1)}, f32[1,256]{1,0:T(1,128)S(1)}, u32[]{:S(2)}, u32[]{:S(2)}) %collective-permute-start.6) | collective-permute-done | bytes 1056 | tf_op jit(solution)/shard_map/ppermute | solution.py:26
  31.6 0.6 %compare_select_fusion = f32[1,256]{1,0:T(1,128)} fusion(f32[1,256]{1,0:T(1,128)S(1)} %shard_map.31, f32[1,256]{1,0:T(1,128)S(1)} %collective-permute-done.6), kind=kLoop, calls=%fused_computation.1 | loop fusion | flops 768 | bytes 3072 | tf_op jit(solution)/shard_map/jit(_where)/select_n | solution.py:284
Async XLA Ops:
  0.0 11.5 %collective-permute-start = (f32[64,256]{1,0:T(8,128)}, f32[64,256]{1,0:T(8,128)S(1)}, u32[]{:S(2)}, u32[]{:S(2)}) collective-permute-start(f32[64,256]{1,0:T(8,128)} %param.2), channel_id=1, source_target_pairs={{0,8},{4,12},{8,4},{12,16},{16,24},{20,28},{24,20},{28,32},{32,40}... | collective-permute-start | bytes 196616 | tf_op jit(solution)/shard_map/ppermute | solution.py:26
  4.0 10.2 %collective-permute-start.2 = (f32[64,256]{1,0:T(8,128)}, f32[64,256]{1,0:T(8,128)S(1)}, u32[]{:S(2)}, u32[]{:S(2)}) collective-permute-start(f32[64,256]{1,0:T(8,128)} %param.2), channel_id=1, source_target_pairs={{0,4},{4,8},{8,16},{12,20},{16,12},{20,24},{24,32},{28,36},{32,28}... | collective-permute-start | bytes 196616 | tf_op jit(solution)/shard_map/ppermute | solution.py:26
  5.0 6.5 %collective-permute-start.1 = (f32[64,256]{1,0:T(8,128)}, f32[64,256]{1,0:T(8,128)S(1)}, u32[]{:S(2)}, u32[]{:S(2)}) collective-permute-start(f32[64,256]{1,0:T(8,128)} %param.2), channel_id=1, source_target_pairs={{0,4},{4,0},{8,12},{12,8},{16,20},{20,16},{24,28},{28,24},{32,36},... | collective-permute-start | bytes 196616 | tf_op jit(solution)/shard_map/ppermute | solution.py:26
  19.7 5.6 %collective-permute-start.4 = (bf16[352,256]{1,0:T(8,128)(2,1)S(1)}, bf16[352,256]{1,0:T(8,128)(2,1)S(1)}, u32[]{:S(2)}, u32[]{:S(2)}) collective-permute-start(bf16[352,256]{1,0:T(8,128)(2,1)S(1)} %get-tuple-element.20), channel_id=1, source_target_pairs={{0,2},{1,3},{2,0},{3,1},{4,6},{5,7},{6,4},{7,5},{8,10},{9,11},{10,... | collective-permute-start | bytes 540680 | tf_op jit(solution)/shard_map/ppermute | solution.py:26
  21.3 5.8 %copy-start = (s32[64]{0:T(128)S(1)}, s32[64]{0:T(128)}, u32[]{:S(2)}) copy-start(s32[64]{0:T(128)} %lens.1) | copy-start | bytes 772
  25.1 2.0 %collective-permute-start.3 = (f32[352,256]{1,0:T(8,128)S(1)}, f32[352,256]{1,0:T(8,128)S(1)}, u32[]{:S(2)}, u32[]{:S(2)}) collective-permute-start(f32[352,256]{1,0:T(8,128)S(1)} %shard_map.30.p0), channel_id=1, source_target_pairs={{0,1},{1,0},{2,3},{3,2},{4,5},{5,4},{6,7},{7,6},{8,9},{9,8},{10,11... | collective-permute-start | bytes 1081352 | tf_op jit(solution)/shard_map/ppermute | solution.py:26
  25.3 1.8 %collective-permute-start.5 = (bf16[352,256]{1,0:T(8,128)(2,1)S(1)}, bf16[352,256]{1,0:T(8,128)(2,1)S(1)}, u32[]{:S(2)}, u32[]{:S(2)}) collective-permute-start(bf16[352,256]{1,0:T(8,128)(2,1)S(1)} %collective-permute-done.4.p2), channel_id=1, source_target_pairs={{0,1},{1,0},{2,3},{3,2},{4,5},{5,4},{6,7},{7,6},{8,9},{9,8},{10,11... | collective-permute-start | bytes 540680 | tf_op jit(solution)/shard_map/ppermute | solution.py:26
  27.9 3.6 %collective-permute-start.6 = (f32[1,256]{1,0:T(1,128)S(1)}, f32[1,256]{1,0:T(1,128)S(1)}, u32[]{:S(2)}, u32[]{:S(2)}) collective-permute-start(f32[1,256]{1,0:T(1,128)S(1)} %shard_map.31), channel_id=1, source_target_pairs={{0,2},{1,3},{2,0},{3,1},{4,6},{5,7},{6,4},{7,5},{8,10},{9,11},{10,... | collective-permute-start | bytes 3080 | tf_op jit(solution)/shard_map/ppermute | solution.py:26

commit v9 on v8

--- a/solution.py
+++ b/solution.py
@@ -34,13 +34,11 @@
 
 
 def second_step(i, count):
-    if i == 0:
-        return 1
+    if i < LINE:
+        return (1, 2, LINE, 0)[i]
     if i == count - 2:
         return count - 1
-    if i == count - 1:
-        return 0
-    return i + (-1, 1, 2, 2)[i % LINE]
+    return i + (-1, 1, 2, -2)[i % LINE]
 
 
 def third_step(i, count):
@@ -157,9 +155,10 @@
             x8[s, first + at : first + at + LANES, :] = x2[at + s : at + s + LANES, :]
 
 
-def neighbours(place, from_first, from_second, from_third):
+def neighbours(place, from_first, from_third, from_second=None, handed_on=None):
     second = from_first if from_second is None else from_second
-    earlier = jnp.where(place < 2, second, from_first)
+    handed_on = from_first if handed_on is None else handed_on
+    earlier = jnp.where(place == 0, second, jnp.where(place == 1, handed_on, from_first))
     odd = lax.rem(place, 2) == 1
     before = jnp.where(odd, from_third, jnp.where(place == 0, from_first, second))
     after = jnp.where(odd, jnp.where(place == 1, from_first, second), from_third)
@@ -171,14 +170,14 @@
 
     @pl.when(place < 2)
     def _():
-        _, before, after = neighbours(place, from_first[...], None, from_third[...])
+        _, before, after = neighbours(place, from_first[...], from_third[...])
         prepare(1, before, own[...], x8, end_m, end_v, work)
         prepare(2, own[...], after, x8, end_m, end_v, work)
 
 
-def far_kernel(own, from_first, from_third, from_second, _x8, _m, _v, out, x8, end_m, end_v, zr, *work):
+def far_kernel(own, from_first, from_third, from_second, handed_on, _x8, _m, _v, out, x8, end_m, end_v, zr, *work):
     place = lax.rem(lax.axis_index("tm"), LINE)
-    earlier, before, after = neighbours(place, from_first[...], from_second[...], from_third[...])
+    earlier, before, after = neighbours(place, from_first[...], from_third[...], from_second[...], handed_on[...])
     prepare(0, earlier, before, x8, end_m, end_v, work)
 
     @pl.when(place >= 2)
@@ -232,6 +231,7 @@
     from_first = sent(series, "tm", first_step)
     from_second = sent(series, "tm", second_step)
     from_third = sent(series, "tm", third_step)
+    handed_on = sent(from_first, "tm", third_step)
     vmem = pl.BlockSpec(memory_space=pltpu.VMEM)
     smem = pl.BlockSpec(memory_space=pltpu.SMEM)
     f32 = jnp.float32
@@ -257,12 +257,12 @@
             tall,
             jax.ShapeDtypeStruct((HALF // STEP_K, UNITS, rows, 2 * LANES), bf16),
         ],
-        in_specs=[vmem] * 7,
+        in_specs=[vmem] * 8,
         out_specs=[vmem] * 5,
-        input_output_aliases={4: 1, 5: 2, 6: 3},
+        input_output_aliases={5: 1, 6: 2, 7: 3},
         scratch_shapes=work,
         compiler_params=pltpu.CompilerParams(vmem_limit_bytes=SMALL_LIMIT),
-    )(own, from_first, from_third, from_second, *early)
+    )(own, from_first, from_third, from_second, handed_on, *early)
     far_got = sent(far, "chan", across(2))
     near = pl.pallas_call(
         near_kernel,

time: 32.3 us -> 33.5 us (1.037)
  waiting for transfers between devices: 10.9 us -> 13.5 us
  starting transfers between devices: 8.23 us -> 6.86 us
    ppermute x7 -> x8, waiting for transfers between devices: 10.9 us -> 13.5 us  [sent(): lax.ppermute(block, axis, [(i, target(i, count)) for i in range(count)])]
    ppermute x7 -> x8, starting transfers between devices: 8.23 us -> 6.86 us  [sent(): lax.ppermute(block, axis, [(i, target(i, count)) for i in range(count)])]
  transfers between devices with their start and end apart: 7 -> 8, of which waited for: 5 -> 5; matrix products, arithmetic and copies ran while one was open for 3% -> 3% of each run, Pallas kernels for 16% -> 16%
where the time goes in v9:
time: 33.5 us; the launch traced here: 33.3 us
  waiting for transfers between devices  13.5 us (40%)
  Pallas kernels  11.5 us (34%)
  starting transfers between devices  6.86 us (20%)
  other arithmetic  1.41 us (4%)
    ppermute x8, waiting for transfers between devices, sent(): lax.ppermute(block, axis, [(i, target(i, count)) for i in range(count)])  13.5 us
    ppermute x8, starting transfers between devices, sent(): lax.ppermute(block, axis, [(i, target(i, count)) for i in range(count)])  6.86 us
    pallas_call x1, Pallas kernels, body(): pl.pallas_call(far_kernel, out_shape=[jax.ShapeDtypeStruct((side, rows),...  5.53 us
    pallas_call x1, Pallas kernels, body(): pl.pallas_call(near_kernel, out_shape=jax.ShapeDtypeStruct((side, rows),...  3.81 us
    pallas_call x1, Pallas kernels, body(): pl.pallas_call(early_kernel, out_shape=[shifted, tall, tall], in_specs=[v...  1.37 us
    max x1, other arithmetic, body(): own = jnp.maximum(series, jnp.finfo(series.dtype).min)  0.85 us
    pallas_call x1, Pallas kernels, body(): pl.pallas_call(functools.partial(peak_kernel, rows), out_shape=jax.ShapeD...  0.83 us
  transfers between devices with their start and end apart: 8, of which 5 were waited for; matrix products, arithmetic and copies ran while one was open for 3% of the time, Pallas kernels for 16%

profile of v9, /device:TPU:0, one launch (start us, length us, event | category | flops | bytes accessed | tf_op | source)
XLA Modules:
  0.0 33.3 jit_solution(1101607570420610188)
XLA Ops:
  0.0 4.0 %collective-permute-start = (f32[64,256]{1,0:T(8,128)}, f32[64,256]{1,0:T(8,128)S(1)}, u32[]{:S(2)}, u32[]{:S(2)}) collective-permute-start(f32[64,256]{1,0:T(8,128)} %param.2), channel_id=1, source_target_pairs={{0,8},{4,12},{8,4},{12,16},{16,24},{20,28},{24,20},{28,32},{32,40}... | collective-permute-start | bytes 196616 | tf_op jit(solution)/shard_map/ppermute | solution.py:26
  4.0 1.0 %collective-permute-start.2 = (f32[64,256]{1,0:T(8,128)}, f32[64,256]{1,0:T(8,128)S(1)}, u32[]{:S(2)}, u32[]{:S(2)}) collective-permute-start(f32[64,256]{1,0:T(8,128)} %param.2), channel_id=1, source_target_pairs={{0,4},{4,8},{8,16},{12,0},{16,12},{20,24},{24,32},{28,20},{32,28},... | collective-permute-start | bytes 196616 | tf_op jit(solution)/shard_map/ppermute | solution.py:26
  5.0 0.0 collective-permute-start.1
  5.0 6.5 %collective-permute-done.from_first = f32[64,256]{1,0:T(8,128)S(1)} collective-permute-done((f32[64,256]{1,0:T(8,128)}, f32[64,256]{1,0:T(8,128)S(1)}, u32[]{:S(2)}, u32[]{:S(2)}) %collective-permute-start) | collective-permute-done | bytes 65568 | tf_op jit(solution)/shard_map/ppermute | solution.py:26
  11.5 0.0 collective-permute-start.3
  11.5 0.8 %broadcast_maximum_fusion.own = f32[64,256]{1,0:T(8,128)S(1)} fusion(f32[64,256]{1,0:T(8,128)} %param.2), kind=kLoop, calls=%fused_computation | loop fusion | flops 16384 | bytes 131072 | tf_op jit(solution)/shard_map/max | solution.py:230
  12.3 0.0 collective-permute-done.1.from_third
  12.3 1.4 %shard_map.28 = (f32[8,1024,128]{2,1,0:T(8,128)S(1)}, f32[1024,128]{1,0:T(8,128)S(1)}, f32[1024,128]{1,0:T(8,128)S(1)}) custom-call(f32[64,256]{1,0:T(8,128)S(1)} %broadcast_maximum_fusion.own, f32[64,256]{1,0:T(8,128)S(1)} %collective-permute-done.from_first, f32[64,256]{1,0:T(8,128)S(1)} %collective-permute-done.1.from_third), custom_call_target="tpu_custom_call" | custom-call | tf_op jit(solution)/shard_map/pallas_call | solution.py:243
  13.7 0.0 collective-permute-done.2.from_second
  13.7 2.0 %collective-permute-done.3.handed_on = f32[64,256]{1,0:T(8,128)S(1)} collective-permute-done((f32[64,256]{1,0:T(8,128)S(1)}, f32[64,256]{1,0:T(8,128)S(1)}, u32[]{:S(2)}, u32[]{:S(2)}) %collective-permute-start.3) | collective-permute-done | bytes 65568 | tf_op jit(solution)/shard_map/ppermute | solution.py:26
  15.8 5.5 %shard_map.29 = (bf16[352,256]{1,0:T(8,128)(2,1)S(1)}, f32[8,1024,128]{2,1,0:T(8,128)S(1)}, f32[1024,128]{1,0:T(8,128)S(1)}, f32[1024,128]{1,0:T(8,128)S(1)}, bf16[32,2,256,256]{3,2,1,0:T(8,128)(2,1)S(1)}) custom-call(f32[64,256]{1,0:T(8,128)S(1)} %broadcast_maximum_fusion.own, ...), custom_call_target="tpu_custom_call", output_to_operand_aliasing={{1}: (5, {}), {2}: (6, {}), {3}: (7, {})} | custom-call | tf_op jit(solution)/shard_map/pallas_call | solution.py:251
  21.3 0.7 %collective-permute-start.5 = (bf16[352,256]{1,0:T(8,128)(2,1)S(1)}, bf16[352,256]{1,0:T(8,128)(2,1)S(1)}, u32[]{:S(2)}, u32[]{:S(2)}) collective-permute-start(bf16[352,256]{1,0:T(8,128)(2,1)S(1)} %get-tuple-element.20), channel_id=1, source_target_pairs={{0,2},{1,3},{2,0},{3,1},{4,6},{5,7},{6,4},{7,5},{8,10},{9,11},{10,... | collective-permute-start | bytes 540680 | tf_op jit(solution)/shard_map/ppermute | solution.py:26
  22.0 0.0 copy-start
  22.0 3.8 %shard_map.30.p0 = f32[352,256]{1,0:T(8,128)S(1)} custom-call(f32[8,1024,128]{2,1,0:T(8,128)S(1)} %get-tuple-element.16.x8, f32[1024,128]{1,0:T(8,128)S(1)} %get-tuple-element.17.end_m, f32[1024,128]{1,0:T(8,128)S(1)} %get-tuple-element.18.end_v, bf16[32,2,256,256]{3,2,1,0:T(8,128)(2,1)S(1)} %get-tuple-element.19.zr), custom_call_target="tpu_custom_call" | custom-call | tf_op jit(solution)/shard_map/pallas_call | solution.py:267
  25.8 0.1 collective-permute-start.4
  25.9 0.9 %collective-permute-done.5.p2 = bf16[352,256]{1,0:T(8,128)(2,1)S(1)} collective-permute-done((bf16[352,256]{1,0:T(8,128)(2,1)S(1)}, bf16[352,256]{1,0:T(8,128)(2,1)S(1)}, u32[]{:S(2)}, u32[]{:S(2)}) %collective-permute-start.5) | collective-permute-done | bytes 180256 | tf_op jit(solution)/shard_map/ppermute | solution.py:26
  26.9 0.0 collective-permute-start.6
  26.9 1.4 %collective-permute-done.6.p3 = bf16[352,256]{1,0:T(8,128)(2,1)S(1)} collective-permute-done((bf16[352,256]{1,0:T(8,128)(2,1)S(1)}, bf16[352,256]{1,0:T(8,128)(2,1)S(1)}, u32[]{:S(2)}, u32[]{:S(2)}) %collective-permute-start.6) | collective-permute-done | bytes 180256 | tf_op jit(solution)/shard_map/ppermute | solution.py:26
  28.3 0.0 collective-permute-done.4.p1
  28.3 0.0 copy-done
  28.3 0.8 %shard_map.31 = f32[1,256]{1,0:T(1,128)S(1)} custom-call(s32[64]{0:T(128)S(1)} %copy-done, f32[352,256]{1,0:T(8,128)S(1)} %shard_map.30.p0, f32[352,256]{1,0:T(8,128)S(1)} %collective-permute-done.4.p1, bf16[352,256]{1,0:T(8,128)(2,1)S(1)} %collective-permute-done.5.p2, bf16[352,256]{1,0:T(8,128)(2,1)S(1)} %collective-permute-done.6.p3), custom_call_target="tpu_custom_call" | custom-call | tf_op jit(solution)/shard_map/pallas_call | solution.py:276
  29.1 1.0 %collective-permute-start.7 = (f32[1,256]{1,0:T(1,128)S(1)}, f32[1,256]{1,0:T(1,128)S(1)}, u32[]{:S(2)}, u32[]{:S(2)}) collective-permute-start(f32[1,256]{1,0:T(1,128)S(1)} %shard_map.31), channel_id=1, source_target_pairs={{0,2},{1,3},{2,0},{3,1},{4,6},{5,7},{6,4},{7,5},{8,10},{9,11},{10,... | collective-permute-start | bytes 3080 | tf_op jit(solution)/shard_map/ppermute | solution.py:26
  30.1 2.6 %collective-permute-done.7 = f32[1,256]{1,0:T(1,128)S(1)} collective-permute-done((f32[1,256]{1,0:T(1,128)S(1)}, f32[1,256]{1,0:T(1,128)S(1)}, u32[]{:S(2)}, u32[]{:S(2)}) %collective-permute-start.7) | collective-permute-done | bytes 1056 | tf_op jit(solution)/shard_map/ppermute | solution.py:26
  32.8 0.6 %compare_select_fusion = f32[1,256]{1,0:T(1,128)} fusion(f32[1,256]{1,0:T(1,128)S(1)} %shard_map.31, f32[1,256]{1,0:T(1,128)S(1)} %collective-permute-done.7), kind=kLoop, calls=%fused_computation.1 | loop fusion | flops 768 | bytes 3072 | tf_op jit(solution)/shard_map/jit(_where)/select_n | solution.py:284
Async XLA Ops:
  0.0 11.5 %collective-permute-start = (f32[64,256]{1,0:T(8,128)}, f32[64,256]{1,0:T(8,128)S(1)}, u32[]{:S(2)}, u32[]{:S(2)}) collective-permute-start(f32[64,256]{1,0:T(8,128)} %param.2), channel_id=1, source_target_pairs={{0,8},{4,12},{8,4},{12,16},{16,24},{20,28},{24,20},{28,32},{32,40}... | collective-permute-start | bytes 196616 | tf_op jit(solution)/shard_map/ppermute | solution.py:26
  4.0 9.8 %collective-permute-start.2 = (f32[64,256]{1,0:T(8,128)}, f32[64,256]{1,0:T(8,128)S(1)}, u32[]{:S(2)}, u32[]{:S(2)}) collective-permute-start(f32[64,256]{1,0:T(8,128)} %param.2), channel_id=1, source_target_pairs={{0,4},{4,8},{8,16},{12,0},{16,12},{20,24},{24,32},{28,20},{32,28},... | collective-permute-start | bytes 196616 | tf_op jit(solution)/shard_map/ppermute | solution.py:26
  5.0 7.4 %collective-permute-start.1 = (f32[64,256]{1,0:T(8,128)}, f32[64,256]{1,0:T(8,128)S(1)}, u32[]{:S(2)}, u32[]{:S(2)}) collective-permute-start(f32[64,256]{1,0:T(8,128)} %param.2), channel_id=1, source_target_pairs={{0,4},{4,0},{8,12},{12,8},{16,20},{20,16},{24,28},{28,24},{32,36},... | collective-permute-start | bytes 196616 | tf_op jit(solution)/shard_map/ppermute | solution.py:26
  11.5 4.3 %collective-permute-start.3 = (f32[64,256]{1,0:T(8,128)S(1)}, f32[64,256]{1,0:T(8,128)S(1)}, u32[]{:S(2)}, u32[]{:S(2)}) collective-permute-start(f32[64,256]{1,0:T(8,128)S(1)} %collective-permute-done.from_first), channel_id=1, source_target_pairs={{0,4},{4,0},{8,12},{12,8},{16,20},{20,16},{24,28},{28,24},{32,36},... | collective-permute-start | bytes 196616 | tf_op jit(solution)/shard_map/ppermute | solution.py:26
  21.3 5.6 %collective-permute-start.5 = (bf16[352,256]{1,0:T(8,128)(2,1)S(1)}, bf16[352,256]{1,0:T(8,128)(2,1)S(1)}, u32[]{:S(2)}, u32[]{:S(2)}) collective-permute-start(bf16[352,256]{1,0:T(8,128)(2,1)S(1)} %get-tuple-element.20), channel_id=1, source_target_pairs={{0,2},{1,3},{2,0},{3,1},{4,6},{5,7},{6,4},{7,5},{8,10},{9,11},{10,... | collective-permute-start | bytes 540680 | tf_op jit(solution)/shard_map/ppermute | solution.py:26
  22.0 6.3 %copy-start = (s32[64]{0:T(128)S(1)}, s32[64]{0:T(128)}, u32[]{:S(2)}) copy-start(s32[64]{0:T(128)} %lens.1) | copy-start | bytes 772
  25.8 2.4 %collective-permute-start.4 = (f32[352,256]{1,0:T(8,128)S(1)}, f32[352,256]{1,0:T(8,128)S(1)}, u32[]{:S(2)}, u32[]{:S(2)}) collective-permute-start(f32[352,256]{1,0:T(8,128)S(1)} %shard_map.30.p0), channel_id=1, source_target_pairs={{0,1},{1,0},{2,3},{3,2},{4,5},{5,4},{6,7},{7,6},{8,9},{9,8},{10,11... | collective-permute-start | bytes 1081352 | tf_op jit(solution)/shard_map/ppermute | solution.py:26
  26.9 1.4 %collective-permute-start.6 = (bf16[352,256]{1,0:T(8,128)(2,1)S(1)}, bf16[352,256]{1,0:T(8,128)(2,1)S(1)}, u32[]{:S(2)}, u32[]{:S(2)}) collective-permute-start(bf16[352,256]{1,0:T(8,128)(2,1)S(1)} %collective-permute-done.5.p2), channel_id=1, source_target_pairs={{0,1},{1,0},{2,3},{3,2},{4,5},{5,4},{6,7},{7,6},{8,9},{9,8},{10,11... | collective-permute-start | bytes 540680 | tf_op jit(solution)/shard_map/ppermute | solution.py:26
  29.1 3.6 %collective-permute-start.7 = (f32[1,256]{1,0:T(1,128)S(1)}, f32[1,256]{1,0:T(1,128)S(1)}, u32[]{:S(2)}, u32[]{:S(2)}) collective-permute-start(f32[1,256]{1,0:T(1,128)S(1)} %shard_map.31), channel_id=1, source_target_pairs={{0,2},{1,3},{2,0},{3,1},{4,6},{5,7},{6,4},{7,5},{8,10},{9,11},{10,... | collective-permute-start | bytes 3080 | tf_op jit(solution)/shard_map/ppermute | solution.py:26

commit v10 on v8

--- a/solution.py
+++ b/solution.py
@@ -78,27 +78,36 @@
     return src_m, src_v, bufs[level % 2]
 
 
+def windows(at, step, x8, mean_ref, scale_ref):
+    mean = mean_ref[pl.ds(at, GROUP), :]
+    scale = scale_ref[pl.ds(at, GROUP), :]
+    lag = lax.rem(step, 2) * STEP_K
+    start = pl.multiple_of(step // 2 * ALIGN + at, ALIGN)
+    z = []
+    for k in range(STEP_K):
+        x = x8[lag + k, pl.ds(start, GROUP), :]
+        z.append(((x - mean) * scale).astype(jnp.bfloat16))
+    return jnp.concatenate(z[:2], axis=1), jnp.concatenate(z[2:], axis=1)
+
+
+def fill_rows(step, x8, mean_ref, scale_ref, zr):
+    rows = zr.shape[2]
+    for at in range(0, rows, GROUP):
+        for unit, z in enumerate(windows(STEPS * rows + at, step, x8, mean_ref, scale_ref)):
+            zr[step, unit, at : at + GROUP, :] = z
+
+
+def reaches(base, size, rows):
+    return base + size > (STEPS - lax.axis_index("tm")) * rows
+
+
 def contract(base, x8, mean_ref, scale_ref, zr, out, fill):
     rows = zr.shape[2]
     size = out.shape[0]
-    first_row = STEPS * rows
-
-    def windows(at, step):
-        mean = mean_ref[pl.ds(at, GROUP), :]
-        scale = scale_ref[pl.ds(at, GROUP), :]
-        lag = lax.rem(step, 2) * STEP_K
-        start = pl.multiple_of(step // 2 * ALIGN + at, ALIGN)
-        z = []
-        for k in range(STEP_K):
-            x = x8[lag + k, pl.ds(start, GROUP), :]
-            z.append(((x - mean) * scale).astype(jnp.bfloat16))
-        return jnp.concatenate(z[:2], axis=1), jnp.concatenate(z[2:], axis=1)
 
     def stage(step):
         if fill:
-            for at in range(0, rows, GROUP):
-                for unit, z in enumerate(windows(first_row + at, step)):
-                    zr[step, unit, at : at + GROUP, :] = z
+            fill_rows(step, x8, mean_ref, scale_ref, zr)
         for unit in range(UNITS):
             pltpu.matmul_push_rhs(zr[step, unit], 0, unit, transpose=True)
 
@@ -107,7 +116,7 @@
 
         def stream(step, following):
             for g, at in enumerate(range(0, size, GROUP)):
-                pair = windows(pl.multiple_of(base + at, GROUP), step)
+                pair = windows(pl.multiple_of(base + at, GROUP), step, x8, mean_ref, scale_ref)
                 for unit in range(UNITS):
                     pltpu.matmul_acc_lhs(sums[unit][g], pair[unit], 0 if g == 0 else None)
                 if g == 0 and following:
@@ -158,41 +167,84 @@
 
 
 def neighbours(place, from_first, from_second, from_third):
-    second = from_first if from_second is None else from_second
-    earlier = jnp.where(place < 2, second, from_first)
+    earlier = jnp.where(place < 2, from_second, from_first)
     odd = lax.rem(place, 2) == 1
-    before = jnp.where(odd, from_third, jnp.where(place == 0, from_first, second))
-    after = jnp.where(odd, jnp.where(place == 1, from_first, second), from_third)
+    before = jnp.where(odd, from_third, jnp.where(place == 0, from_first, from_second))
+    after = jnp.where(odd, jnp.where(place == 1, from_first, from_second), from_third)
     return earlier, before, after
 
 
-def early_kernel(own, from_first, from_third, x8, end_m, end_v, *work):
+def first_kernel(own, from_first, x8, end_m, end_v, *work):
     place = lax.rem(lax.axis_index("tm"), LINE)
 
+    @pl.when(place == 0)
+    def _():
+        prepare(1, from_first[...], own[...], x8, end_m, end_v, work)
+
+    @pl.when(place == 1)
+    def _():
+        prepare(2, own[...], from_first[...], x8, end_m, end_v, work)
+
+
+def third_kernel(own, from_third, _x8, _m, _v, x8, end_m, end_v, zr, *work):
+    place = lax.rem(lax.axis_index("tm"), LINE)
+
+    @pl.when(place == 0)
+    def _():
+        prepare(2, own[...], from_third[...], x8, end_m, end_v, work)
+
+    @pl.when(place == 1)
+    def _():
+        prepare(1, from_third[...], own[...], x8, end_m, end_v, work)
+
     @pl.when(place < 2)
     def _():
-        _, before, after = neighbours(place, from_first[...], None, from_third[...])
+        def step(p, carry):
+            fill_rows(p, x8, end_m, end_v, zr)
+            return carry
+
+        lax.fori_loop(0, zr.shape[0], step, 0)
+
+
+def far_kernel(own, from_first, from_third, from_second, _x8, _m, _v, _zr, out, x8, end_m, end_v, zr, *work):
+    place = lax.rem(lax.axis_index("tm"), LINE)
+    size = out.shape[0]
+    base = (1 - lax.axis_index("chan") // 2) * size
+    live = reaches(base, size, own.shape[1])
+
+    @pl.when(place < 2)
+    def _():
+        prepare(0, from_second[...], jnp.where(place == 0, from_first[...], from_third[...]), x8, end_m, end_v, work)
+
+        @pl.when(live)
+        def _():
+            contract(base, x8, end_m, end_v, zr, out, False)
+
+        @pl.when(jnp.logical_not(live))
+        def _():
+            out[...] = jnp.zeros_like(out)
+
+    @pl.when(place >= 2)
+    def _():
+        earlier, before, after = neighbours(place, from_first[...], from_second[...], from_third[...])
+        prepare(0, earlier, before, x8, end_m, end_v, work)
         prepare(1, before, own[...], x8, end_m, end_v, work)
         prepare(2, own[...], after, x8, end_m, end_v, work)
-
-
-def far_kernel(own, from_first, from_third, from_second, _x8, _m, _v, out, x8, end_m, end_v, zr, *work):
-    place = lax.rem(lax.axis_index("tm"), LINE)
-    earlier, before, after = neighbours(place, from_first[...], from_second[...], from_third[...])
-    prepare(0, earlier, before, x8, end_m, end_v, work)
-
-    @pl.when(place >= 2)
-    def _():
-        prepare(1, before, own[...], x8, end_m, end_v, work)
-        prepare(2, own[...], after, x8, end_m, end_v, work)
-
-    base = (1 - lax.axis_index("chan") // 2) * out.shape[0]
-    contract(base, x8, end_m, end_v, zr, out, True)
+        contract(base, x8, end_m, end_v, zr, out, True)
 
 
 def near_kernel(x8, end_m, end_v, zr, out):
-    base = lax.axis_index("chan") // 2 * out.shape[0]
-    contract(base, x8, end_m, end_v, zr, out, False)
+    size = out.shape[0]
+    base = lax.axis_index("chan") // 2 * size
+    live = reaches(base, size, zr.shape[2])
+
+    @pl.when(live)
+    def _():
+        contract(base, x8, end_m, end_v, zr, out, False)
+
+    @pl.when(jnp.logical_not(live))
+    def _():
+        out[...] = jnp.zeros_like(out)
 
 
 def peak_kernel(rows, lens, p0, p1, p2, p3, out):
@@ -240,29 +292,34 @@
     tall = jax.ShapeDtypeStruct((room, LANES), f32)
     shifted = jax.ShapeDtypeStruct((ALIGN, room, LANES), f32)
     work = [pltpu.VMEM((rows + 2 * HALF, LANES), f32)] * 5
-    early = pl.pallas_call(
-        early_kernel,
+    row_windows = jax.ShapeDtypeStruct((HALF // STEP_K, UNITS, rows, 2 * LANES), bf16)
+    params = pltpu.CompilerParams(vmem_limit_bytes=SMALL_LIMIT)
+    after_first = pl.pallas_call(
+        first_kernel,
         out_shape=[shifted, tall, tall],
-        in_specs=[vmem] * 3,
+        in_specs=[vmem] * 2,
         out_specs=[vmem] * 3,
         scratch_shapes=work,
-        compiler_params=pltpu.CompilerParams(vmem_limit_bytes=SMALL_LIMIT),
-    )(own, from_first, from_third)
+        compiler_params=params,
+    )(own, from_first)
+    after_third = pl.pallas_call(
+        third_kernel,
+        out_shape=[shifted, tall, tall, row_windows],
+        in_specs=[vmem] * 5,
+        out_specs=[vmem] * 4,
+        input_output_aliases={2: 0, 3: 1, 4: 2},
+        scratch_shapes=work,
+        compiler_params=params,
+    )(own, from_third, *after_first)
     far, *shared = pl.pallas_call(
         far_kernel,
-        out_shape=[
-            jax.ShapeDtypeStruct((side, rows), bf16),
-            shifted,
-            tall,
-            tall,
-            jax.ShapeDtypeStruct((HALF // STEP_K, UNITS, rows, 2 * LANES), bf16),
-        ],
-        in_specs=[vmem] * 7,
+        out_shape=[jax.ShapeDtypeStruct((side, rows), bf16), shifted, tall, tall, row_windows],
+        in_specs=[vmem] * 8,
         out_specs=[vmem] * 5,
-        input_output_aliases={4: 1, 5: 2, 6: 3},
+        input_output_aliases={4: 1, 5: 2, 6: 3, 7: 4},
         scratch_shapes=work,
-        compiler_params=pltpu.CompilerParams(vmem_limit_bytes=SMALL_LIMIT),
-    )(own, from_first, from_third, from_second, *early)
+        compiler_params=params,
+    )(own, from_first, from_third, from_second, *after_third)
     far_got = sent(far, "chan", across(2))
     near = pl.pallas_call(
         near_kernel,

time: 32.3 us -> 31.5 us (0.975)
  waiting for transfers between devices: 10.9 us -> 14.9 us
  Pallas kernels: 11.5 us -> 8.65 us
  starting transfers between devices: 8.23 us -> 6.22 us
    ppermute x7, waiting for transfers between devices: 10.9 us -> 14.9 us  [sent(): lax.ppermute(block, axis, [(i, target(i, count)) for i in range(count)])]
    pallas_call x1, Pallas kernels: 3.81 us -> 0.05 us  [body(): pl.pallas_call(near_kernel, out_shape=jax.ShapeDtypeStruct((side, rows),...]
    ppermute x7, starting transfers between devices: 8.23 us -> 6.22 us  [sent(): lax.ppermute(block, axis, [(i, target(i, count)) for i in range(count)])]
    pallas_call x1 -> x2, Pallas kernels: 1.35 us -> 3.25 us  [the longest x1 2.56 us: body(): pl.pallas_call(third_kernel, out_shape=[shifted, tall, tall, row_windows]...]
    pallas_call x1, Pallas kernels: 5.53 us -> 4.52 us  [body(): pl.pallas_call(far_kernel, out_shape=[jax.ShapeDtypeStruct((side, rows),...]
  transfers between devices with their start and end apart: 7 -> 7, of which waited for: 5 -> 4; matrix products, arithmetic and copies ran while one was open for 3% -> 3% of each run, Pallas kernels for 16% -> 11%
where the time goes in v10:
time: 31.5 us; the launch traced here: 31.3 us
  waiting for transfers between devices  14.9 us (47%)
  Pallas kernels  8.65 us (27%)
  starting transfers between devices  6.22 us (20%)
  other arithmetic  1.45 us (5%)
    ppermute x7, waiting for transfers between devices, sent(): lax.ppermute(block, axis, [(i, target(i, count)) for i in range(count)])  14.9 us
    ppermute x7, starting transfers between devices, sent(): lax.ppermute(block, axis, [(i, target(i, count)) for i in range(count)])  6.22 us
    pallas_call x1, Pallas kernels, body(): pl.pallas_call(far_kernel, out_shape=[jax.ShapeDtypeStruct((side, rows),...  4.52 us
    pallas_call x1, Pallas kernels, body(): pl.pallas_call(third_kernel, out_shape=[shifted, tall, tall, row_windows]...  2.56 us
    max x1, other arithmetic, body(): own = jnp.maximum(series, jnp.finfo(series.dtype).min)  0.88 us
    pallas_call x1, Pallas kernels, body(): pl.pallas_call(functools.partial(peak_kernel, rows), out_shape=jax.ShapeD...  0.83 us
    pallas_call x1, Pallas kernels, body(): pl.pallas_call(first_kernel, out_shape=[shifted, tall, tall], in_specs=[v...  0.69 us
  transfers between devices with their start and end apart: 7, of which 4 were waited for; matrix products, arithmetic and copies ran while one was open for 3% of the time, Pallas kernels for 11%

profile of v10, /device:TPU:0, one launch (start us, length us, event | category | flops | bytes accessed | tf_op | source)
XLA Modules:
  0.0 31.3 jit_solution(3111940162736794366)
XLA Ops:
  0.0 4.0 %collective-permute-start = (f32[64,256]{1,0:T(8,128)}, f32[64,256]{1,0:T(8,128)S(1)}, u32[]{:S(2)}, u32[]{:S(2)}) collective-permute-start(f32[64,256]{1,0:T(8,128)} %param.2), channel_id=1, source_target_pairs={{0,8},{4,12},{8,4},{12,16},{16,24},{20,28},{24,20},{28,32},{32,40}... | collective-permute-start | bytes 196616 | tf_op jit(solution)/shard_map/ppermute | solution.py:26
  4.0 1.0 %collective-permute-start.2 = (f32[64,256]{1,0:T(8,128)}, f32[64,256]{1,0:T(8,128)S(1)}, u32[]{:S(2)}, u32[]{:S(2)}) collective-permute-start(f32[64,256]{1,0:T(8,128)} %param.2), channel_id=1, source_target_pairs={{0,4},{4,8},{8,16},{12,20},{16,12},{20,24},{24,32},{28,36},{32,28}... | collective-permute-start | bytes 196616 | tf_op jit(solution)/shard_map/ppermute | solution.py:26
  5.0 0.0 collective-permute-start.1
  5.0 0.9 %broadcast_maximum_fusion.own = f32[64,256]{1,0:T(8,128)S(1)} fusion(f32[64,256]{1,0:T(8,128)} %param.2), kind=kLoop, calls=%fused_computation | loop fusion | flops 16384 | bytes 131072 | tf_op jit(solution)/shard_map/max | solution.py:283
  5.9 5.6 %collective-permute-done.from_first = f32[64,256]{1,0:T(8,128)S(1)} collective-permute-done((f32[64,256]{1,0:T(8,128)}, f32[64,256]{1,0:T(8,128)S(1)}, u32[]{:S(2)}, u32[]{:S(2)}) %collective-permute-start) | collective-permute-done | bytes 65568 | tf_op jit(solution)/shard_map/ppermute | solution.py:26
  11.5 0.7 %shard_map.28 = (f32[8,1024,128]{2,1,0:T(8,128)S(1)}, f32[1024,128]{1,0:T(8,128)S(1)}, f32[1024,128]{1,0:T(8,128)S(1)}) custom-call(f32[64,256]{1,0:T(8,128)S(1)} %broadcast_maximum_fusion.own, f32[64,256]{1,0:T(8,128)S(1)} %collective-permute-done.from_first), custom_call_target="tpu_custom_call" | custom-call | tf_op jit(solution)/shard_map/pallas_call | solution.py:297
  12.2 0.0 collective-permute-done.1.from_third
  12.2 2.6 %shard_map.29 = (f32[8,1024,128]{2,1,0:T(8,128)S(1)}, f32[1024,128]{1,0:T(8,128)S(1)}, f32[1024,128]{1,0:T(8,128)S(1)}, bf16[32,2,256,256]{3,2,1,0:T(8,128)(2,1)S(1)}) custom-call(f32[64,256]{1,0:T(8,128)S(1)} %broadcast_maximum_fusion.own, ...), custom_call_target="tpu_custom_call", output_to_operand_aliasing={{0}: (2, {}), {1}: (3, {}), {2}: (4, {})} | custom-call | tf_op jit(solution)/shard_map/pallas_call | solution.py:305
  14.8 0.0 collective-permute-done.2.from_second
  14.8 4.5 %shard_map.30 = (bf16[352,256]{1,0:T(8,128)(2,1)S(1)}, f32[8,1024,128]{2,1,0:T(8,128)S(1)}, f32[1024,128]{1,0:T(8,128)S(1)}, f32[1024,128]{1,0:T(8,128)S(1)}, bf16[32,2,256,256]{3,2,1,0:T(8,128)(2,1)S(1)}) custom-call(f32[64,256]{1,0:T(8,128)S(1)} %broadcast_maximum_fusion.own, ...), custom_call_target="tpu_custom_call", output_to_operand_aliasing={{1}: (4, {}), {2}: (5, {}), {3}: (6, {}), {4}: (7, {})} | custom-call | tf_op jit(solution)/shard_map/pallas_call | solution.py:314
  19.3 0.1 collective-permute-start.4
  19.4 0.0 copy-start
  19.5 0.1 collective-permute-start.3
  19.5 5.3 %collective-permute-done.4.p2 = bf16[352,256]{1,0:T(8,128)(2,1)S(1)} collective-permute-done((bf16[352,256]{1,0:T(8,128)(2,1)S(1)}, bf16[352,256]{1,0:T(8,128)(2,1)S(1)}, u32[]{:S(2)}, u32[]{:S(2)}) %collective-permute-start.4) | collective-permute-done | bytes 180256 | tf_op jit(solution)/shard_map/ppermute | solution.py:26
  24.9 0.0 collective-permute-start.5
  24.9 1.4 %collective-permute-done.5.p3 = bf16[352,256]{1,0:T(8,128)(2,1)S(1)} collective-permute-done((bf16[352,256]{1,0:T(8,128)(2,1)S(1)}, bf16[352,256]{1,0:T(8,128)(2,1)S(1)}, u32[]{:S(2)}, u32[]{:S(2)}) %collective-permute-start.5) | collective-permute-done | bytes 180256 | tf_op jit(solution)/shard_map/ppermute | solution.py:26
  26.3 0.0 collective-permute-done.3.p1
  26.3 0.0 copy-done
  26.3 0.8 %shard_map.32 = f32[1,256]{1,0:T(1,128)S(1)} custom-call(s32[64]{0:T(128)S(1)} %copy-done, f32[352,256]{1,0:T(8,128)S(1)} %shard_map.31.p0, f32[352,256]{1,0:T(8,128)S(1)} %collective-permute-done.3.p1, bf16[352,256]{1,0:T(8,128)(2,1)S(1)} %collective-permute-done.4.p2, bf16[352,256]{1,0:T(8,128)(2,1)S(1)} %collective-permute-done.5.p3), custom_call_target="tpu_custom_call" | custom-call | tf_op jit(solution)/shard_map/pallas_call | solution.py:333
  27.1 1.0 %collective-permute-start.6 = (f32[1,256]{1,0:T(1,128)S(1)}, f32[1,256]{1,0:T(1,128)S(1)}, u32[]{:S(2)}, u32[]{:S(2)}) collective-permute-start(f32[1,256]{1,0:T(1,128)S(1)} %shard_map.32), channel_id=1, source_target_pairs={{0,2},{1,3},{2,0},{3,1},{4,6},{5,7},{6,4},{7,5},{8,10},{9,11},{10,... | collective-permute-start | bytes 3080 | tf_op jit(solution)/shard_map/ppermute | solution.py:26
  28.2 2.6 %collective-permute-done.6 = f32[1,256]{1,0:T(1,128)S(1)} collective-permute-done((f32[1,256]{1,0:T(1,128)S(1)}, f32[1,256]{1,0:T(1,128)S(1)}, u32[]{:S(2)}, u32[]{:S(2)}) %collective-permute-start.6) | collective-permute-done | bytes 1056 | tf_op jit(solution)/shard_map/ppermute | solution.py:26
  30.8 0.6 %compare_select_fusion = f32[1,256]{1,0:T(1,128)} fusion(f32[1,256]{1,0:T(1,128)S(1)} %shard_map.32, f32[1,256]{1,0:T(1,128)S(1)} %collective-permute-done.6), kind=kLoop, calls=%fused_computation.1 | loop fusion | flops 768 | bytes 3072 | tf_op jit(solution)/shard_map/jit(_where)/select_n | solution.py:341
  (1 shorter events, 0.0 us)
Async XLA Ops:
  0.0 11.5 %collective-permute-start = (f32[64,256]{1,0:T(8,128)}, f32[64,256]{1,0:T(8,128)S(1)}, u32[]{:S(2)}, u32[]{:S(2)}) collective-permute-start(f32[64,256]{1,0:T(8,128)} %param.2), channel_id=1, source_target_pairs={{0,8},{4,12},{8,4},{12,16},{16,24},{20,28},{24,20},{28,32},{32,40}... | collective-permute-start | bytes 196616 | tf_op jit(solution)/shard_map/ppermute | solution.py:26
  4.0 10.8 %collective-permute-start.2 = (f32[64,256]{1,0:T(8,128)}, f32[64,256]{1,0:T(8,128)S(1)}, u32[]{:S(2)}, u32[]{:S(2)}) collective-permute-start(f32[64,256]{1,0:T(8,128)} %param.2), channel_id=1, source_target_pairs={{0,4},{4,8},{8,16},{12,20},{16,12},{20,24},{24,32},{28,36},{32,28}... | collective-permute-start | bytes 196616 | tf_op jit(solution)/shard_map/ppermute | solution.py:26
  5.0 7.2 %collective-permute-start.1 = (f32[64,256]{1,0:T(8,128)}, f32[64,256]{1,0:T(8,128)S(1)}, u32[]{:S(2)}, u32[]{:S(2)}) collective-permute-start(f32[64,256]{1,0:T(8,128)} %param.2), channel_id=1, source_target_pairs={{0,4},{4,0},{8,12},{12,8},{16,20},{20,16},{24,28},{28,24},{32,36},... | collective-permute-start | bytes 196616 | tf_op jit(solution)/shard_map/ppermute | solution.py:26
  19.3 5.6 %collective-permute-start.4 = (bf16[352,256]{1,0:T(8,128)(2,1)S(1)}, bf16[352,256]{1,0:T(8,128)(2,1)S(1)}, u32[]{:S(2)}, u32[]{:S(2)}) collective-permute-start(bf16[352,256]{1,0:T(8,128)(2,1)S(1)} %get-tuple-element.28), channel_id=1, source_target_pairs={{0,2},{1,3},{2,0},{3,1},{4,6},{5,7},{6,4},{7,5},{8,10},{9,11},{10,... | collective-permute-start | bytes 540680 | tf_op jit(solution)/shard_map/ppermute | solution.py:26
  19.4 6.9 %copy-start = (s32[64]{0:T(128)S(1)}, s32[64]{0:T(128)}, u32[]{:S(2)}) copy-start(s32[64]{0:T(128)} %lens.1) | copy-start | bytes 772
  19.5 6.8 %collective-permute-start.3 = (f32[352,256]{1,0:T(8,128)S(1)}, f32[352,256]{1,0:T(8,128)S(1)}, u32[]{:S(2)}, u32[]{:S(2)}) collective-permute-start(f32[352,256]{1,0:T(8,128)S(1)} %shard_map.31.p0), channel_id=1, source_target_pairs={{0,1},{1,0},{2,3},{3,2},{4,5},{5,4},{6,7},{7,6},{8,9},{9,8},{10,11... | collective-permute-start | bytes 1081352 | tf_op jit(solution)/shard_map/ppermute | solution.py:26
  24.9 1.4 %collective-permute-start.5 = (bf16[352,256]{1,0:T(8,128)(2,1)S(1)}, bf16[352,256]{1,0:T(8,128)(2,1)S(1)}, u32[]{:S(2)}, u32[]{:S(2)}) collective-permute-start(bf16[352,256]{1,0:T(8,128)(2,1)S(1)} %collective-permute-done.4.p2), channel_id=1, source_target_pairs={{0,1},{1,0},{2,3},{3,2},{4,5},{5,4},{6,7},{7,6},{8,9},{9,8},{10,11... | collective-permute-start | bytes 540680 | tf_op jit(solution)/shard_map/ppermute | solution.py:26
  27.1 3.6 %collective-permute-start.6 = (f32[1,256]{1,0:T(1,128)S(1)}, f32[1,256]{1,0:T(1,128)S(1)}, u32[]{:S(2)}, u32[]{:S(2)}) collective-permute-start(f32[1,256]{1,0:T(1,128)S(1)} %shard_map.32), channel_id=1, source_target_pairs={{0,2},{1,3},{2,0},{3,1},{4,6},{5,7},{6,4},{7,5},{8,10},{9,11},{10,... | collective-permute-start | bytes 3080 | tf_op jit(solution)/shard_map/ppermute | solution.py:26

commit v11 on v10

--- a/solution.py
+++ b/solution.py
@@ -78,11 +78,11 @@
     return src_m, src_v, bufs[level % 2]
 
 
-def windows(at, step, x8, mean_ref, scale_ref):
+def windows(at, two, half, x8, mean_ref, scale_ref):
     mean = mean_ref[pl.ds(at, GROUP), :]
     scale = scale_ref[pl.ds(at, GROUP), :]
-    lag = lax.rem(step, 2) * STEP_K
-    start = pl.multiple_of(step // 2 * ALIGN + at, ALIGN)
+    lag = half * STEP_K
+    start = pl.multiple_of(two * ALIGN + at, ALIGN)
     z = []
     for k in range(STEP_K):
         x = x8[lag + k, pl.ds(start, GROUP), :]
@@ -90,10 +90,11 @@
     return jnp.concatenate(z[:2], axis=1), jnp.concatenate(z[2:], axis=1)
 
 
-def fill_rows(step, x8, mean_ref, scale_ref, zr):
+def fill_rows(two, half, x8, mean_ref, scale_ref, zr):
     rows = zr.shape[2]
+    step = 2 * two + half
     for at in range(0, rows, GROUP):
-        for unit, z in enumerate(windows(STEPS * rows + at, step, x8, mean_ref, scale_ref)):
+        for unit, z in enumerate(windows(STEPS * rows + at, two, half, x8, mean_ref, scale_ref)):
             zr[step, unit, at : at + GROUP, :] = z
 
 
@@ -105,35 +106,38 @@
     rows = zr.shape[2]
     size = out.shape[0]
 
-    def stage(step):
+    def stage(two, half):
+        step = 2 * two + half
         if fill:
-            fill_rows(step, x8, mean_ref, scale_ref, zr)
+            fill_rows(two, half, x8, mean_ref, scale_ref, zr)
         for unit in range(UNITS):
             pltpu.matmul_push_rhs(zr[step, unit], 0, unit, transpose=True)
 
     def run(*sums):
         sums = sums[: len(sums) // UNITS], sums[len(sums) // UNITS :]
 
-        def stream(step, following):
+        def stream(two, half, following):
             for g, at in enumerate(range(0, size, GROUP)):
-                pair = windows(pl.multiple_of(base + at, GROUP), step, x8, mean_ref, scale_ref)
+                pair = windows(pl.multiple_of(base + at, GROUP), two, half, x8, mean_ref, scale_ref)
                 for unit in range(UNITS):
                     pltpu.matmul_acc_lhs(sums[unit][g], pair[unit], 0 if g == 0 else None)
-                if g == 0 and following:
-                    stage(step + 1)
+                if g == 0 and following is not None:
+                    stage(*following)
 
         for g in range(size // GROUP):
             for unit in range(UNITS):
                 pltpu.matmul_pop(sums[unit][g])
-        steps = HALF // STEP_K
-        stage(0)
-
-        def advance(step, carry):
-            stream(step, True)
+        twos = HALF // STEP_K // 2
+        stage(0, 0)
+
+        def advance(two, carry):
+            stream(two, 0, (two, 1))
+            stream(two, 1, (two + 1, 0))
             return carry
 
-        lax.fori_loop(0, steps - 1, advance, 0)
-        stream(steps - 1, False)
+        lax.fori_loop(0, twos - 1, advance, 0)
+        stream(twos - 1, 0, (twos - 1, 1))
+        stream(twos - 1, 1, None)
         for g, at in enumerate(range(0, size, GROUP)):
             both = pltpu.matmul_pop(sums[0][g]) + pltpu.matmul_pop(sums[1][g])
             out[at : at + GROUP, :] = both.astype(out.dtype)
@@ -177,7 +181,7 @@
 def first_kernel(own, from_first, x8, end_m, end_v, *work):
     place = lax.rem(lax.axis_index("tm"), LINE)
 
-    @pl.when(place == 0)
+    @pl.when((place == 0) & (lax.axis_index("tm") > 0))
     def _():
         prepare(1, from_first[...], own[...], x8, end_m, end_v, work)
 
@@ -200,10 +204,11 @@
     @pl.when(place < 2)
     def _():
         def step(p, carry):
-            fill_rows(p, x8, end_m, end_v, zr)
+            fill_rows(p, 0, x8, end_m, end_v, zr)
+            fill_rows(p, 1, x8, end_m, end_v, zr)
             return carry
 
-        lax.fori_loop(0, zr.shape[0], step, 0)
+        lax.fori_loop(0, zr.shape[0] // 2, step, 0)
 
 
 def far_kernel(own, from_first, from_third, from_second, _x8, _m, _v, _zr, out, x8, end_m, end_v, zr, *work):
@@ -214,7 +219,9 @@
 
     @pl.when(place < 2)
     def _():
-        prepare(0, from_second[...], jnp.where(place == 0, from_first[...], from_third[...]), x8, end_m, end_v, work)
+        @pl.when(lax.axis_index("tm") > 1)
+        def _():
+            prepare(0, from_second[...], jnp.where(place == 0, from_first[...], from_third[...]), x8, end_m, end_v, work)
 
         @pl.when(live)
         def _():

time: 31.5 us -> 30.4 us (0.965); the launches traced: 31.3 us -> 29.9 us
  Pallas kernels: 8.65 us -> 7.05 us
  waiting for transfers between devices: 14.9 us -> 15.3 us
    pallas_call x1, Pallas kernels: 4.52 us -> 3.71 us  [body(): pl.pallas_call(far_kernel, out_shape=[jax.ShapeDtypeStruct((side, rows),...]
    pallas_call x1, Pallas kernels: 0.69 us -> 0.01 us  [body(): pl.pallas_call(first_kernel, out_shape=[shifted, tall, tall], in_specs=[v...]
    ppermute x7, waiting for transfers between devices: 14.9 us -> 15.3 us  [sent(): lax.ppermute(block, axis, [(i, target(i, count)) for i in range(count)])]
  transfers between devices with their start and end apart: 7 -> 7, of which waited for: 4 -> 5; matrix products, arithmetic and copies ran while one was open for 3% -> 3% of each run, Pallas kernels for 11% -> 8%
where the time goes in v11:
time: 30.4 us; the launch traced here: 29.9 us
  waiting for transfers between devices  15.3 us (50%)
  Pallas kernels  7.05 us (23%)
  starting transfers between devices  6.11 us (20%)
  other arithmetic  1.45 us (5%)
    ppermute x7, waiting for transfers between devices, sent(): lax.ppermute(block, axis, [(i, target(i, count)) for i in range(count)])  15.3 us
    ppermute x7, starting transfers between devices, sent(): lax.ppermute(block, axis, [(i, target(i, count)) for i in range(count)])  6.11 us
    pallas_call x1, Pallas kernels, body(): pl.pallas_call(far_kernel, out_shape=[jax.ShapeDtypeStruct((side, rows),...  3.71 us
    pallas_call x1, Pallas kernels, body(): pl.pallas_call(third_kernel, out_shape=[shifted, tall, tall, row_windows]...  2.46 us
    max x1, other arithmetic, body(): own = jnp.maximum(series, jnp.finfo(series.dtype).min)  0.88 us
    pallas_call x1, Pallas kernels, body(): pl.pallas_call(functools.partial(peak_kernel, rows), out_shape=jax.ShapeD...  0.83 us
  transfers between devices with their start and end apart: 7, of which 5 were waited for; matrix products, arithmetic and copies ran while one was open for 3% of the time, Pallas kernels for 8%

profile of v11, /device:TPU:0, one launch (start us, length us, event | category | flops | bytes accessed | tf_op | source)
XLA Modules:
  0.0 29.9 jit_solution(8293383163690212959)
XLA Ops:
  0.0 4.0 %collective-permute-start = (f32[64,256]{1,0:T(8,128)}, f32[64,256]{1,0:T(8,128)S(1)}, u32[]{:S(2)}, u32[]{:S(2)}) collective-permute-start(f32[64,256]{1,0:T(8,128)} %param.2), channel_id=1, source_target_pairs={{0,8},{4,12},{8,4},{12,16},{16,24},{20,28},{24,20},{28,32},{32,40}... | collective-permute-start | bytes 196616 | tf_op jit(solution)/shard_map/ppermute | solution.py:26
  4.0 1.0 %collective-permute-start.2 = (f32[64,256]{1,0:T(8,128)}, f32[64,256]{1,0:T(8,128)S(1)}, u32[]{:S(2)}, u32[]{:S(2)}) collective-permute-start(f32[64,256]{1,0:T(8,128)} %param.2), channel_id=1, source_target_pairs={{0,4},{4,8},{8,16},{12,20},{16,12},{20,24},{24,32},{28,36},{32,28}... | collective-permute-start | bytes 196616 | tf_op jit(solution)/shard_map/ppermute | solution.py:26
  5.0 0.0 collective-permute-start.1
  5.0 0.9 %broadcast_maximum_fusion.own = f32[64,256]{1,0:T(8,128)S(1)} fusion(f32[64,256]{1,0:T(8,128)} %param.2), kind=kLoop, calls=%fused_computation | loop fusion | flops 16384 | bytes 131072 | tf_op jit(solution)/shard_map/max | solution.py:290
  5.9 5.6 %collective-permute-done.from_first = f32[64,256]{1,0:T(8,128)S(1)} collective-permute-done((f32[64,256]{1,0:T(8,128)}, f32[64,256]{1,0:T(8,128)S(1)}, u32[]{:S(2)}, u32[]{:S(2)}) %collective-permute-start) | collective-permute-done | bytes 65568 | tf_op jit(solution)/shard_map/ppermute | solution.py:26
  11.5 0.0 collective-permute-done.1.from_third
  11.5 2.5 %shard_map.29 = (f32[8,1024,128]{2,1,0:T(8,128)S(1)}, f32[1024,128]{1,0:T(8,128)S(1)}, f32[1024,128]{1,0:T(8,128)S(1)}, bf16[32,2,256,256]{3,2,1,0:T(8,128)(2,1)S(1)}) custom-call(f32[64,256]{1,0:T(8,128)S(1)} %broadcast_maximum_fusion.own, ...), custom_call_target="tpu_custom_call", output_to_operand_aliasing={{0}: (2, {}), {1}: (3, {}), {2}: (4, {})} | custom-call | tf_op jit(solution)/shard_map/pallas_call | solution.py:312
  14.0 0.2 collective-permute-done.2.from_second
  14.2 3.7 %shard_map.30 = (bf16[352,256]{1,0:T(8,128)(2,1)S(1)}, f32[8,1024,128]{2,1,0:T(8,128)S(1)}, f32[1024,128]{1,0:T(8,128)S(1)}, f32[1024,128]{1,0:T(8,128)S(1)}, bf16[32,2,256,256]{3,2,1,0:T(8,128)(2,1)S(1)}) custom-call(f32[64,256]{1,0:T(8,128)S(1)} %broadcast_maximum_fusion.own, ...), custom_call_target="tpu_custom_call", output_to_operand_aliasing={{1}: (4, {}), {2}: (5, {}), {3}: (6, {}), {4}: (7, {})} | custom-call | tf_op jit(solution)/shard_map/pallas_call | solution.py:321
  17.9 0.1 collective-permute-start.4
  18.0 0.0 copy-start
  18.0 0.1 collective-permute-start.3
  18.1 5.3 %collective-permute-done.4.p2 = bf16[352,256]{1,0:T(8,128)(2,1)S(1)} collective-permute-done((bf16[352,256]{1,0:T(8,128)(2,1)S(1)}, bf16[352,256]{1,0:T(8,128)(2,1)S(1)}, u32[]{:S(2)}, u32[]{:S(2)}) %collective-permute-start.4) | collective-permute-done | bytes 180256 | tf_op jit(solution)/shard_map/ppermute | solution.py:26
  23.5 0.0 collective-permute-start.5
  23.5 1.4 %collective-permute-done.5.p3 = bf16[352,256]{1,0:T(8,128)(2,1)S(1)} collective-permute-done((bf16[352,256]{1,0:T(8,128)(2,1)S(1)}, bf16[352,256]{1,0:T(8,128)(2,1)S(1)}, u32[]{:S(2)}, u32[]{:S(2)}) %collective-permute-start.5) | collective-permute-done | bytes 180256 | tf_op jit(solution)/shard_map/ppermute | solution.py:26
  24.9 0.0 collective-permute-done.3.p1
  24.9 0.0 copy-done
  24.9 0.8 %shard_map.32 = f32[1,256]{1,0:T(1,128)S(1)} custom-call(s32[64]{0:T(128)S(1)} %copy-done, f32[352,256]{1,0:T(8,128)S(1)} %shard_map.31.p0, f32[352,256]{1,0:T(8,128)S(1)} %collective-permute-done.3.p1, bf16[352,256]{1,0:T(8,128)(2,1)S(1)} %collective-permute-done.4.p2, bf16[352,256]{1,0:T(8,128)(2,1)S(1)} %collective-permute-done.5.p3), custom_call_target="tpu_custom_call" | custom-call | tf_op jit(solution)/shard_map/pallas_call | solution.py:340
  25.7 0.9 %collective-permute-start.6 = (f32[1,256]{1,0:T(1,128)S(1)}, f32[1,256]{1,0:T(1,128)S(1)}, u32[]{:S(2)}, u32[]{:S(2)}) collective-permute-start(f32[1,256]{1,0:T(1,128)S(1)} %shard_map.32), channel_id=1, source_target_pairs={{0,2},{1,3},{2,0},{3,1},{4,6},{5,7},{6,4},{7,5},{8,10},{9,11},{10,... | collective-permute-start | bytes 3080 | tf_op jit(solution)/shard_map/ppermute | solution.py:26
  26.6 2.7 %collective-permute-done.6 = f32[1,256]{1,0:T(1,128)S(1)} collective-permute-done((f32[1,256]{1,0:T(1,128)S(1)}, f32[1,256]{1,0:T(1,128)S(1)}, u32[]{:S(2)}, u32[]{:S(2)}) %collective-permute-start.6) | collective-permute-done | bytes 1056 | tf_op jit(solution)/shard_map/ppermute | solution.py:26
  29.4 0.6 %compare_select_fusion = f32[1,256]{1,0:T(1,128)} fusion(f32[1,256]{1,0:T(1,128)S(1)} %shard_map.32, f32[1,256]{1,0:T(1,128)S(1)} %collective-permute-done.6), kind=kLoop, calls=%fused_computation.1 | loop fusion | flops 768 | bytes 3072 | tf_op jit(solution)/shard_map/jit(_where)/select_n | solution.py:348
  (2 shorter events, 0.0 us)
Async XLA Ops:
  0.0 11.5 %collective-permute-start = (f32[64,256]{1,0:T(8,128)}, f32[64,256]{1,0:T(8,128)S(1)}, u32[]{:S(2)}, u32[]{:S(2)}) collective-permute-start(f32[64,256]{1,0:T(8,128)} %param.2), channel_id=1, source_target_pairs={{0,8},{4,12},{8,4},{12,16},{16,24},{20,28},{24,20},{28,32},{32,40}... | collective-permute-start | bytes 196616 | tf_op jit(solution)/shard_map/ppermute | solution.py:26
  4.0 10.2 %collective-permute-start.2 = (f32[64,256]{1,0:T(8,128)}, f32[64,256]{1,0:T(8,128)S(1)}, u32[]{:S(2)}, u32[]{:S(2)}) collective-permute-start(f32[64,256]{1,0:T(8,128)} %param.2), channel_id=1, source_target_pairs={{0,4},{4,8},{8,16},{12,20},{16,12},{20,24},{24,32},{28,36},{32,28}... | collective-permute-start | bytes 196616 | tf_op jit(solution)/shard_map/ppermute | solution.py:26
  5.0 6.5 %collective-permute-start.1 = (f32[64,256]{1,0:T(8,128)}, f32[64,256]{1,0:T(8,128)S(1)}, u32[]{:S(2)}, u32[]{:S(2)}) collective-permute-start(f32[64,256]{1,0:T(8,128)} %param.2), channel_id=1, source_target_pairs={{0,4},{4,0},{8,12},{12,8},{16,20},{20,16},{24,28},{28,24},{32,36},... | collective-permute-start | bytes 196616 | tf_op jit(solution)/shard_map/ppermute | solution.py:26
  17.9 5.6 %collective-permute-start.4 = (bf16[352,256]{1,0:T(8,128)(2,1)S(1)}, bf16[352,256]{1,0:T(8,128)(2,1)S(1)}, u32[]{:S(2)}, u32[]{:S(2)}) collective-permute-start(bf16[352,256]{1,0:T(8,128)(2,1)S(1)} %get-tuple-element.28), channel_id=1, source_target_pairs={{0,2},{1,3},{2,0},{3,1},{4,6},{5,7},{6,4},{7,5},{8,10},{9,11},{10,... | collective-permute-start | bytes 540680 | tf_op jit(solution)/shard_map/ppermute | solution.py:26
  18.0 6.9 %copy-start = (s32[64]{0:T(128)S(1)}, s32[64]{0:T(128)}, u32[]{:S(2)}) copy-start(s32[64]{0:T(128)} %lens.1) | copy-start | bytes 772
  18.0 6.8 %collective-permute-start.3 = (f32[352,256]{1,0:T(8,128)S(1)}, f32[352,256]{1,0:T(8,128)S(1)}, u32[]{:S(2)}, u32[]{:S(2)}) collective-permute-start(f32[352,256]{1,0:T(8,128)S(1)} %shard_map.31.p0), channel_id=1, source_target_pairs={{0,1},{1,0},{2,3},{3,2},{4,5},{5,4},{6,7},{7,6},{8,9},{9,8},{10,11... | collective-permute-start | bytes 1081352 | tf_op jit(solution)/shard_map/ppermute | solution.py:26
  23.5 1.4 %collective-permute-start.5 = (bf16[352,256]{1,0:T(8,128)(2,1)S(1)}, bf16[352,256]{1,0:T(8,128)(2,1)S(1)}, u32[]{:S(2)}, u32[]{:S(2)}) collective-permute-start(bf16[352,256]{1,0:T(8,128)(2,1)S(1)} %collective-permute-done.4.p2), channel_id=1, source_target_pairs={{0,1},{1,0},{2,3},{3,2},{4,5},{5,4},{6,7},{7,6},{8,9},{9,8},{10,11... | collective-permute-start | bytes 540680 | tf_op jit(solution)/shard_map/ppermute | solution.py:26
  25.7 3.6 %collective-permute-start.6 = (f32[1,256]{1,0:T(1,128)S(1)}, f32[1,256]{1,0:T(1,128)S(1)}, u32[]{:S(2)}, u32[]{:S(2)}) collective-permute-start(f32[1,256]{1,0:T(1,128)S(1)} %shard_map.32), channel_id=1, source_target_pairs={{0,2},{1,3},{2,0},{3,1},{4,6},{5,7},{6,4},{7,5},{8,10},{9,11},{10,... | collective-permute-start | bytes 3080 | tf_op jit(solution)/shard_map/ppermute | solution.py:26

commit v12 on v11

--- a/solution.py
+++ b/solution.py
@@ -16,6 +16,7 @@
 STEP_K = 4
 GROUP = 32
 UNITS = 2
+BODY = 4
 LANES = 128
 ALIGN = 8
 SMALL_LIMIT = 8 << 20
@@ -130,14 +131,17 @@
         twos = HALF // STEP_K // 2
         stage(0, 0)
 
-        def advance(two, carry):
-            stream(two, 0, (two, 1))
-            stream(two, 1, (two + 1, 0))
+        def several(two, ends):
+            for t in range(BODY):
+                stream(two + t, 0, (two + t, 1))
+                stream(two + t, 1, None if ends and t == BODY - 1 else (two + t + 1, 0))
+
+        def advance(p, carry):
+            several(p * BODY, False)
             return carry
 
-        lax.fori_loop(0, twos - 1, advance, 0)
-        stream(twos - 1, 0, (twos - 1, 1))
-        stream(twos - 1, 1, None)
+        lax.fori_loop(0, twos // BODY - 1, advance, 0)
+        several(twos - BODY, True)
         for g, at in enumerate(range(0, size, GROUP)):
             both = pltpu.matmul_pop(sums[0][g]) + pltpu.matmul_pop(sums[1][g])
             out[at : at + GROUP, :] = both.astype(out.dtype)

time: 30.4 us -> 29.7 us (0.977)
  starting transfers between devices: 6.11 us -> 5.59 us
  Pallas kernels: 7.05 us -> 6.53 us
  waiting for transfers between devices: 15.3 us -> 15.8 us
    pallas_call x1, Pallas kernels: 3.71 us -> 3.19 us  [body(): pl.pallas_call(far_kernel, out_shape=[jax.ShapeDtypeStruct((side, rows),...]
    ppermute x7, waiting for transfers between devices: 15.3 us -> 15.8 us  [sent(): lax.ppermute(block, axis, [(i, target(i, count)) for i in range(count)])]
    ppermute x7, starting transfers between devices: 6.11 us -> 5.59 us  [sent(): lax.ppermute(block, axis, [(i, target(i, count)) for i in range(count)])]
  transfers between devices with their start and end apart: 7 -> 7, of which waited for: 5 -> 5; matrix products, arithmetic and copies ran while one was open for 3% -> 3% of each run, Pallas kernels for 8% -> 9%
where the time goes in v12:
time: 29.7 us; the launch traced here: 29.4 us
  waiting for transfers between devices  15.8 us (53%)
  Pallas kernels  6.53 us (22%)
  starting transfers between devices  5.59 us (19%)
  other arithmetic  1.45 us (5%)
    ppermute x7, waiting for transfers between devices, sent(): lax.ppermute(block, axis, [(i, target(i, count)) for i in range(count)])  15.8 us
    ppermute x7, starting transfers between devices, sent(): lax.ppermute(block, axis, [(i, target(i, count)) for i in range(count)])  5.59 us
    pallas_call x1, Pallas kernels, body(): pl.pallas_call(far_kernel, out_shape=[jax.ShapeDtypeStruct((side, rows),...  3.19 us
    pallas_call x1, Pallas kernels, body(): pl.pallas_call(third_kernel, out_shape=[shifted, tall, tall, row_windows]...  2.46 us
    max x1, other arithmetic, body(): own = jnp.maximum(series, jnp.finfo(series.dtype).min)  0.88 us
    pallas_call x1, Pallas kernels, body(): pl.pallas_call(functools.partial(peak_kernel, rows), out_shape=jax.ShapeD...  0.83 us
  transfers between devices with their start and end apart: 7, of which 5 were waited for; matrix products, arithmetic and copies ran while one was open for 3% of the time, Pallas kernels for 9%

profile of v12, /device:TPU:0, one launch (start us, length us, event | category | flops | bytes accessed | tf_op | source)
XLA Modules:
  0.0 29.4 jit_solution(11830131184192091183)
XLA Ops:
  0.0 4.0 %collective-permute-start = (f32[64,256]{1,0:T(8,128)}, f32[64,256]{1,0:T(8,128)S(1)}, u32[]{:S(2)}, u32[]{:S(2)}) collective-permute-start(f32[64,256]{1,0:T(8,128)} %param.2), channel_id=1, source_target_pairs={{0,8},{4,12},{8,4},{12,16},{16,24},{20,28},{24,20},{28,32},{32,40}... | collective-permute-start | bytes 196616 | tf_op jit(solution)/shard_map/ppermute | solution.py:27
  4.0 1.0 %collective-permute-start.2 = (f32[64,256]{1,0:T(8,128)}, f32[64,256]{1,0:T(8,128)S(1)}, u32[]{:S(2)}, u32[]{:S(2)}) collective-permute-start(f32[64,256]{1,0:T(8,128)} %param.2), channel_id=1, source_target_pairs={{0,4},{4,8},{8,16},{12,20},{16,12},{20,24},{24,32},{28,36},{32,28}... | collective-permute-start | bytes 196616 | tf_op jit(solution)/shard_map/ppermute | solution.py:27
  5.0 0.0 collective-permute-start.1
  5.0 0.9 %broadcast_maximum_fusion.own = f32[64,256]{1,0:T(8,128)S(1)} fusion(f32[64,256]{1,0:T(8,128)} %param.2), kind=kLoop, calls=%fused_computation | loop fusion | flops 16384 | bytes 131072 | tf_op jit(solution)/shard_map/max | solution.py:294
  5.9 5.6 %collective-permute-done.from_first = f32[64,256]{1,0:T(8,128)S(1)} collective-permute-done((f32[64,256]{1,0:T(8,128)}, f32[64,256]{1,0:T(8,128)S(1)}, u32[]{:S(2)}, u32[]{:S(2)}) %collective-permute-start) | collective-permute-done | bytes 65568 | tf_op jit(solution)/shard_map/ppermute | solution.py:27
  11.5 0.0 collective-permute-done.1.from_third
  11.5 2.5 %shard_map.29 = (f32[8,1024,128]{2,1,0:T(8,128)S(1)}, f32[1024,128]{1,0:T(8,128)S(1)}, f32[1024,128]{1,0:T(8,128)S(1)}, bf16[32,2,256,256]{3,2,1,0:T(8,128)(2,1)S(1)}) custom-call(f32[64,256]{1,0:T(8,128)S(1)} %broadcast_maximum_fusion.own, ...), custom_call_target="tpu_custom_call", output_to_operand_aliasing={{0}: (2, {}), {1}: (3, {}), {2}: (4, {})} | custom-call | tf_op jit(solution)/shard_map/pallas_call | solution.py:316
  14.0 0.2 collective-permute-done.2.from_second
  14.2 3.2 %shard_map.30 = (bf16[352,256]{1,0:T(8,128)(2,1)S(1)}, f32[8,1024,128]{2,1,0:T(8,128)S(1)}, f32[1024,128]{1,0:T(8,128)S(1)}, f32[1024,128]{1,0:T(8,128)S(1)}, bf16[32,2,256,256]{3,2,1,0:T(8,128)(2,1)S(1)}) custom-call(f32[64,256]{1,0:T(8,128)S(1)} %broadcast_maximum_fusion.own, ...), custom_call_target="tpu_custom_call", output_to_operand_aliasing={{1}: (4, {}), {2}: (5, {}), {3}: (6, {}), {4}: (7, {})} | custom-call | tf_op jit(solution)/shard_map/pallas_call | solution.py:325
  17.4 0.1 collective-permute-start.4
  17.5 0.0 copy-start
  17.5 0.1 collective-permute-start.3
  17.6 5.3 %collective-permute-done.4.p2 = bf16[352,256]{1,0:T(8,128)(2,1)S(1)} collective-permute-done((bf16[352,256]{1,0:T(8,128)(2,1)S(1)}, bf16[352,256]{1,0:T(8,128)(2,1)S(1)}, u32[]{:S(2)}, u32[]{:S(2)}) %collective-permute-start.4) | collective-permute-done | bytes 180256 | tf_op jit(solution)/shard_map/ppermute | solution.py:27
  22.9 0.0 collective-permute-start.5
  22.9 1.4 %collective-permute-done.5.p3 = bf16[352,256]{1,0:T(8,128)(2,1)S(1)} collective-permute-done((bf16[352,256]{1,0:T(8,128)(2,1)S(1)}, bf16[352,256]{1,0:T(8,128)(2,1)S(1)}, u32[]{:S(2)}, u32[]{:S(2)}) %collective-permute-start.5) | collective-permute-done | bytes 180256 | tf_op jit(solution)/shard_map/ppermute | solution.py:27
  24.4 0.0 collective-permute-done.3.p1
  24.4 0.0 copy-done
  24.4 0.8 %shard_map.32 = f32[1,256]{1,0:T(1,128)S(1)} custom-call(s32[64]{0:T(128)S(1)} %copy-done, f32[352,256]{1,0:T(8,128)S(1)} %shard_map.31.p0, f32[352,256]{1,0:T(8,128)S(1)} %collective-permute-done.3.p1, bf16[352,256]{1,0:T(8,128)(2,1)S(1)} %collective-permute-done.4.p2, bf16[352,256]{1,0:T(8,128)(2,1)S(1)} %collective-permute-done.5.p3), custom_call_target="tpu_custom_call" | custom-call | tf_op jit(solution)/shard_map/pallas_call | solution.py:344
  25.2 0.4 %collective-permute-start.6 = (f32[1,256]{1,0:T(1,128)S(1)}, f32[1,256]{1,0:T(1,128)S(1)}, u32[]{:S(2)}, u32[]{:S(2)}) collective-permute-start(f32[1,256]{1,0:T(1,128)S(1)} %shard_map.32), channel_id=1, source_target_pairs={{0,2},{1,3},{2,0},{3,1},{4,6},{5,7},{6,4},{7,5},{8,10},{9,11},{10,... | collective-permute-start | bytes 3080 | tf_op jit(solution)/shard_map/ppermute | solution.py:27
  25.6 3.2 %collective-permute-done.6 = f32[1,256]{1,0:T(1,128)S(1)} collective-permute-done((f32[1,256]{1,0:T(1,128)S(1)}, f32[1,256]{1,0:T(1,128)S(1)}, u32[]{:S(2)}, u32[]{:S(2)}) %collective-permute-start.6) | collective-permute-done | bytes 1056 | tf_op jit(solution)/shard_map/ppermute | solution.py:27
  28.8 0.6 %compare_select_fusion = f32[1,256]{1,0:T(1,128)} fusion(f32[1,256]{1,0:T(1,128)S(1)} %shard_map.32, f32[1,256]{1,0:T(1,128)S(1)} %collective-permute-done.6), kind=kLoop, calls=%fused_computation.1 | loop fusion | flops 768 | bytes 3072 | tf_op jit(solution)/shard_map/jit(_where)/select_n | solution.py:352
  (2 shorter events, 0.0 us)
Async XLA Ops:
  0.0 11.5 %collective-permute-start = (f32[64,256]{1,0:T(8,128)}, f32[64,256]{1,0:T(8,128)S(1)}, u32[]{:S(2)}, u32[]{:S(2)}) collective-permute-start(f32[64,256]{1,0:T(8,128)} %param.2), channel_id=1, source_target_pairs={{0,8},{4,12},{8,4},{12,16},{16,24},{20,28},{24,20},{28,32},{32,40}... | collective-permute-start | bytes 196616 | tf_op jit(solution)/shard_map/ppermute | solution.py:27
  4.0 10.2 %collective-permute-start.2 = (f32[64,256]{1,0:T(8,128)}, f32[64,256]{1,0:T(8,128)S(1)}, u32[]{:S(2)}, u32[]{:S(2)}) collective-permute-start(f32[64,256]{1,0:T(8,128)} %param.2), channel_id=1, source_target_pairs={{0,4},{4,8},{8,16},{12,20},{16,12},{20,24},{24,32},{28,36},{32,28}... | collective-permute-start | bytes 196616 | tf_op jit(solution)/shard_map/ppermute | solution.py:27
  5.0 6.5 %collective-permute-start.1 = (f32[64,256]{1,0:T(8,128)}, f32[64,256]{1,0:T(8,128)S(1)}, u32[]{:S(2)}, u32[]{:S(2)}) collective-permute-start(f32[64,256]{1,0:T(8,128)} %param.2), channel_id=1, source_target_pairs={{0,4},{4,0},{8,12},{12,8},{16,20},{20,16},{24,28},{28,24},{32,36},... | collective-permute-start | bytes 196616 | tf_op jit(solution)/shard_map/ppermute | solution.py:27
  17.4 5.6 %collective-permute-start.4 = (bf16[352,256]{1,0:T(8,128)(2,1)S(1)}, bf16[352,256]{1,0:T(8,128)(2,1)S(1)}, u32[]{:S(2)}, u32[]{:S(2)}) collective-permute-start(bf16[352,256]{1,0:T(8,128)(2,1)S(1)} %get-tuple-element.28), channel_id=1, source_target_pairs={{0,2},{1,3},{2,0},{3,1},{4,6},{5,7},{6,4},{7,5},{8,10},{9,11},{10,... | collective-permute-start | bytes 540680 | tf_op jit(solution)/shard_map/ppermute | solution.py:27
  17.5 6.9 %copy-start = (s32[64]{0:T(128)S(1)}, s32[64]{0:T(128)}, u32[]{:S(2)}) copy-start(s32[64]{0:T(128)} %lens.1) | copy-start | bytes 772
  17.5 6.8 %collective-permute-start.3 = (f32[352,256]{1,0:T(8,128)S(1)}, f32[352,256]{1,0:T(8,128)S(1)}, u32[]{:S(2)}, u32[]{:S(2)}) collective-permute-start(f32[352,256]{1,0:T(8,128)S(1)} %shard_map.31.p0), channel_id=1, source_target_pairs={{0,1},{1,0},{2,3},{3,2},{4,5},{5,4},{6,7},{7,6},{8,9},{9,8},{10,11... | collective-permute-start | bytes 1081352 | tf_op jit(solution)/shard_map/ppermute | solution.py:27
  22.9 1.4 %collective-permute-start.5 = (bf16[352,256]{1,0:T(8,128)(2,1)S(1)}, bf16[352,256]{1,0:T(8,128)(2,1)S(1)}, u32[]{:S(2)}, u32[]{:S(2)}) collective-permute-start(bf16[352,256]{1,0:T(8,128)(2,1)S(1)} %collective-permute-done.4.p2), channel_id=1, source_target_pairs={{0,1},{1,0},{2,3},{3,2},{4,5},{5,4},{6,7},{7,6},{8,9},{9,8},{10,11... | collective-permute-start | bytes 540680 | tf_op jit(solution)/shard_map/ppermute | solution.py:27
  25.2 3.6 %collective-permute-start.6 = (f32[1,256]{1,0:T(1,128)S(1)}, f32[1,256]{1,0:T(1,128)S(1)}, u32[]{:S(2)}, u32[]{:S(2)}) collective-permute-start(f32[1,256]{1,0:T(1,128)S(1)} %shard_map.32), channel_id=1, source_target_pairs={{0,2},{1,3},{2,0},{3,1},{4,6},{5,7},{6,4},{7,5},{8,10},{9,11},{10,... | collective-permute-start | bytes 3080 | tf_op jit(solution)/shard_map/ppermute | solution.py:27

commit v13 on v12

--- a/solution.py
+++ b/solution.py
@@ -1,5 +1,3 @@
-import functools
-
 import jax
 import jax.numpy as jnp
 from jax import lax
@@ -182,7 +180,8 @@
     return earlier, before, after
 
 
-def first_kernel(own, from_first, x8, end_m, end_v, *work):
+def first_kernel(own, from_first, lens, x8, end_m, end_v, reach, row_ok, *work):
+    limits(own.shape[1], lens, reach, row_ok)
     place = lax.rem(lax.axis_index("tm"), LINE)
 
     @pl.when((place == 0) & (lax.axis_index("tm") > 0))
@@ -208,11 +207,12 @@
     @pl.when(place < 2)
     def _():
         def step(p, carry):
-            fill_rows(p, 0, x8, end_m, end_v, zr)
-            fill_rows(p, 1, x8, end_m, end_v, zr)
+            for t in range(BODY):
+                fill_rows(p * BODY + t, 0, x8, end_m, end_v, zr)
+                fill_rows(p * BODY + t, 1, x8, end_m, end_v, zr)
             return carry
 
-        lax.fori_loop(0, zr.shape[0] // 2, step, 0)
+        lax.fori_loop(0, zr.shape[0] // (2 * BODY), step, 0)
 
 
 def far_kernel(own, from_first, from_third, from_second, _x8, _m, _v, _zr, out, x8, end_m, end_v, zr, *work):
@@ -258,32 +258,38 @@
         out[...] = jnp.zeros_like(out)
 
 
-def peak_kernel(rows, lens, p0, p1, p2, p3, out):
-    quarter = p0.shape[0]
+def limits(rows, lens, reach, row_ok):
+    quarter = reach.shape[0]
     block = lax.axis_index("tm")
     part = lax.axis_index("chan") // 2
     last = rows * lax.axis_size("tm") - WIN
     seg = rows // 2
     start = (block - STEPS) * rows
-    f32 = jnp.float32
-    score = (p0[...] + p1[...]) + (p2[...].astype(f32) + p3[...].astype(f32))
-    shape = (quarter, LANES)
-    j = part * quarter + lax.broadcasted_iota(jnp.int32, shape, 0)
-    stop = jnp.zeros(shape, jnp.int32)
+    j = part * quarter + lax.broadcasted_iota(jnp.int32, reach.shape, 0)
+    stop = jnp.zeros(reach.shape, jnp.int32)
     for s in range(2 * (STEPS + 1)):
         which = (block - STEPS) * 2 + s
         length = jnp.where(which >= 0, lens[jnp.maximum(which, 0)], 0)
         end = jnp.minimum(s * seg + length, last + 1 - start)
         stop = jnp.where(j >= s * seg, end, stop)
-    reach = jnp.where(j < stop, j + EXCL, 2 * (STEPS + 1) * rows)
-    lane = lax.broadcasted_iota(jnp.int32, shape, 1)
+    reach[...] = jnp.where(j < stop, j + EXCL, 2 * (STEPS + 1) * rows)
+    r = lax.broadcasted_iota(jnp.int32, row_ok.shape, 1)
+    own = jnp.where(r < seg, lens[block * 2], seg + lens[block * 2 + 1])
+    row_ok[...] = jnp.where(r < jnp.minimum(own, last + 1 - block * rows), 1, 0)
+
+
+def peak_kernel(reach, row_ok, p0, p1, p2, p3, out):
+    rows = out.shape[1]
+    f32 = jnp.float32
+    first_row = reach[...]
+    lane = lax.broadcasted_iota(jnp.int32, first_row.shape, 1)
     for at in range(0, rows, LANES):
+        part = slice(at, at + LANES)
+        score = (p0[:, part] + p1[:, part]) + (p2[:, part].astype(f32) + p3[:, part].astype(f32))
         i = lane + (STEPS * rows + at)
-        best = jnp.max(jnp.where(i >= reach, score[:, at : at + LANES], MASKED), axis=0, keepdims=True)
+        best = jnp.max(jnp.where(i >= first_row, score, MASKED), axis=0, keepdims=True)
         best = jnp.where(best > 0.5 * MASKED, best * (1.0 / WIN), MASKED)
-        r = i[:1, :] - STEPS * rows
-        own = jnp.where(r < seg, lens[block * 2], seg + lens[block * 2 + 1])
-        out[:, at : at + LANES] = jnp.where(r < jnp.minimum(own, last + 1 - block * rows), best, MASKED)
+        out[:, part] = jnp.where(row_ok[:, part] > 0, best, MASKED)
 
 
 def body(series, lengths):
@@ -305,14 +311,20 @@
     work = [pltpu.VMEM((rows + 2 * HALF, LANES), f32)] * 5
     row_windows = jax.ShapeDtypeStruct((HALF // STEP_K, UNITS, rows, 2 * LANES), bf16)
     params = pltpu.CompilerParams(vmem_limit_bytes=SMALL_LIMIT)
-    after_first = pl.pallas_call(
+    *after_first, reach, row_ok = pl.pallas_call(
         first_kernel,
-        out_shape=[shifted, tall, tall],
-        in_specs=[vmem] * 2,
-        out_specs=[vmem] * 3,
+        out_shape=[
+            shifted,
+            tall,
+            tall,
+            jax.ShapeDtypeStruct((side, LANES), jnp.int32),
+            jax.ShapeDtypeStruct((1, rows), jnp.int32),
+        ],
+        in_specs=[vmem, vmem, smem],
+        out_specs=[vmem] * 5,
         scratch_shapes=work,
         compiler_params=params,
-    )(own, from_first)
+    )(own, from_first, lengths)
     after_third = pl.pallas_call(
         third_kernel,
         out_shape=[shifted, tall, tall, row_windows],
@@ -342,12 +354,12 @@
     near_peer = sent(near, "chan", across(1))
     far_peer = sent(far_got, "chan", across(1))
     best = pl.pallas_call(
-        functools.partial(peak_kernel, rows),
+        peak_kernel,
         out_shape=jax.ShapeDtypeStruct((1, rows), f32),
-        in_specs=[smem] + [vmem] * 4,
+        in_specs=[vmem] * 6,
         out_specs=vmem,
         compiler_params=pltpu.CompilerParams(vmem_limit_bytes=SMALL_LIMIT),
-    )(lengths, near, near_peer, far_got, far_peer)
+    )(reach, row_ok, near, near_peer, far_got, far_peer)
     best = jnp.maximum(best, sent(best, "chan", across(2)))
     return jnp.where(best > 0.5 * MASKED, best, 0.0).reshape(rows)
 

time: 29.7 us -> 30.6 us (1.030)
  local copies, waits for them, and re-layouts: 0.01 us -> 0.66 us
  waiting for transfers between devices: 15.8 us -> 15.2 us
  Pallas kernels: 6.53 us -> 7.07 us
  starting transfers between devices: 5.59 us -> 5.97 us
    unnamed x2, local copies, waits for them, and re-layouts: 0.01 us -> 0.66 us
    ppermute x7, waiting for transfers between devices: 15.8 us -> 15.2 us  [sent(): lax.ppermute(block, axis, [(i, target(i, count)) for i in range(count)])]
    pallas_call x1, Pallas kernels: 3.19 us -> 3.6 us  [body(): pl.pallas_call(far_kernel, out_shape=[jax.ShapeDtypeStruct((side, rows),...]
    ppermute x7, starting transfers between devices: 5.59 us -> 5.97 us  [sent(): lax.ppermute(block, axis, [(i, target(i, count)) for i in range(count)])]
  transfers between devices with their start and end apart: 7 -> 7, of which waited for: 5 -> 4; matrix products, arithmetic and copies ran while one was open for 3% -> 3% of each run, Pallas kernels for 9% -> 11%
where the time goes in v13:
time: 30.6 us; the launch traced here: 30.4 us
  waiting for transfers between devices  15.2 us (50%)
  Pallas kernels  7.07 us (23%)
  starting transfers between devices  5.97 us (20%)
  other arithmetic  1.45 us (5%)
  local copies, waits for them, and re-layouts  0.66 us (2%)
    ppermute x7, waiting for transfers between devices, sent(): lax.ppermute(block, axis, [(i, target(i, count)) for i in range(count)])  15.2 us
    ppermute x7, starting transfers between devices, sent(): lax.ppermute(block, axis, [(i, target(i, count)) for i in range(count)])  5.97 us
    pallas_call x1, Pallas kernels, body(): pl.pallas_call(far_kernel, out_shape=[jax.ShapeDtypeStruct((side, rows),...  3.6 us
    pallas_call x1, Pallas kernels, body(): pl.pallas_call(third_kernel, out_shape=[shifted, tall, tall, row_windows]...  2.57 us
    max x1, other arithmetic, body(): own = jnp.maximum(series, jnp.finfo(series.dtype).min)  0.88 us
    pallas_call x1, Pallas kernels, body(): pl.pallas_call(first_kernel, out_shape=[shifted, tall, tall, jax.ShapeDty...  0.66 us
    unnamed x2, local copies, waits for them, and re-layouts  0.66 us
  transfers between devices with their start and end apart: 7, of which 4 were waited for; matrix products, arithmetic and copies ran while one was open for 3% of the time, Pallas kernels for 11%

profile of v13, /device:TPU:0, one launch (start us, length us, event | category | flops | bytes accessed | tf_op | source)
XLA Modules:
  0.0 30.4 jit_solution(12288218097400711290)
XLA Ops:
  0.0 4.0 %collective-permute-start = (f32[64,256]{1,0:T(8,128)}, f32[64,256]{1,0:T(8,128)S(1)}, u32[]{:S(2)}, u32[]{:S(2)}) collective-permute-start(f32[64,256]{1,0:T(8,128)} %param.2), channel_id=1, source_target_pairs={{0,8},{4,12},{8,4},{12,16},{16,24},{20,28},{24,20},{28,32},{32,40}... | collective-permute-start | bytes 196616 | tf_op jit(solution)/shard_map/ppermute | solution.py:25
  4.0 1.0 %collective-permute-start.2 = (f32[64,256]{1,0:T(8,128)}, f32[64,256]{1,0:T(8,128)S(1)}, u32[]{:S(2)}, u32[]{:S(2)}) collective-permute-start(f32[64,256]{1,0:T(8,128)} %param.2), channel_id=1, source_target_pairs={{0,4},{4,8},{8,16},{12,20},{16,12},{20,24},{24,32},{28,36},{32,28}... | collective-permute-start | bytes 196616 | tf_op jit(solution)/shard_map/ppermute | solution.py:25
  5.0 0.0 collective-permute-start.1
  5.0 0.9 %broadcast_maximum_fusion.own = f32[64,256]{1,0:T(8,128)S(1)} fusion(f32[64,256]{1,0:T(8,128)} %param.2), kind=kLoop, calls=%fused_computation | loop fusion | flops 16384 | bytes 131072 | tf_op jit(solution)/shard_map/max | solution.py:300
  5.9 5.6 %collective-permute-done.from_first = f32[64,256]{1,0:T(8,128)S(1)} collective-permute-done((f32[64,256]{1,0:T(8,128)}, f32[64,256]{1,0:T(8,128)S(1)}, u32[]{:S(2)}, u32[]{:S(2)}) %collective-permute-start) | collective-permute-done | bytes 65568 | tf_op jit(solution)/shard_map/ppermute | solution.py:25
  11.5 0.0 copy-start
  11.5 0.7 %copy-done = s32[64]{0:T(128)S(1)} copy-done((s32[64]{0:T(128)S(1)}, s32[64]{0:T(128)}, u32[]{:S(2)}) %copy-start) | copy-done | bytes 280
  12.1 0.7 %shard_map.28 = (f32[8,1024,128]{2,1,0:T(8,128)S(1)}, f32[1024,128]{1,0:T(8,128)S(1)}, f32[1024,128]{1,0:T(8,128)S(1)}, s32[352,128]{1,0:T(8,128)S(1)}, s32[1,256]{1,0:T(1,128)S(1)}) custom-call(f32[64,256]{1,0:T(8,128)S(1)} %broadcast_maximum_fusion.own, f32[64,256]{1,0:T(8,128)S(1)} %collective-permute-done.from_first, s32[64]{0:T(128)S(1)} %copy-done), custom_call_target="tpu_custom_call" | custom-call | tf_op jit(solution)/shard_map/pallas_call | solution.py:314
  12.8 0.0 collective-permute-done.1.from_third
  12.8 2.6 %shard_map.29 = (f32[8,1024,128]{2,1,0:T(8,128)S(1)}, f32[1024,128]{1,0:T(8,128)S(1)}, f32[1024,128]{1,0:T(8,128)S(1)}, bf16[32,2,256,256]{3,2,1,0:T(8,128)(2,1)S(1)}) custom-call(f32[64,256]{1,0:T(8,128)S(1)} %broadcast_maximum_fusion.own, ...), custom_call_target="tpu_custom_call", output_to_operand_aliasing={{0}: (2, {}), {1}: (3, {}), {2}: (4, {})} | custom-call | tf_op jit(solution)/shard_map/pallas_call | solution.py:328
  15.4 0.0 collective-permute-done.2.from_second
  15.4 3.6 %shard_map.30 = (bf16[352,256]{1,0:T(8,128)(2,1)S(1)}, f32[8,1024,128]{2,1,0:T(8,128)S(1)}, f32[1024,128]{1,0:T(8,128)S(1)}, f32[1024,128]{1,0:T(8,128)S(1)}, bf16[32,2,256,256]{3,2,1,0:T(8,128)(2,1)S(1)}) custom-call(f32[64,256]{1,0:T(8,128)S(1)} %broadcast_maximum_fusion.own, ...), custom_call_target="tpu_custom_call", output_to_operand_aliasing={{1}: (4, {}), {2}: (5, {}), {3}: (6, {}), {4}: (7, {})} | custom-call | tf_op jit(solution)/shard_map/pallas_call | solution.py:337
  19.0 0.1 collective-permute-start.4
  19.2 0.1 collective-permute-start.3
  19.3 5.3 %collective-permute-done.4.p2 = bf16[352,256]{1,0:T(8,128)(2,1)S(1)} collective-permute-done((bf16[352,256]{1,0:T(8,128)(2,1)S(1)}, bf16[352,256]{1,0:T(8,128)(2,1)S(1)}, u32[]{:S(2)}, u32[]{:S(2)}) %collective-permute-start.4) | collective-permute-done | bytes 180256 | tf_op jit(solution)/shard_map/ppermute | solution.py:25
  24.6 0.0 collective-permute-start.5
  24.6 1.4 %collective-permute-done.5.p3 = bf16[352,256]{1,0:T(8,128)(2,1)S(1)} collective-permute-done((bf16[352,256]{1,0:T(8,128)(2,1)S(1)}, bf16[352,256]{1,0:T(8,128)(2,1)S(1)}, u32[]{:S(2)}, u32[]{:S(2)}) %collective-permute-start.5) | collective-permute-done | bytes 180256 | tf_op jit(solution)/shard_map/ppermute | solution.py:25
  26.0 0.0 collective-permute-done.3.p1
  26.0 0.2 shard_map.32
  26.2 0.8 %collective-permute-start.6 = (f32[1,256]{1,0:T(1,128)S(1)}, f32[1,256]{1,0:T(1,128)S(1)}, u32[]{:S(2)}, u32[]{:S(2)}) collective-permute-start(f32[1,256]{1,0:T(1,128)S(1)} %shard_map.32), channel_id=1, source_target_pairs={{0,2},{1,3},{2,0},{3,1},{4,6},{5,7},{6,4},{7,5},{8,10},{9,11},{10,... | collective-permute-start | bytes 3080 | tf_op jit(solution)/shard_map/ppermute | solution.py:25
  27.0 2.9 %collective-permute-done.6 = f32[1,256]{1,0:T(1,128)S(1)} collective-permute-done((f32[1,256]{1,0:T(1,128)S(1)}, f32[1,256]{1,0:T(1,128)S(1)}, u32[]{:S(2)}, u32[]{:S(2)}) %collective-permute-start.6) | collective-permute-done | bytes 1056 | tf_op jit(solution)/shard_map/ppermute | solution.py:25
  29.9 0.6 %compare_select_fusion = f32[1,256]{1,0:T(1,128)} fusion(f32[1,256]{1,0:T(1,128)S(1)} %shard_map.32, f32[1,256]{1,0:T(1,128)S(1)} %collective-permute-done.6), kind=kLoop, calls=%fused_computation.1 | loop fusion | flops 768 | bytes 3072 | tf_op jit(solution)/shard_map/jit(_where)/select_n | solution.py:364
  (1 shorter events, 0.0 us)
Async XLA Ops:
  0.0 11.5 %collective-permute-start = (f32[64,256]{1,0:T(8,128)}, f32[64,256]{1,0:T(8,128)S(1)}, u32[]{:S(2)}, u32[]{:S(2)}) collective-permute-start(f32[64,256]{1,0:T(8,128)} %param.2), channel_id=1, source_target_pairs={{0,8},{4,12},{8,4},{12,16},{16,24},{20,28},{24,20},{28,32},{32,40}... | collective-permute-start | bytes 196616 | tf_op jit(solution)/shard_map/ppermute | solution.py:25
  4.0 11.4 %collective-permute-start.2 = (f32[64,256]{1,0:T(8,128)}, f32[64,256]{1,0:T(8,128)S(1)}, u32[]{:S(2)}, u32[]{:S(2)}) collective-permute-start(f32[64,256]{1,0:T(8,128)} %param.2), channel_id=1, source_target_pairs={{0,4},{4,8},{8,16},{12,20},{16,12},{20,24},{24,32},{28,36},{32,28}... | collective-permute-start | bytes 196616 | tf_op jit(solution)/shard_map/ppermute | solution.py:25
  5.0 7.8 %collective-permute-start.1 = (f32[64,256]{1,0:T(8,128)}, f32[64,256]{1,0:T(8,128)S(1)}, u32[]{:S(2)}, u32[]{:S(2)}) collective-permute-start(f32[64,256]{1,0:T(8,128)} %param.2), channel_id=1, source_target_pairs={{0,4},{4,0},{8,12},{12,8},{16,20},{20,16},{24,28},{28,24},{32,36},... | collective-permute-start | bytes 196616 | tf_op jit(solution)/shard_map/ppermute | solution.py:25
  11.5 0.7 %copy-start = (s32[64]{0:T(128)S(1)}, s32[64]{0:T(128)}, u32[]{:S(2)}) copy-start(s32[64]{0:T(128)} %lens.1) | copy-start | bytes 772
  19.0 5.6 %collective-permute-start.4 = (bf16[352,256]{1,0:T(8,128)(2,1)S(1)}, bf16[352,256]{1,0:T(8,128)(2,1)S(1)}, u32[]{:S(2)}, u32[]{:S(2)}) collective-permute-start(bf16[352,256]{1,0:T(8,128)(2,1)S(1)} %get-tuple-element.32), channel_id=1, source_target_pairs={{0,2},{1,3},{2,0},{3,1},{4,6},{5,7},{6,4},{7,5},{8,10},{9,11},{10,... | collective-permute-start | bytes 540680 | tf_op jit(solution)/shard_map/ppermute | solution.py:25
  19.2 6.8 %collective-permute-start.3 = (f32[352,256]{1,0:T(8,128)S(1)}, f32[352,256]{1,0:T(8,128)S(1)}, u32[]{:S(2)}, u32[]{:S(2)}) collective-permute-start(f32[352,256]{1,0:T(8,128)S(1)} %shard_map.31.p0), channel_id=1, source_target_pairs={{0,1},{1,0},{2,3},{3,2},{4,5},{5,4},{6,7},{7,6},{8,9},{9,8},{10,11... | collective-permute-start | bytes 1081352 | tf_op jit(solution)/shard_map/ppermute | solution.py:25
  24.6 1.4 %collective-permute-start.5 = (bf16[352,256]{1,0:T(8,128)(2,1)S(1)}, bf16[352,256]{1,0:T(8,128)(2,1)S(1)}, u32[]{:S(2)}, u32[]{:S(2)}) collective-permute-start(bf16[352,256]{1,0:T(8,128)(2,1)S(1)} %collective-permute-done.4.p2), channel_id=1, source_target_pairs={{0,1},{1,0},{2,3},{3,2},{4,5},{5,4},{6,7},{7,6},{8,9},{9,8},{10,11... | collective-permute-start | bytes 540680 | tf_op jit(solution)/shard_map/ppermute | solution.py:25
  26.2 3.6 %collective-permute-start.6 = (f32[1,256]{1,0:T(1,128)S(1)}, f32[1,256]{1,0:T(1,128)S(1)}, u32[]{:S(2)}, u32[]{:S(2)}) collective-permute-start(f32[1,256]{1,0:T(1,128)S(1)} %shard_map.32), channel_id=1, source_target_pairs={{0,2},{1,3},{2,0},{3,1},{4,6},{5,7},{6,4},{7,5},{8,10},{9,11},{10,... | collective-permute-start | bytes 3080 | tf_op jit(solution)/shard_map/ppermute | solution.py:25

commit v14 on v12

--- a/solution.py
+++ b/solution.py
@@ -14,7 +14,7 @@
 MASKED = -1000000000.0
 EXCL = WIN // 4
 STEP_K = 4
-GROUP = 32
+GROUP = 16
 UNITS = 2
 BODY = 4
 LANES = 128

time: 29.7 us -> 29.8 us (level)
  no operation moved by 1% of the time
where the time goes in v14:
time: 29.8 us; the launch traced here: 29.4 us
  waiting for transfers between devices  15.7 us (53%)
  Pallas kernels  6.59 us (22%)
  starting transfers between devices  5.59 us (19%)
  other arithmetic  1.45 us (5%)
    ppermute x7, waiting for transfers between devices, sent(): lax.ppermute(block, axis, [(i, target(i, count)) for i in range(count)])  15.7 us
    ppermute x7, starting transfers between devices, sent(): lax.ppermute(block, axis, [(i, target(i, count)) for i in range(count)])  5.59 us
    pallas_call x1, Pallas kernels, body(): pl.pallas_call(far_kernel, out_shape=[jax.ShapeDtypeStruct((side, rows),...  3.19 us
    pallas_call x1, Pallas kernels, body(): pl.pallas_call(third_kernel, out_shape=[shifted, tall, tall, row_windows]...  2.52 us
    max x1, other arithmetic, body(): own = jnp.maximum(series, jnp.finfo(series.dtype).min)  0.88 us
    pallas_call x1, Pallas kernels, body(): pl.pallas_call(functools.partial(peak_kernel, rows), out_shape=jax.ShapeD...  0.83 us
  transfers between devices with their start and end apart: 7, of which 5 were waited for; matrix products, arithmetic and copies ran while one was open for 3% of the time, Pallas kernels for 9%

profile of v14, /device:TPU:0, one launch (start us, length us, event | category | flops | bytes accessed | tf_op | source)
XLA Modules:
  0.0 29.4 jit_solution(9447356699736267409)
XLA Ops:
  0.0 4.0 %collective-permute-start = (f32[64,256]{1,0:T(8,128)}, f32[64,256]{1,0:T(8,128)S(1)}, u32[]{:S(2)}, u32[]{:S(2)}) collective-permute-start(f32[64,256]{1,0:T(8,128)} %param.2), channel_id=1, source_target_pairs={{0,8},{4,12},{8,4},{12,16},{16,24},{20,28},{24,20},{28,32},{32,40}... | collective-permute-start | bytes 196616 | tf_op jit(solution)/shard_map/ppermute | solution.py:27
  4.0 1.0 %collective-permute-start.2 = (f32[64,256]{1,0:T(8,128)}, f32[64,256]{1,0:T(8,128)S(1)}, u32[]{:S(2)}, u32[]{:S(2)}) collective-permute-start(f32[64,256]{1,0:T(8,128)} %param.2), channel_id=1, source_target_pairs={{0,4},{4,8},{8,16},{12,20},{16,12},{20,24},{24,32},{28,36},{32,28}... | collective-permute-start | bytes 196616 | tf_op jit(solution)/shard_map/ppermute | solution.py:27
  5.0 0.0 collective-permute-start.1
  5.0 0.9 %broadcast_maximum_fusion.own = f32[64,256]{1,0:T(8,128)S(1)} fusion(f32[64,256]{1,0:T(8,128)} %param.2), kind=kLoop, calls=%fused_computation | loop fusion | flops 16384 | bytes 131072 | tf_op jit(solution)/shard_map/max | solution.py:294
  5.9 5.6 %collective-permute-done.from_first = f32[64,256]{1,0:T(8,128)S(1)} collective-permute-done((f32[64,256]{1,0:T(8,128)}, f32[64,256]{1,0:T(8,128)S(1)}, u32[]{:S(2)}, u32[]{:S(2)}) %collective-permute-start) | collective-permute-done | bytes 65568 | tf_op jit(solution)/shard_map/ppermute | solution.py:27
  11.5 0.0 collective-permute-done.1.from_third
  11.5 2.5 %shard_map.29 = (f32[8,1024,128]{2,1,0:T(8,128)S(1)}, f32[1024,128]{1,0:T(8,128)S(1)}, f32[1024,128]{1,0:T(8,128)S(1)}, bf16[32,2,256,256]{3,2,1,0:T(8,128)(2,1)S(1)}) custom-call(f32[64,256]{1,0:T(8,128)S(1)} %broadcast_maximum_fusion.own, ...), custom_call_target="tpu_custom_call", output_to_operand_aliasing={{0}: (2, {}), {1}: (3, {}), {2}: (4, {})} | custom-call | tf_op jit(solution)/shard_map/pallas_call | solution.py:316
  14.0 0.1 collective-permute-done.2.from_second
  14.2 3.2 %shard_map.30 = (bf16[352,256]{1,0:T(8,128)(2,1)S(1)}, f32[8,1024,128]{2,1,0:T(8,128)S(1)}, f32[1024,128]{1,0:T(8,128)S(1)}, f32[1024,128]{1,0:T(8,128)S(1)}, bf16[32,2,256,256]{3,2,1,0:T(8,128)(2,1)S(1)}) custom-call(f32[64,256]{1,0:T(8,128)S(1)} %broadcast_maximum_fusion.own, ...), custom_call_target="tpu_custom_call", output_to_operand_aliasing={{1}: (4, {}), {2}: (5, {}), {3}: (6, {}), {4}: (7, {})} | custom-call | tf_op jit(solution)/shard_map/pallas_call | solution.py:325
  17.4 0.1 collective-permute-start.4
  17.5 0.0 copy-start
  17.5 0.1 collective-permute-start.3
  17.6 5.3 %collective-permute-done.4.p2 = bf16[352,256]{1,0:T(8,128)(2,1)S(1)} collective-permute-done((bf16[352,256]{1,0:T(8,128)(2,1)S(1)}, bf16[352,256]{1,0:T(8,128)(2,1)S(1)}, u32[]{:S(2)}, u32[]{:S(2)}) %collective-permute-start.4) | collective-permute-done | bytes 180256 | tf_op jit(solution)/shard_map/ppermute | solution.py:27
  22.9 0.0 collective-permute-start.5
  22.9 1.4 %collective-permute-done.5.p3 = bf16[352,256]{1,0:T(8,128)(2,1)S(1)} collective-permute-done((bf16[352,256]{1,0:T(8,128)(2,1)S(1)}, bf16[352,256]{1,0:T(8,128)(2,1)S(1)}, u32[]{:S(2)}, u32[]{:S(2)}) %collective-permute-start.5) | collective-permute-done | bytes 180256 | tf_op jit(solution)/shard_map/ppermute | solution.py:27
  24.4 0.0 collective-permute-done.3.p1
  24.4 0.0 copy-done
  24.4 0.8 %shard_map.32 = f32[1,256]{1,0:T(1,128)S(1)} custom-call(s32[64]{0:T(128)S(1)} %copy-done, f32[352,256]{1,0:T(8,128)S(1)} %shard_map.31.p0, f32[352,256]{1,0:T(8,128)S(1)} %collective-permute-done.3.p1, bf16[352,256]{1,0:T(8,128)(2,1)S(1)} %collective-permute-done.4.p2, bf16[352,256]{1,0:T(8,128)(2,1)S(1)} %collective-permute-done.5.p3), custom_call_target="tpu_custom_call" | custom-call | tf_op jit(solution)/shard_map/pallas_call | solution.py:344
  25.2 0.4 %collective-permute-start.6 = (f32[1,256]{1,0:T(1,128)S(1)}, f32[1,256]{1,0:T(1,128)S(1)}, u32[]{:S(2)}, u32[]{:S(2)}) collective-permute-start(f32[1,256]{1,0:T(1,128)S(1)} %shard_map.32), channel_id=1, source_target_pairs={{0,2},{1,3},{2,0},{3,1},{4,6},{5,7},{6,4},{7,5},{8,10},{9,11},{10,... | collective-permute-start | bytes 3080 | tf_op jit(solution)/shard_map/ppermute | solution.py:27
  25.6 3.2 %collective-permute-done.6 = f32[1,256]{1,0:T(1,128)S(1)} collective-permute-done((f32[1,256]{1,0:T(1,128)S(1)}, f32[1,256]{1,0:T(1,128)S(1)}, u32[]{:S(2)}, u32[]{:S(2)}) %collective-permute-start.6) | collective-permute-done | bytes 1056 | tf_op jit(solution)/shard_map/ppermute | solution.py:27
  28.8 0.6 %compare_select_fusion = f32[1,256]{1,0:T(1,128)} fusion(f32[1,256]{1,0:T(1,128)S(1)} %shard_map.32, f32[1,256]{1,0:T(1,128)S(1)} %collective-permute-done.6), kind=kLoop, calls=%fused_computation.1 | loop fusion | flops 768 | bytes 3072 | tf_op jit(solution)/shard_map/jit(_where)/select_n | solution.py:352
  (2 shorter events, 0.0 us)
Async XLA Ops:
  0.0 11.5 %collective-permute-start = (f32[64,256]{1,0:T(8,128)}, f32[64,256]{1,0:T(8,128)S(1)}, u32[]{:S(2)}, u32[]{:S(2)}) collective-permute-start(f32[64,256]{1,0:T(8,128)} %param.2), channel_id=1, source_target_pairs={{0,8},{4,12},{8,4},{12,16},{16,24},{20,28},{24,20},{28,32},{32,40}... | collective-permute-start | bytes 196616 | tf_op jit(solution)/shard_map/ppermute | solution.py:27
  4.0 10.2 %collective-permute-start.2 = (f32[64,256]{1,0:T(8,128)}, f32[64,256]{1,0:T(8,128)S(1)}, u32[]{:S(2)}, u32[]{:S(2)}) collective-permute-start(f32[64,256]{1,0:T(8,128)} %param.2), channel_id=1, source_target_pairs={{0,4},{4,8},{8,16},{12,20},{16,12},{20,24},{24,32},{28,36},{32,28}... | collective-permute-start | bytes 196616 | tf_op jit(solution)/shard_map/ppermute | solution.py:27
  5.0 6.5 %collective-permute-start.1 = (f32[64,256]{1,0:T(8,128)}, f32[64,256]{1,0:T(8,128)S(1)}, u32[]{:S(2)}, u32[]{:S(2)}) collective-permute-start(f32[64,256]{1,0:T(8,128)} %param.2), channel_id=1, source_target_pairs={{0,4},{4,0},{8,12},{12,8},{16,20},{20,16},{24,28},{28,24},{32,36},... | collective-permute-start | bytes 196616 | tf_op jit(solution)/shard_map/ppermute | solution.py:27
  17.4 5.6 %collective-permute-start.4 = (bf16[352,256]{1,0:T(8,128)(2,1)S(1)}, bf16[352,256]{1,0:T(8,128)(2,1)S(1)}, u32[]{:S(2)}, u32[]{:S(2)}) collective-permute-start(bf16[352,256]{1,0:T(8,128)(2,1)S(1)} %get-tuple-element.28), channel_id=1, source_target_pairs={{0,2},{1,3},{2,0},{3,1},{4,6},{5,7},{6,4},{7,5},{8,10},{9,11},{10,... | collective-permute-start | bytes 540680 | tf_op jit(solution)/shard_map/ppermute | solution.py:27
  17.5 6.9 %copy-start = (s32[64]{0:T(128)S(1)}, s32[64]{0:T(128)}, u32[]{:S(2)}) copy-start(s32[64]{0:T(128)} %lens.1) | copy-start | bytes 772
  17.5 6.8 %collective-permute-start.3 = (f32[352,256]{1,0:T(8,128)S(1)}, f32[352,256]{1,0:T(8,128)S(1)}, u32[]{:S(2)}, u32[]{:S(2)}) collective-permute-start(f32[352,256]{1,0:T(8,128)S(1)} %shard_map.31.p0), channel_id=1, source_target_pairs={{0,1},{1,0},{2,3},{3,2},{4,5},{5,4},{6,7},{7,6},{8,9},{9,8},{10,11... | collective-permute-start | bytes 1081352 | tf_op jit(solution)/shard_map/ppermute | solution.py:27
  22.9 1.4 %collective-permute-start.5 = (bf16[352,256]{1,0:T(8,128)(2,1)S(1)}, bf16[352,256]{1,0:T(8,128)(2,1)S(1)}, u32[]{:S(2)}, u32[]{:S(2)}) collective-permute-start(bf16[352,256]{1,0:T(8,128)(2,1)S(1)} %collective-permute-done.4.p2), channel_id=1, source_target_pairs={{0,1},{1,0},{2,3},{3,2},{4,5},{5,4},{6,7},{7,6},{8,9},{9,8},{10,11... | collective-permute-start | bytes 540680 | tf_op jit(solution)/shard_map/ppermute | solution.py:27
  25.2 3.6 %collective-permute-start.6 = (f32[1,256]{1,0:T(1,128)S(1)}, f32[1,256]{1,0:T(1,128)S(1)}, u32[]{:S(2)}, u32[]{:S(2)}) collective-permute-start(f32[1,256]{1,0:T(1,128)S(1)} %shard_map.32), channel_id=1, source_target_pairs={{0,2},{1,3},{2,0},{3,1},{4,6},{5,7},{6,4},{7,5},{8,10},{9,11},{10,... | collective-permute-start | bytes 3080 | tf_op jit(solution)/shard_map/ppermute | solution.py:27
